TPU v7x, 32 devices: a whole 2x2x4 slice. The times are simulated.
32 devices in a mesh: wide: 8 (over z, y), narrow: 4 (over x, core).
Axes of the slice: x: 2, y: 2, z: 4, core: 2. Of those that a mesh axis runs over, the one named last changes fastest.
Arguments:
- source_old: float32 [512, 1024], P(None, ('wide', 'narrow')), may hold values from -90 to 90
- reaction_old: float32 [512, 1024], P(None, ('wide', 'narrow')), may hold values from 0.5 to 4
- new_place: int32 [1024], P(('wide', 'narrow')), may hold values from 0 to 127, as said below
Outputs:
- solution: float32 [512, 1024], P(None, ('wide', 'narrow'))
- strong_residual: float32 [512, 1024], P(None, ('wide', 'narrow'))
Inputs may be any that keep to these rules, and one draw needn't show every extreme that they name: Within the 128 rows of each index of wide, new_place is a permutation of 0 to 127: the row goes to the device of the same index of wide whose index of narrow is new_place // 32, as its element new_place % 32. The rows of one device send at most 16 elements to one device, and every device sends exactly 16 to some device.
All inputs are finite; a program needn't handle non-finite values.
Results may differ from a plain program's by a relative error of at most 0.0001.
Values sent between devices are 32-bit elements; how exact they have to be, the bound alone decides.
No kernel may reach another device: no remote copies, remote signals or barrier semaphores. Data moves between devices by JAX's collectives and lax.ppermute only.
A program may use at most 64 MiB of HBM per device.

v0:
```python
import functools

import jax
import jax.numpy as jnp
import numpy as np
from jax import lax
from jax.experimental import pallas as pl
from jax.experimental.pallas import tpu as pltpu
from jax.sharding import PartitionSpec as P

NP = 8
BX = 2
BY = 4
EZ = 4
PTS = NP**3
PLANE = NP * NP
LANES = 128
HALF = PLANE // 2
XSTEP = BY * EZ

DIFFUSION = 0.05


def legendre_values(abscissa, num_points):
    columns = [np.ones(abscissa.shape), abscissa]
    for degree in range(2, num_points):
        columns.append(
            ((2 * degree - 1) * abscissa * columns[degree - 1] - (degree - 1) * columns[degree - 2])
            / degree
        )
    return np.stack(columns, 1)


def gll_tables(num_points):
    poly_order = num_points - 1
    abscissa = np.cos(np.pi * np.arange(num_points) / poly_order)
    for newton_step in range(60):
        legendre = legendre_values(abscissa, num_points)
        abscissa = abscissa - (abscissa * legendre[:, poly_order] - legendre[:, poly_order - 1]) / (
            num_points * legendre[:, poly_order]
        )
    legendre = legendre_values(abscissa, num_points)
    top_values = legendre[:, poly_order][::-1]
    abscissa = abscissa[::-1]
    weights = 2.0 / (poly_order * num_points * top_values**2)
    identity = np.eye(num_points)
    differ = np.where(identity > 0, 1.0, abscissa[:, None] - abscissa[None, :])
    deriv_table = np.where(identity > 0, 0.0, top_values[:, None] / (top_values[None, :] * differ))
    quarter = poly_order * num_points / 4.0
    edge_fix = np.concatenate([np.array([-quarter]), np.zeros(num_points - 2), np.array([quarter])])
    deriv_table = deriv_table + identity * edge_fix[:, None]
    return (weights, deriv_table)


def stiffness():
    weights, deriv = gll_tables(NP)
    stiff = DIFFUSION * deriv.T @ np.diag(weights) @ deriv
    return weights, 0.5 * (stiff + stiff.T)


WEIGHTS, STIFF = stiffness()
EVEN = 0.5 * (STIFF[:4, :4] + STIFF[:4, 7:3:-1])
ODD = 0.5 * (STIFF[:4, :4] - STIFF[:4, 7:3:-1])


def apply_stiff(f):
    even = [f[j] + f[7 - j] for j in range(4)]
    odd = [f[j] - f[7 - j] for j in range(4)]
    out = [None] * NP
    for i in range(4):
        e = sum_of([float(EVEN[i, j]) * even[j] for j in range(4)])
        o = sum_of([float(ODD[i, j]) * odd[j] for j in range(4)])
        out[i] = e + o
        out[7 - i] = e - o
    return out


def sum_of(terms):
    while len(terms) > 1:
        terms = [
            terms[k] + terms[k + 1] if k + 1 < len(terms) else terms[k]
            for k in range(0, len(terms), 2)
        ]
    return terms[0]


class Grid:
    def __init__(self, lanes, wide):
        self.lanes = lanes
        self.wide = wide
        self.lane = lax.broadcasted_iota(jnp.int32, (NP, lanes), 1)
        self.row = lax.broadcasted_iota(jnp.int32, (NP, lanes), 0)
        self.s = self.lane & (EZ - 1)
        self.j = (self.lane // EZ) & (BY - 1)
        self.i = (self.lane // XSTEP) & (BX - 1)
        self.lower = self.i == 0
        w = jnp.full((NP, lanes), float(WEIGHTS[0]), jnp.float32)
        for c in range(1, NP):
            w = jnp.where(self.row == c, float(WEIGHTS[c]), w)
        self.w = w

    def has_neighbour(self):
        u = lax.axis_index("wide")
        low = jnp.where(u > 0, 1, 0)
        high = jnp.where(u < self.wide - 1, 1, 0)
        return jnp.where(self.lower, low, high) > 0

    def roll(self, x, shift):
        return pltpu.roll(x, shift % self.lanes, axis=x.ndim - 1)

    def share(self, lo, hi, axis):
        if axis == "x":
            new_lo = lo + jnp.where(self.lower, 0.0, self.roll(hi, XSTEP))
            new_hi = hi + jnp.where(self.lower, self.roll(lo, -XSTEP), 0.0)
        elif axis == "y":
            block = BX * XSTEP
            jump = block - (BY - 1) * EZ
            from_hi = jnp.where(self.j > 0, self.roll(hi, EZ), self.roll(hi, jump))
            from_lo = jnp.where(self.j < BY - 1, self.roll(lo, -EZ), self.roll(lo, -jump))
            first = (self.j == 0) & (self.lane < block)
            last = (self.j == BY - 1) & (self.lane >= self.lanes - block)
            new_lo = lo + jnp.where(first, 0.0, from_hi)
            new_hi = hi + jnp.where(last, 0.0, from_lo)
        else:
            new_lo = lo + jnp.where(self.s > 0, self.roll(hi, 1), 0.0)
            new_hi = hi + jnp.where(self.s < EZ - 1, self.roll(lo, -1), 0.0)
        return new_lo, new_hi

    def assemble(self, ref):
        for b in range(NP):
            lo, hi = rows(0, b), rows(NP - 1, b)
            ref[lo, :], ref[hi, :] = self.share(ref[lo, :], ref[hi, :], "x")
        for a in range(NP):
            lo, hi = rows(a, 0), rows(a, NP - 1)
            ref[lo, :], ref[hi, :] = self.share(ref[lo, :], ref[hi, :], "y")
        for a in range(NP):
            lo, hi = self.share(column(ref, PLANE * a), column(ref, PLANE * a + NP - 1), "z")
            put_column(ref, PLANE * a, lo)
            put_column(ref, PLANE * a + NP - 1, hi)

    def plane_product(self, f_ref, base, out_ref):
        z = apply_stiff([column(f_ref, base + c) for c in range(NP)])
        for c in range(NP):
            put_column(out_ref, c, self.w * z[c])
        y = apply_stiff([f_ref[pl.ds(base + NP * b, NP), :] for b in range(NP)])
        return [self.w * y[b] + out_ref[pl.ds(NP * b, NP), :] for b in range(NP)]

    def local(self, f_ref, reaction_ref, out_ref, tmp_ref):
        for a in range(NP):
            flat = self.plane_product(f_ref, PLANE * a, tmp_ref)
            wa = float(WEIGHTS[a])
            for b in range(NP):
                r = rows(a, b)
                mass = (wa * float(WEIGHTS[b])) * self.w
                out_ref[r, :] = wa * flat[b] + (reaction_ref[r, :] * mass) * f_ref[r, :]
        for b in range(NP):
            x = apply_stiff([f_ref[rows(a, b), :] for a in range(NP)])
            wb = float(WEIGHTS[b]) * self.w
            for a in range(NP):
                r = rows(a, b)
                out_ref[r, :] = out_ref[r, :] + wb * x[a]

    def count_weights(self):
        nb = self.has_neighbour()
        one = jnp.ones((NP, self.lanes), jnp.float32)
        x0 = jnp.where(~self.lower | nb, 0.5, one)
        x7 = jnp.where(self.lower | nb, 0.5, one)
        block = BX * XSTEP
        first = (self.j == 0) & (self.lane < block)
        last = (self.j == BY - 1) & (self.lane >= self.lanes - block)
        y0 = jnp.where(first, one, 0.5)
        y7 = jnp.where(last, one, 0.5)
        z = jnp.where((self.row == 0) & (self.s > 0), 0.5, one)
        z = jnp.where((self.row == NP - 1) & (self.s < EZ - 1), 0.5, z)
        zx = [z * x0, z, z * x7]
        return [[m * y0, m, m * y7] for m in zx]


def place(a):
    return 0 if a == 0 else (2 if a == NP - 1 else 1)


def rows(a, b):
    return pl.ds(PLANE * a + NP * b, NP)


def column(ref, start):
    if ref.shape[1] == LANES:
        return ref[pl.ds(start, NP, stride=NP), :]
    return jnp.concatenate([ref[pl.ds(start + NP * b, 1), :] for b in range(NP)], axis=0)


def put_column(ref, start, value):
    if ref.shape[1] == LANES:
        ref[pl.ds(start, NP, stride=NP), :] = value
    else:
        for b in range(NP):
            ref[pl.ds(start + NP * b, 1), :] = value[b : b + 1, :]


def pack_face(grid, face, write):
    u = lax.axis_index("wide")
    even = (u % 2) == 0
    for b in range(NP // 2):
        top, bottom = face[b], face[b + NP // 2]
        up = jnp.where(grid.lower, grid.roll(bottom, -XSTEP), top)
        down = jnp.where(grid.lower, top, grid.roll(bottom, XSTEP))
        write(b, jnp.where(even, up, down), jnp.where(even, down, up))


def unpack_face(grid, read_a, read_b, nb):
    u = lax.axis_index("wide")
    even = (u % 2) == 0
    tops, bottoms = [], []
    for b in range(NP // 2):
        first, second = read_a(b), read_b(b)
        from_up = jnp.where(even, first, second)
        from_down = jnp.where(even, second, first)
        top = jnp.where(grid.lower, grid.roll(from_down, -XSTEP), grid.roll(from_up, XSTEP))
        bottom = jnp.where(grid.lower, from_down, from_up)
        tops.append(jnp.where(nb, top, 0.0))
        bottoms.append(jnp.where(nb, bottom, 0.0))
    return tops + bottoms


def pack_kernel(source_ref, reaction_ref, place_ref, out_ref):
    v = lax.axis_index("narrow")
    per = source_ref.shape[1]
    groups = LANES // per
    block = PTS // groups
    shift = (v % groups) * per
    for k, ref in enumerate((source_ref, reaction_ref)):
        dense = jnp.concatenate([ref[block * g : block * (g + 1), :] for g in range(groups)], axis=1)
        out_ref[block * k : block * (k + 1), :] = pltpu.roll(dense, shift, axis=1)
    row = lax.broadcasted_iota(jnp.int32, (NP, LANES), 0)
    lane = lax.broadcasted_iota(jnp.int32, (NP, LANES), 1)
    position = row * LANES + lane
    owner = jnp.zeros((NP, LANES), jnp.int32)
    for col in range(per):
        owner = jnp.where(position == place_ref[col], v * per + (col + 1), owner)
    out_ref[2 * block : 2 * block + NP, :] = owner.astype(jnp.float32)


def first_kernel(per, narrow, wide, got_ref, rhs_ref, reaction_ref, msg_a_ref, msg_b_ref, owner_ref):
    groups = LANES // per
    block = PTS // groups
    lanes = per * narrow
    grid = Grid(lanes, wide)
    total = got_ref[0, 2 * block : 2 * block + NP, :]
    for v in range(1, narrow):
        total = total + got_ref[v, 2 * block : 2 * block + NP, :]
    owner_ref[...] = total.astype(jnp.int32) - 1
    lane = lax.broadcasted_iota(jnp.int32, (NP, LANES), 1)
    tiles = []
    for t in range(lanes // LANES):
        owner = jnp.broadcast_to(owner_ref[t : t + 1, :], (NP, LANES))
        tiles.append((owner // per, owner % per))
    spot = lane // per
    for m in range(groups):
        idx = [per * ((v + m) % groups) + col for v, col in tiles]
        for k, ref in enumerate((rhs_ref, reaction_ref)):
            for r in range(block // NP):
                where_in = pl.ds(block * k + NP * r, NP)
                picks = []
                for h in range(narrow // groups):
                    pick = got_ref[groups * h + (0 - m) % groups, where_in, :]
                    for g in range(1, groups):
                        pick = jnp.where(
                            spot == g, got_ref[groups * h + (g - m) % groups, where_in, :], pick
                        )
                    picks.append(pick)
                at = block * m + NP * r
                a, b = at // PLANE, (at % PLANE) // NP
                for t, (v, col) in enumerate(tiles):
                    value = jnp.take_along_axis(picks[0], idx[t], axis=1)
                    for h in range(1, narrow // groups):
                        other = jnp.take_along_axis(picks[h], idx[t], axis=1)
                        value = jnp.where(v // groups == h, other, value)
                    if k == 0:
                        mass = float(WEIGHTS[a]) * float(WEIGHTS[b])
                        value = value * (mass * grid.w[:, t * LANES : (t + 1) * LANES])
                    ref[pl.ds(at, NP), t * LANES : (t + 1) * LANES] = value
    grid.assemble(rhs_ref)

    def write(part):
        def put(b, first, second):
            msg_a_ref[pl.ds(part * HALF + NP * b, NP), :] = first
            msg_b_ref[pl.ds(part * HALF + NP * b, NP), :] = second

        return put

    last = NP - 1
    pack_face(
        grid,
        [jnp.where(grid.lower, rhs_ref[rows(0, b), :], rhs_ref[rows(last, b), :]) for b in range(NP)],
        write(0),
    )
    part = []
    for b in range(NP):
        f = [rhs_ref[rows(a, b), :] for a in range(NP)]
        low = sum_of([float(STIFF[0, a]) * f[a] for a in range(1, NP)])
        high = sum_of([float(STIFF[last, a]) * f[a] for a in range(last)])
        part.append((float(WEIGHTS[b]) * grid.w) * jnp.where(grid.lower, low, high))
    pack_face(grid, part, write(1))
    pack_face(
        grid,
        [
            jnp.where(grid.lower, reaction_ref[rows(0, b), :], reaction_ref[rows(last, b), :])
            for b in range(NP)
        ],
        write(2),
    )


def second_kernel(
    wide,
    rhs_ref,
    reaction_ref,
    got_a_ref,
    got_b_ref,
    v0_ref,
    v1_ref,
    v2_ref,
    msg_a_ref,
    msg_b_ref,
    sums_ref,
    face_ref,
    tmp_ref,
):
    lanes = rhs_ref.shape[1]
    grid = Grid(lanes, wide)
    nb = grid.has_neighbour()
    last = NP - 1

    def reader(part):
        def first(b):
            return got_a_ref[pl.ds(part * HALF + NP * b, NP), :]

        def second(b):
            return got_b_ref[pl.ds(part * HALF + NP * b, NP), :]

        return first, second

    extra = unpack_face(grid, *reader(0), nb)
    v0_ref[...] = rhs_ref[...]
    for b in range(NP):
        low = rhs_ref[rows(0, b), :] + jnp.where(grid.lower, extra[b], 0.0)
        high = rhs_ref[rows(last, b), :] + jnp.where(grid.lower, 0.0, extra[b])
        v0_ref[rows(0, b), :] = low
        v0_ref[rows(last, b), :] = high
        face_ref[pl.ds(NP * b, NP), :] = jnp.where(grid.lower, low, high)
    grid.local(v0_ref, reaction_ref, v1_ref, tmp_ref)
    flat = grid.plane_product(face_ref, 0, tmp_ref)
    slopes = unpack_face(grid, *reader(1), nb)
    reactions = unpack_face(grid, *reader(2), nb)
    for b in range(NP):
        wb = float(WEIGHTS[b]) * grid.w
        face = face_ref[pl.ds(NP * b, NP), :]
        own = float(WEIGHTS[0]) * flat[b] + wb * (
            float(STIFF[0, 0]) * face + (float(WEIGHTS[0]) * reactions[b]) * face
        )
        more = jnp.where(nb, slopes[b] + own, 0.0)
        low, high = rows(0, b), rows(last, b)
        v1_ref[low, :] = v1_ref[low, :] + jnp.where(grid.lower, more, 0.0)
        v1_ref[high, :] = v1_ref[high, :] + jnp.where(grid.lower, 0.0, more)
    grid.assemble(v1_ref)
    grid.local(v1_ref, reaction_ref, v2_ref, tmp_ref)
    weight = grid.count_weights()
    parts = [[], [], [], []]
    for a in range(NP):
        terms = [[], [], [], []]
        for b in range(NP):
            r = rows(a, b)
            v0, v1, v2 = v0_ref[r, :], v1_ref[r, :], v2_ref[r, :]
            wt = weight[place(a)][place(b)]
            w1 = wt * v1
            for t, value in zip(terms, ((wt * v0) * v0, w1 * v0, w1 * v1, v1 * v2)):
                t.append(value)
        for p, t in zip(parts, terms):
            p.append(sum_of(t))
    row = grid.row
    out = jnp.zeros((NP, lanes), jnp.float32)
    for k, p in enumerate(parts):
        total = jnp.sum(sum_of(p), axis=0, keepdims=True)
        out = jnp.where(row == k, jnp.broadcast_to(total, (NP, lanes)), out)
    sums_ref[...] = out
    grid.assemble(v2_ref)

    def write(b, first, second):
        msg_a_ref[pl.ds(NP * b, NP), :] = first
        msg_b_ref[pl.ds(NP * b, NP), :] = second

    pack_face(
        grid,
        [jnp.where(grid.lower, v2_ref[rows(0, b), :], v2_ref[rows(last, b), :]) for b in range(NP)],
        write,
    )


def last_kernel(
    per, wide, v0_ref, v1_ref, v2_ref, got_a_ref, got_b_ref, sums_ref, solution_ref, strong_ref
):
    lanes = v0_ref.shape[1]
    grid = Grid(lanes, wide)
    nb = grid.has_neighbour()
    last = NP - 1
    v = lax.axis_index("narrow")
    shift = (lanes - v * per) % lanes
    extra = unpack_face(
        grid,
        lambda b: got_a_ref[pl.ds(NP * b, NP), :],
        lambda b: got_b_ref[pl.ds(NP * b, NP), :],
        nb,
    )
    g = [jnp.sum(sums_ref[k : k + 1, :], axis=1, keepdims=True) for k in range(4)]
    alpha = g[0] / g[1]
    norm = g[0] - 2.0 * alpha * g[1] + (alpha * alpha) * g[2]
    beta = norm / g[0]
    one = 1.0 + beta
    curve = one * one * g[1] - 2.0 * one * alpha * g[2] + (alpha * alpha) * g[3]
    step = norm / curve
    first = jnp.broadcast_to(alpha + step * one, (NP, lanes))
    second = jnp.broadcast_to(alpha * step, (NP, lanes))
    weight = grid.count_weights()
    inverse = 1.0 / grid.w
    weight = [[w * inverse for w in line] for line in weight]
    for a in range(NP):
        for b in range(NP):
            r = rows(a, b)
            v0, v1, v2 = v0_ref[r, :], v1_ref[r, :], v2_ref[r, :]
            if a == 0:
                v2 = v2 + jnp.where(grid.lower, extra[b], 0.0)
            if a == last:
                v2 = v2 + jnp.where(grid.lower, 0.0, extra[b])
            out = first * v0 - second * v1
            left = v0 - first * v1 + second * v2
            scale = float(1.0 / (WEIGHTS[a] * WEIGHTS[b]))
            left = left * (scale * weight[place(a)][place(b)])
            solution_ref[r, :] = pltpu.roll(out, shift, axis=1)[:, :per]
            strong_ref[r, :] = pltpu.roll(left, shift, axis=1)[:, :per]


VM = pl.BlockSpec(memory_space=pltpu.VMEM)
SM = pl.BlockSpec(memory_space=pltpu.SMEM)


def call(kernel, out_shapes, in_specs, scratch=(), name=None):
    return pl.pallas_call(
        kernel,
        out_shape=[jax.ShapeDtypeStruct(s, jnp.float32) for s in out_shapes],
        in_specs=in_specs,
        out_specs=[VM] * len(out_shapes),
        scratch_shapes=list(scratch),
        compiler_params=pltpu.CompilerParams(vmem_limit_bytes=16 * 1024 * 1024),
        name=name,
    )


def exchange(first, second, wide):
    pairs = [(u, u ^ 1) for u in range(wide)]
    across = [(u, min(max(u + 1 if u % 2 else u - 1, 0), wide - 1)) for u in range(wide)]
    return lax.ppermute(first, "wide", pairs), lax.ppermute(second, "wide", across)


def reduce_wide(sums, wide):
    if wide & (wide - 1):
        return lax.psum(sums, "wide")
    hop = 1
    while hop < wide:
        sums = sums + lax.ppermute(sums, "wide", [(u, u ^ hop) for u in range(wide)])
        hop *= 2
    return sums


def local(wide, narrow, source_old, reaction_old, new_place):
    per = source_old.shape[1]
    lanes = per * narrow
    packed = call(pack_kernel, [(2 * PTS * per // LANES + NP, LANES)], [VM, VM, SM], name="pack")(
        source_old, reaction_old, new_place
    )[0]
    got = lax.all_gather(packed, "narrow")
    full = (PTS, lanes)
    rhs, reaction, msg_a, msg_b = call(
        functools.partial(first_kernel, per, narrow, wide),
        [full, full, (3 * HALF, lanes), (3 * HALF, lanes)],
        [VM],
        [pltpu.VMEM((NP, LANES), jnp.int32)],
        name="first",
    )(got)
    got_a, got_b = exchange(msg_a, msg_b, wide)
    v0, v1, v2, msg_a, msg_b, sums = call(
        functools.partial(second_kernel, wide),
        [full, full, full, (HALF, lanes), (HALF, lanes), (NP, lanes)],
        [VM] * 4,
        [pltpu.VMEM((PLANE, lanes), jnp.float32), pltpu.VMEM((PLANE, lanes), jnp.float32)],
        name="second",
    )(rhs, reaction, got_a, got_b)
    got_a, got_b = exchange(msg_a, msg_b, wide)
    sums = reduce_wide(sums, wide)
    return tuple(
        call(
            functools.partial(last_kernel, per, wide),
            [(PTS, per), (PTS, per)],
            [VM] * 6,
            name="last",
        )(v0, v1, v2, got_a, got_b, sums)
    )


def solution(mesh):
    placed = (P(None, ("wide", "narrow")), P(None, ("wide", "narrow")), P(("wide", "narrow")))
    return jax.shard_map(
        functools.partial(local, mesh.shape["wide"], mesh.shape["narrow"]),
        mesh=mesh,
        in_specs=placed,
        out_specs=(P(None, ("wide", "narrow")), P(None, ("wide", "narrow"))),
        check_vma=False,
    )
```

profile of v0, /device:TPU:0, one launch (start us, length us, event | category | flops | bytes accessed | tf_op | source)
XLA Modules:
  0.0 39.2 jit_solution(13691145046638069932)
XLA Ops:
  0.6 0.0 copy-start.1
  0.6 1.0 %copy.5.source_ref = f32[512,32]{1,0:T(8,128)S(1)} copy(f32[512,32]{0,1:T(8,128)} %param.3) | data formatting | bytes 131072 | tf_op args[0]
  1.6 0.0 copy-done.1
  1.6 0.0 copy-start
  1.7 0.1 copy.6.reaction_ref
  1.8 0.5 %copy-done = s32[32]{0:T(128)S(1)} copy-done((s32[32]{0:T(128)S(1)}, s32[32]{0:T(128)}, u32[]{:S(2)}) %copy-start) | copy-done | bytes 152
  2.3 0.8 %pack.1 = f32[264,128]{1,0:T(8,128)S(1)} custom-call(f32[512,32]{1,0:T(8,128)S(1)} %copy.5.source_ref, f32[512,32]{1,0:T(8,128)S(1)} %copy.6.reaction_ref, s32[32]{0:T(128)S(1)} %copy-done), custom_call_target="tpu_custom_call" | custom-call | tf_op jit(solution)/shard_map/pack/pallas_call | solution.py:478
  3.1 8.7 %all-gather = f32[1056,128]{1,0:T(8,128)S(1)} all-gather(f32[264,128]{1,0:T(8,128)S(1)} %pack.1), channel_id=2, replica_groups=mesh['wide'=8,'narrow'=4] {'narrow'}, dimensions={0}, use_global_device_ids=true | all-gather | bytes 675840 | tf_op jit(solution)/shard_map/all_gather | solution.py:481
  11.9 0.5 %first.1 = (f32[512,128]{1,0:T(8,128)S(1)}, f32[512,128]{1,0:T(8,128)S(1)}, f32[96,128]{1,0:T(8,128)S(1)}, f32[96,128]{1,0:T(8,128)S(1)}) custom-call(f32[4,264,128]{2,1,0:T(8,128)S(1)} %bitcast.1), custom_call_target="tpu_custom_call" | custom-call | tf_op jit(solution)/shard_map/first/pallas_call | solution.py:483
  12.4 1.6 %collective-permute-start = (f32[96,128]{1,0:T(8,128)S(1)}, f32[96,128]{1,0:T(8,128)S(1)}, u32[]{:S(2)}, u32[]{:S(2)}) collective-permute-start(f32[96,128]{1,0:T(8,128)S(1)} %get-tuple-element.14), channel_id=1, source_target_pairs={{0,4},{4,0},{8,12},{12,8},{16,20},{20,16},{24,28},{28,24},{1,5},{5... | collective-permute-start | bytes 147464 | tf_op jit(solution)/shard_map/ppermute | solution.py:462
  14.0 0.7 %collective-permute-start.1 = (f32[96,128]{1,0:T(8,128)S(1)}, f32[96,128]{1,0:T(8,128)S(1)}, u32[]{:S(2)}, u32[]{:S(2)}) collective-permute-start(f32[96,128]{1,0:T(8,128)S(1)} %get-tuple-element.15), channel_id=1, source_target_pairs={{0,0},{4,8},{8,4},{12,16},{16,12},{20,24},{24,20},{28,28},{1,1},{5... | collective-permute-start | bytes 147464 | tf_op jit(solution)/shard_map/ppermute | solution.py:462
  14.7 1.9 %collective-permute-done.got_a_ref = f32[96,128]{1,0:T(8,128)S(1)} collective-permute-done((f32[96,128]{1,0:T(8,128)S(1)}, f32[96,128]{1,0:T(8,128)S(1)}, u32[]{:S(2)}, u32[]{:S(2)}) %collective-permute-start) | collective-permute-done | bytes 49184 | tf_op jit(solution)/shard_map/ppermute | solution.py:462
  16.6 0.0 collective-permute-done.1.got_b_ref
  16.6 1.2 %second.1 = (f32[512,128]{1,0:T(8,128)S(1)}, f32[512,128]{1,0:T(8,128)S(1)}, f32[512,128]{1,0:T(8,128)S(1)}, f32[32,128]{1,0:T(8,128)S(1)}, f32[32,128]{1,0:T(8,128)S(1)}, /*index=5*/f32[8,128]{1,0:T(8,128)S(1)}) custom-call(f32[512,128]{1,0:T(8,128)S(1)} %get-tuple-element.12.rhs_ref, f32[512,128]{1,0:T(8,128)S(1)} %get-tuple-element.13.reaction_ref, ...), custom_call_target="tpu_custom_call" | custom-call | tf_op jit(solution)/shard_map/second/pallas_call | solution.py:491
  17.8 4.9 %collective-permute-start.2 = (f32[32,128]{1,0:T(8,128)S(1)}, f32[32,128]{1,0:T(8,128)S(1)}, u32[]{:S(2)}, u32[]{:S(2)}) collective-permute-start(f32[32,128]{1,0:T(8,128)S(1)} %get-tuple-element.19), channel_id=1, source_target_pairs={{0,4},{4,0},{8,12},{12,8},{16,20},{20,16},{24,28},{28,24},{1,5},{5... | collective-permute-start | bytes 49160 | tf_op jit(solution)/shard_map/ppermute | solution.py:462
  22.6 0.7 %collective-permute-start.3 = (f32[32,128]{1,0:T(8,128)S(1)}, f32[32,128]{1,0:T(8,128)S(1)}, u32[]{:S(2)}, u32[]{:S(2)}) collective-permute-start(f32[32,128]{1,0:T(8,128)S(1)} %get-tuple-element.20), channel_id=1, source_target_pairs={{0,0},{4,8},{8,4},{12,16},{16,12},{20,24},{24,20},{28,28},{1,1},{5... | collective-permute-start | bytes 49160 | tf_op jit(solution)/shard_map/ppermute | solution.py:462
  23.3 4.4 %collective-permute-start.4 = (f32[8,128]{1,0:T(8,128)S(1)}, f32[8,128]{1,0:T(8,128)S(1)}, u32[]{:S(2)}, u32[]{:S(2)}) collective-permute-start(f32[8,128]{1,0:T(8,128)S(1)} %get-tuple-element.21), channel_id=1, source_target_pairs={{0,4},{4,0},{8,12},{12,8},{16,20},{20,16},{24,28},{28,24},{1,5},{5... | collective-permute-start | bytes 12296 | tf_op jit(solution)/shard_map/ppermute | solution.py:470
  27.6 1.6 %collective-permute-done.4 = f32[8,128]{1,0:T(8,128)S(1)} collective-permute-done((f32[8,128]{1,0:T(8,128)S(1)}, f32[8,128]{1,0:T(8,128)S(1)}, u32[]{:S(2)}, u32[]{:S(2)}) %collective-permute-start.4) | collective-permute-done | bytes 4128 | tf_op jit(solution)/shard_map/ppermute | solution.py:470
  29.2 1.6 %collective-permute-start.5 = (f32[8,128]{1,0:T(8,128)S(1)}, f32[8,128]{1,0:T(8,128)S(1)}, u32[]{:S(2)}, u32[]{:S(2)}) collective-permute-start(f32[8,128]{1,0:T(8,128)S(1)} %add.9), channel_id=1, source_target_pairs={{0,8},{4,12},{8,0},{12,4},{16,24},{20,28},{24,16},{28,20},{1,9},{5... | collective-permute-start | bytes 12296 | tf_op jit(solution)/shard_map/ppermute | solution.py:470
  30.8 2.0 %collective-permute-done.5 = f32[8,128]{1,0:T(8,128)S(1)} collective-permute-done((f32[8,128]{1,0:T(8,128)S(1)}, f32[8,128]{1,0:T(8,128)S(1)}, u32[]{:S(2)}, u32[]{:S(2)}) %collective-permute-start.5) | collective-permute-done | bytes 4128 | tf_op jit(solution)/shard_map/ppermute | solution.py:470
  32.8 3.0 %collective-permute-start.6 = (f32[8,128]{1,0:T(8,128)S(1)}, f32[8,128]{1,0:T(8,128)S(1)}, u32[]{:S(2)}, u32[]{:S(2)}) collective-permute-start(f32[8,128]{1,0:T(8,128)S(1)} %add.10), channel_id=1, source_target_pairs={{0,16},{4,20},{8,24},{12,28},{16,0},{20,4},{24,8},{28,12},{1,17},{... | collective-permute-start | bytes 12296 | tf_op jit(solution)/shard_map/ppermute | solution.py:470
  35.8 1.6 %collective-permute-done.6 = f32[8,128]{1,0:T(8,128)S(1)} collective-permute-done((f32[8,128]{1,0:T(8,128)S(1)}, f32[8,128]{1,0:T(8,128)S(1)}, u32[]{:S(2)}, u32[]{:S(2)}) %collective-permute-start.6) | collective-permute-done | bytes 4128 | tf_op jit(solution)/shard_map/ppermute | solution.py:470
  37.4 0.0 collective-permute-done.2.got_a_ref
  37.4 0.0 collective-permute-done.3.got_b_ref
  37.4 0.3 last.1
  37.8 0.7 %copy.7 = f32[512,32]{0,1:T(8,128)} copy(f32[512,32]{1,0:T(8,128)S(1)} %get-tuple-element.22) | data formatting | bytes 131072 | tf_op jit(solution)/shard_map/last/pallas_call | solution.py:501
  38.5 0.7 %copy.8 = f32[512,32]{0,1:T(8,128)} copy(f32[512,32]{1,0:T(8,128)S(1)} %get-tuple-element.23) | data formatting | bytes 131072 | tf_op jit(solution)/shard_map/last/pallas_call | solution.py:501
  (3 shorter events, 0.0 us)
Async XLA Ops:
  0.6 1.0 %copy-start.1 = (f32[512,32]{0,1:T(8,128)S(1)}, f32[512,32]{0,1:T(8,128)}, u32[]{:S(2)}) copy-start(f32[512,32]{0,1:T(8,128)} %param.4) | copy-start | bytes 196612
  1.6 0.7 %copy-start = (s32[32]{0:T(128)S(1)}, s32[32]{0:T(128)}, u32[]{:S(2)}) copy-start(s32[32]{0:T(128)} %place_ref.1) | copy-start | bytes 388
  12.4 4.2 %collective-permute-start = (f32[96,128]{1,0:T(8,128)S(1)}, f32[96,128]{1,0:T(8,128)S(1)}, u32[]{:S(2)}, u32[]{:S(2)}) collective-permute-start(f32[96,128]{1,0:T(8,128)S(1)} %get-tuple-element.14), channel_id=1, source_target_pairs={{0,4},{4,0},{8,12},{12,8},{16,20},{20,16},{24,28},{28,24},{1,5},{5... | collective-permute-start | bytes 147464 | tf_op jit(solution)/shard_map/ppermute | solution.py:462
  14.0 2.6 %collective-permute-start.1 = (f32[96,128]{1,0:T(8,128)S(1)}, f32[96,128]{1,0:T(8,128)S(1)}, u32[]{:S(2)}, u32[]{:S(2)}) collective-permute-start(f32[96,128]{1,0:T(8,128)S(1)} %get-tuple-element.15), channel_id=1, source_target_pairs={{0,0},{4,8},{8,4},{12,16},{16,12},{20,24},{24,20},{28,28},{1,1},{5... | collective-permute-start | bytes 147464 | tf_op jit(solution)/shard_map/ppermute | solution.py:462
  17.8 19.6 %collective-permute-start.2 = (f32[32,128]{1,0:T(8,128)S(1)}, f32[32,128]{1,0:T(8,128)S(1)}, u32[]{:S(2)}, u32[]{:S(2)}) collective-permute-start(f32[32,128]{1,0:T(8,128)S(1)} %get-tuple-element.19), channel_id=1, source_target_pairs={{0,4},{4,0},{8,12},{12,8},{16,20},{20,16},{24,28},{28,24},{1,5},{5... | collective-permute-start | bytes 49160 | tf_op jit(solution)/shard_map/ppermute | solution.py:462
  22.6 14.8 %collective-permute-start.3 = (f32[32,128]{1,0:T(8,128)S(1)}, f32[32,128]{1,0:T(8,128)S(1)}, u32[]{:S(2)}, u32[]{:S(2)}) collective-permute-start(f32[32,128]{1,0:T(8,128)S(1)} %get-tuple-element.20), channel_id=1, source_target_pairs={{0,0},{4,8},{8,4},{12,16},{16,12},{20,24},{24,20},{28,28},{1,1},{5... | collective-permute-start | bytes 49160 | tf_op jit(solution)/shard_map/ppermute | solution.py:462
  23.3 5.9 %collective-permute-start.4 = (f32[8,128]{1,0:T(8,128)S(1)}, f32[8,128]{1,0:T(8,128)S(1)}, u32[]{:S(2)}, u32[]{:S(2)}) collective-permute-start(f32[8,128]{1,0:T(8,128)S(1)} %get-tuple-element.21), channel_id=1, source_target_pairs={{0,4},{4,0},{8,12},{12,8},{16,20},{20,16},{24,28},{28,24},{1,5},{5... | collective-permute-start | bytes 12296 | tf_op jit(solution)/shard_map/ppermute | solution.py:470
  29.2 3.6 %collective-permute-start.5 = (f32[8,128]{1,0:T(8,128)S(1)}, f32[8,128]{1,0:T(8,128)S(1)}, u32[]{:S(2)}, u32[]{:S(2)}) collective-permute-start(f32[8,128]{1,0:T(8,128)S(1)} %add.9), channel_id=1, source_target_pairs={{0,8},{4,12},{8,0},{12,4},{16,24},{20,28},{24,16},{28,20},{1,9},{5... | collective-permute-start | bytes 12296 | tf_op jit(solution)/shard_map/ppermute | solution.py:470
  32.8 4.6 %collective-permute-start.6 = (f32[8,128]{1,0:T(8,128)S(1)}, f32[8,128]{1,0:T(8,128)S(1)}, u32[]{:S(2)}, u32[]{:S(2)}) collective-permute-start(f32[8,128]{1,0:T(8,128)S(1)} %add.10), channel_id=1, source_target_pairs={{0,16},{4,20},{8,24},{12,28},{16,0},{20,4},{24,8},{28,12},{1,17},{... | collective-permute-start | bytes 12296 | tf_op jit(solution)/shard_map/ppermute | solution.py:470
where the time goes:
time: 39.4 us; the launch traced here: 39.2 us
  starting transfers between devices  16.6 us (42%)
  blocking collectives  8.73 us (22%)
  waiting for transfers between devices  7.12 us (18%)
  local copies, waits for them, and re-layouts  3.12 us (8%)
  Pallas kernels  2.92 us (7%)
  between operations  0.7 us (2%)
    ppermute x3, starting transfers between devices, reduce_wide(): lax.ppermute(sums, 'wide', [(u, u ^ hop) for u in range(wide)])  8.9 us
    all_gather x1, blocking collectives, local(): got = lax.all_gather(packed, 'narrow')  8.73 us
    ppermute x2, starting transfers between devices, exchange(): lax.ppermute(first, 'wide', pairs)  6.44 us
    ppermute x3, waiting for transfers between devices, reduce_wide(): lax.ppermute(sums, 'wide', [(u, u ^ hop) for u in range(wide)])  5.2 us
    ppermute x2, waiting for transfers between devices, exchange(): lax.ppermute(first, 'wide', pairs)  1.91 us
    unnamed x6, local copies, waits for them, and re-layouts  1.64 us
    pallas_call x2, local copies, waits for them, and re-layouts, local(): call(functools.partial(last_kernel, per, wide), [(PTS, per), (PTS, per)],...  1.48 us
    ppermute x2, starting transfers between devices, exchange(): lax.ppermute(second, 'wide', across)  1.3 us
  transfers between devices with their start and end apart: 7, of which 4 were waited for; matrix products, arithmetic and copies ran while one was open for 0% of the time, Pallas kernels for 0%

commit v1 on v0

--- a/solution.py
+++ b/solution.py
@@ -223,63 +223,72 @@
     return tops + bottoms
 
 
-def pack_kernel(source_ref, reaction_ref, place_ref, out_ref):
+def pack_kernel(source_ref, reaction_ref, place_ref, out_ref, near_ref, sems):
+    per = source_ref.shape[0]
+    blocks = 2 * (PTS // LANES)
+    places = pltpu.make_async_copy(place_ref, near_ref, sems.at[blocks])
+    places.start()
+    copies = []
+    for k, ref in enumerate((source_ref, reaction_ref)):
+        for q in range(PTS // LANES):
+            n = len(copies)
+            copy = pltpu.make_async_copy(
+                ref.at[:, pl.ds(q * LANES, LANES)], out_ref.at[pl.ds(per * n, per), :], sems.at[n]
+            )
+            copy.start()
+            copies.append(copy)
     v = lax.axis_index("narrow")
-    per = source_ref.shape[1]
     groups = LANES // per
-    block = PTS // groups
-    shift = (v % groups) * per
-    for k, ref in enumerate((source_ref, reaction_ref)):
-        dense = jnp.concatenate([ref[block * g : block * (g + 1), :] for g in range(groups)], axis=1)
-        out_ref[block * k : block * (k + 1), :] = pltpu.roll(dense, shift, axis=1)
     row = lax.broadcasted_iota(jnp.int32, (NP, LANES), 0)
     lane = lax.broadcasted_iota(jnp.int32, (NP, LANES), 1)
-    position = row * LANES + lane
-    owner = jnp.zeros((NP, LANES), jnp.int32)
-    for col in range(per):
-        owner = jnp.where(position == place_ref[col], v * per + (col + 1), owner)
-    out_ref[2 * block : 2 * block + NP, :] = owner.astype(jnp.float32)
-
-
-def first_kernel(per, narrow, wide, got_ref, rhs_ref, reaction_ref, msg_a_ref, msg_b_ref, owner_ref):
+    mine = (row == v // groups) & (lane // per == v % groups)
+    places.wait()
+    places = jnp.concatenate([near_ref[...].astype(jnp.float32)] * groups, axis=1)
+    out_ref[per * blocks :, :] = jnp.where(mine, jnp.broadcast_to(places, (NP, LANES)), 0.0)
+    for copy in copies:
+        copy.wait()
+
+
+def first_kernel(per, narrow, wide, got_ref, rhs_ref, reaction_ref, msg_a_ref, msg_b_ref):
+    lanes = per * narrow
+    tiles = lanes // LANES
     groups = LANES // per
-    block = PTS // groups
-    lanes = per * narrow
+    blocks = PTS // LANES
     grid = Grid(lanes, wide)
-    total = got_ref[0, 2 * block : 2 * block + NP, :]
-    for v in range(1, narrow):
-        total = total + got_ref[v, 2 * block : 2 * block + NP, :]
-    owner_ref[...] = total.astype(jnp.int32) - 1
-    lane = lax.broadcasted_iota(jnp.int32, (NP, LANES), 1)
-    tiles = []
-    for t in range(lanes // LANES):
-        owner = jnp.broadcast_to(owner_ref[t : t + 1, :], (NP, LANES))
-        tiles.append((owner // per, owner % per))
-    spot = lane // per
-    for m in range(groups):
-        idx = [per * ((v + m) % groups) + col for v, col in tiles]
-        for k, ref in enumerate((rhs_ref, reaction_ref)):
-            for r in range(block // NP):
-                where_in = pl.ds(block * k + NP * r, NP)
-                picks = []
-                for h in range(narrow // groups):
-                    pick = got_ref[groups * h + (0 - m) % groups, where_in, :]
-                    for g in range(1, groups):
-                        pick = jnp.where(
-                            spot == g, got_ref[groups * h + (g - m) % groups, where_in, :], pick
+    spot = lax.broadcasted_iota(jnp.int32, (LANES, lanes), 1).astype(jnp.float32)
+    row = lax.broadcasted_iota(jnp.int32, (LANES, lanes), 0)
+    places = sum_of([got_ref[v, 2 * blocks * per :, :] for v in range(narrow)])
+    came = jnp.zeros((1, lanes), jnp.float32)
+    for t in range(tiles):
+        new = jnp.transpose(jnp.broadcast_to(places[t : t + 1, :], (LANES, LANES)))
+        new = jnp.concatenate([new] * tiles, axis=1)
+        old = (row + t * LANES).astype(jnp.float32)
+        came = came + jnp.sum(jnp.where(new == spot, old, 0.0), axis=0, keepdims=True)
+    came = jnp.broadcast_to(came.astype(jnp.int32), (NP, lanes))
+    for k, out_ref in enumerate((rhs_ref, reaction_ref)):
+        for q in range(blocks):
+            block = pl.ds(per * (blocks * k + q), per)
+            old = [
+                jnp.transpose(
+                    jnp.concatenate([got_ref[groups * t + g, block, :] for g in range(groups)], axis=0)
+                )
+                for t in range(tiles)
+            ]
+            for r in range(LANES // NP):
+                at = q * LANES + NP * r
+                a, b = at // PLANE, (at % PLANE) // NP
+                for t in range(tiles):
+                    owner = came[:, t * LANES : (t + 1) * LANES]
+                    value = None
+                    for h in range(tiles):
+                        pick = jnp.take_along_axis(
+                            old[h][NP * r : NP * (r + 1), :], owner % LANES, axis=1
                         )
-                    picks.append(pick)
-                at = block * m + NP * r
-                a, b = at // PLANE, (at % PLANE) // NP
-                for t, (v, col) in enumerate(tiles):
-                    value = jnp.take_along_axis(picks[0], idx[t], axis=1)
-                    for h in range(1, narrow // groups):
-                        other = jnp.take_along_axis(picks[h], idx[t], axis=1)
-                        value = jnp.where(v // groups == h, other, value)
+                        value = pick if value is None else jnp.where(owner // LANES == h, pick, value)
                     if k == 0:
                         mass = float(WEIGHTS[a]) * float(WEIGHTS[b])
                         value = value * (mass * grid.w[:, t * LANES : (t + 1) * LANES])
-                    ref[pl.ds(at, NP), t * LANES : (t + 1) * LANES] = value
+                    out_ref[pl.ds(at, NP), t * LANES : (t + 1) * LANES] = value
     grid.assemble(rhs_ref)
 
     def write(part):
@@ -323,7 +332,6 @@
     v2_ref,
     msg_a_ref,
     msg_b_ref,
-    sums_ref,
     face_ref,
     tmp_ref,
 ):
@@ -383,7 +391,8 @@
     for k, p in enumerate(parts):
         total = jnp.sum(sum_of(p), axis=0, keepdims=True)
         out = jnp.where(row == k, jnp.broadcast_to(total, (NP, lanes)), out)
-    sums_ref[...] = out
+    msg_a_ref[HALF : HALF + NP, :] = out
+    msg_b_ref[HALF : HALF + NP, :] = out
     grid.assemble(v2_ref)
 
     def write(b, first, second):
@@ -397,114 +406,194 @@
     )
 
 
+def own_kernel(per, wide, *refs):
+    *in_refs, scratch_ref = refs
+    vector_refs, out_refs = in_refs[:3], in_refs[3:]
+    lanes = vector_refs[0].shape[1]
+    grid = Grid(lanes, wide)
+    mine = pl.ds(pl.multiple_of(lax.axis_index("narrow") * per, per), per)
+    weight = grid.count_weights()
+    inverse = 1.0 / grid.w
+    weight = [[w * inverse for w in line] for line in weight]
+    for q in range(PTS // LANES):
+        lines = []
+        for r in range(LANES // NP):
+            at = q * LANES + NP * r
+            a, b = at // PLANE, (at % PLANE) // NP
+            lines.append(float(1.0 / (WEIGHTS[a] * WEIGHTS[b])) * weight[place(a)][place(b)])
+        scale = jnp.concatenate(lines, axis=0)
+        fields = [ref[q * LANES : (q + 1) * LANES, :] for ref in vector_refs] + [scale]
+        for k, (field, ref) in enumerate(zip(fields, out_refs)):
+            for t in range(lanes // LANES):
+                scratch_ref[k, t * LANES : (t + 1) * LANES, :] = jnp.transpose(
+                    field[:, t * LANES : (t + 1) * LANES]
+                )
+            ref[:, q * LANES : (q + 1) * LANES] = scratch_ref[k, mine, :]
+
+
 def last_kernel(
-    per, wide, v0_ref, v1_ref, v2_ref, got_a_ref, got_b_ref, sums_ref, solution_ref, strong_ref
+    wide,
+    v0_ref,
+    v1_ref,
+    v2_ref,
+    scale_ref,
+    got_a_ref,
+    got_b_ref,
+    twin_b_ref,
+    sums_ref,
+    twin_sums_ref,
+    solution_ref,
+    strong_ref,
+    face_ref,
+    turned_ref,
 ):
-    lanes = v0_ref.shape[1]
+    per = v0_ref.shape[0]
+    lanes = got_a_ref.shape[1]
     grid = Grid(lanes, wide)
     nb = grid.has_neighbour()
-    last = NP - 1
     v = lax.axis_index("narrow")
-    shift = (lanes - v * per) % lanes
+    core = v % 2
     extra = unpack_face(
         grid,
         lambda b: got_a_ref[pl.ds(NP * b, NP), :],
-        lambda b: got_b_ref[pl.ds(NP * b, NP), :],
+        lambda b: jnp.where(
+            core == 0, twin_b_ref[pl.ds(NP * b, NP), :], got_b_ref[pl.ds(NP * b, NP), :]
+        ),
         nb,
     )
-    g = [jnp.sum(sums_ref[k : k + 1, :], axis=1, keepdims=True) for k in range(4)]
+    for b in range(NP):
+        face_ref[pl.ds(NP * b, NP), :] = extra[b]
+        face_ref[pl.ds(PLANE + NP * b, NP), :] = extra[b]
+    for t in range(lanes // LANES):
+        turned_ref[t * LANES : (t + 1) * LANES, :] = jnp.transpose(
+            face_ref[:, t * LANES : (t + 1) * LANES]
+        )
+    face = turned_ref[pl.ds(pl.multiple_of(v * per, per), per), :]
+    spot = lax.broadcasted_iota(jnp.int32, (per, LANES), 1)
+    layer = lax.broadcasted_iota(jnp.int32, (per, LANES), 0) // XSTEP
+    ends = {
+        0: jnp.where((spot < PLANE) & (layer == 0), face, 0.0),
+        PTS // LANES - 1: jnp.where((spot >= PLANE) & (layer == BX - 1), face, 0.0),
+    }
+    total = sums_ref[...] + twin_sums_ref[...]
+    g = [jnp.sum(total[k : k + 1, :], axis=1, keepdims=True) for k in range(4)]
     alpha = g[0] / g[1]
     norm = g[0] - 2.0 * alpha * g[1] + (alpha * alpha) * g[2]
     beta = norm / g[0]
     one = 1.0 + beta
     curve = one * one * g[1] - 2.0 * one * alpha * g[2] + (alpha * alpha) * g[3]
     step = norm / curve
-    first = jnp.broadcast_to(alpha + step * one, (NP, lanes))
-    second = jnp.broadcast_to(alpha * step, (NP, lanes))
-    weight = grid.count_weights()
-    inverse = 1.0 / grid.w
-    weight = [[w * inverse for w in line] for line in weight]
-    for a in range(NP):
-        for b in range(NP):
-            r = rows(a, b)
-            v0, v1, v2 = v0_ref[r, :], v1_ref[r, :], v2_ref[r, :]
-            if a == 0:
-                v2 = v2 + jnp.where(grid.lower, extra[b], 0.0)
-            if a == last:
-                v2 = v2 + jnp.where(grid.lower, 0.0, extra[b])
-            out = first * v0 - second * v1
-            left = v0 - first * v1 + second * v2
-            scale = float(1.0 / (WEIGHTS[a] * WEIGHTS[b]))
-            left = left * (scale * weight[place(a)][place(b)])
-            solution_ref[r, :] = pltpu.roll(out, shift, axis=1)[:, :per]
-            strong_ref[r, :] = pltpu.roll(left, shift, axis=1)[:, :per]
+    first = jnp.broadcast_to(alpha + step * one, (per, LANES))
+    second = jnp.broadcast_to(alpha * step, (per, LANES))
+    for q in range(PTS // LANES):
+        at = (slice(None), slice(q * LANES, (q + 1) * LANES))
+        v0, v1, v2 = v0_ref[at], v1_ref[at], v2_ref[at]
+        if q in ends:
+            v2 = v2 + ends[q]
+        solution_ref[at] = first * v0 - second * v1
+        strong_ref[at] = (v0 - first * v1 + second * v2) * scale_ref[at]
 
 
 VM = pl.BlockSpec(memory_space=pltpu.VMEM)
-SM = pl.BlockSpec(memory_space=pltpu.SMEM)
-
-
-def call(kernel, out_shapes, in_specs, scratch=(), name=None):
+
+
+def call(kernel, out_shapes, in_specs, scratch=(), name=None, grant=16 * 1024 * 1024):
     return pl.pallas_call(
         kernel,
         out_shape=[jax.ShapeDtypeStruct(s, jnp.float32) for s in out_shapes],
         in_specs=in_specs,
         out_specs=[VM] * len(out_shapes),
         scratch_shapes=list(scratch),
-        compiler_params=pltpu.CompilerParams(vmem_limit_bytes=16 * 1024 * 1024),
+        compiler_params=pltpu.CompilerParams(vmem_limit_bytes=grant),
         name=name,
     )
 
 
-def exchange(first, second, wide):
-    pairs = [(u, u ^ 1) for u in range(wide)]
-    across = [(u, min(max(u + 1 if u % 2 else u - 1, 0), wide - 1)) for u in range(wide)]
-    return lax.ppermute(first, "wide", pairs), lax.ppermute(second, "wide", across)
-
-
-def reduce_wide(sums, wide):
-    if wide & (wide - 1):
-        return lax.psum(sums, "wide")
-    hop = 1
-    while hop < wide:
-        sums = sums + lax.ppermute(sums, "wide", [(u, u ^ hop) for u in range(wide)])
-        hop *= 2
-    return sums
+def swap(x, wide, narrow, *partner_of):
+    pairs = []
+    for u in range(wide):
+        to = [partner(u) for partner in partner_of]
+        idle = [not 0 <= t < wide for t in to]
+        for v in range(narrow):
+            k = v % len(to)
+            away = v ^ 1 if all(idle) else v ^ 2
+            target = u * narrow + away if idle[k] else to[k] * narrow + v
+            pairs.append((u * narrow + v, target))
+    return lax.ppermute(x, ("wide", "narrow"), pairs)
+
+
+def same_pair(u):
+    return u ^ 1
+
+
+def next_pair(u):
+    return u + 1 if u % 2 else u - 1
+
+
+def twin(x, narrow):
+    return lax.ppermute(x, "narrow", [(v, v ^ 1) for v in range(narrow)])
+
+
+def finish(msg_a, msg_b, wide, narrow):
+    got_a = swap(msg_a, wide, narrow, same_pair)
+    if wide == 8:
+        pair = msg_a[HALF:] + got_a[HALF:]
+        got_b = swap(
+            jnp.concatenate([msg_b[:HALF], pair], axis=0), wide, narrow, lambda u: u ^ 4, next_pair
+        )
+        more = swap(pair, wide, narrow, lambda u: u ^ 2, lambda u: u ^ 6)
+        even = lax.axis_index("narrow") % 2 == 0
+        sums = more + jnp.where(even, pair + got_b[HALF:], 0.0)
+        return got_a[:HALF], got_b[:HALF], twin(got_b[:HALF], narrow), sums, twin(sums, narrow)
+    got_b = swap(msg_b, wide, narrow, next_pair)[:HALF]
+    sums = lax.psum(msg_a[HALF:], "wide")
+    return got_a[:HALF], got_b, got_b, sums, jnp.zeros_like(sums)
 
 
 def local(wide, narrow, source_old, reaction_old, new_place):
     per = source_old.shape[1]
     lanes = per * narrow
-    packed = call(pack_kernel, [(2 * PTS * per // LANES + NP, LANES)], [VM, VM, SM], name="pack")(
-        source_old, reaction_old, new_place
-    )[0]
-    got = lax.all_gather(packed, "narrow")
+    blocks = 2 * (PTS // LANES)
+    packed = call(
+        pack_kernel,
+        [(blocks * per + NP, LANES)],
+        [pl.BlockSpec(memory_space=pltpu.HBM)] * 3,
+        [pltpu.VMEM((1, per), jnp.int32), pltpu.SemaphoreType.DMA((blocks + 1,))],
+        name="pack",
+        grant=None,
+    )(source_old.T, reaction_old.T, new_place.reshape(1, per))[0]
     full = (PTS, lanes)
     rhs, reaction, msg_a, msg_b = call(
         functools.partial(first_kernel, per, narrow, wide),
         [full, full, (3 * HALF, lanes), (3 * HALF, lanes)],
         [VM],
-        [pltpu.VMEM((NP, LANES), jnp.int32)],
         name="first",
-    )(got)
-    got_a, got_b = exchange(msg_a, msg_b, wide)
-    v0, v1, v2, msg_a, msg_b, sums = call(
+    )(lax.all_gather(packed, "narrow"))
+    got_a = swap(msg_a, wide, narrow, same_pair)
+    got_b = swap(msg_b, wide, narrow, next_pair)
+    v0, v1, v2, msg_a, msg_b = call(
         functools.partial(second_kernel, wide),
-        [full, full, full, (HALF, lanes), (HALF, lanes), (NP, lanes)],
+        [full, full, full, (HALF + NP, lanes), (HALF + NP, lanes)],
         [VM] * 4,
         [pltpu.VMEM((PLANE, lanes), jnp.float32), pltpu.VMEM((PLANE, lanes), jnp.float32)],
         name="second",
     )(rhs, reaction, got_a, got_b)
-    got_a, got_b = exchange(msg_a, msg_b, wide)
-    sums = reduce_wide(sums, wide)
-    return tuple(
-        call(
-            functools.partial(last_kernel, per, wide),
-            [(PTS, per), (PTS, per)],
-            [VM] * 6,
-            name="last",
-        )(v0, v1, v2, got_a, got_b, sums)
-    )
+    arrived = finish(msg_a, msg_b, wide, narrow)
+    own = call(
+        functools.partial(own_kernel, per, wide),
+        [(per, PTS)] * 4,
+        [VM] * 3,
+        [pltpu.VMEM((4, lanes, LANES), jnp.float32)],
+        name="own",
+    )(v0, v1, v2)
+    out = call(
+        functools.partial(last_kernel, wide),
+        [(per, PTS), (per, PTS)],
+        [VM] * 9,
+        [pltpu.VMEM((LANES, lanes), jnp.float32), pltpu.VMEM((lanes, LANES), jnp.float32)],
+        name="last",
+    )(*own, *arrived)
+    return tuple(x.T for x in out)
 
 
 def solution(mesh):

time: 39.4 us -> 31.9 us (0.81)
  starting transfers between devices: 16.6 us -> 10.3 us
  local copies, waits for them, and re-layouts: 3.12 us -> 0.01 us
  Pallas kernels: 2.92 us -> 4.62 us
    ppermute x7, starting transfers between devices: 16.6 us -> 10.3 us  [the longest x5 10.3 us: swap(): return lax.ppermute(x, ('wide', 'narrow'), pairs)]
    unnamed x6 -> x0, local copies, waits for them, and re-layouts: 1.64 us -> none
    pallas_call x3 -> x4, Pallas kernels: 2.38 us -> 3.92 us  [the longest x1 1.57 us: local(): call(pack_kernel, [(blocks * per + NP, LANES)], [pl.BlockSpec(memory_spac...]
    pallas_call x2 -> x0, local copies, waits for them, and re-layouts: 1.48 us -> none  [local(): call(functools.partial(last_kernel, per, wide), [(PTS, per), (PTS, per)],...]
  transfers between devices with their start and end apart: 7 -> 7, of which waited for: 4 -> 5; matrix products, arithmetic and copies ran while one was open for 0% -> 0% of each run, Pallas kernels for 0% -> 1%
where the time goes in v1:
time: 31.9 us; the launch traced here: 31.7 us
  starting transfers between devices  10.3 us (32%)
  blocking collectives  8.95 us (28%)
  waiting for transfers between devices  7.1 us (22%)
  Pallas kernels  4.62 us (14%)
  between operations  0.67 us (2%)
    ppermute x5, starting transfers between devices, swap(): return lax.ppermute(x, ('wide', 'narrow'), pairs)  10.3 us
    all_gather x1, blocking collectives, local(): lax.all_gather(packed, 'narrow')  8.95 us
    ppermute x5, waiting for transfers between devices, swap(): return lax.ppermute(x, ('wide', 'narrow'), pairs)  6.29 us
    pallas_call x1, Pallas kernels, local(): call(pack_kernel, [(blocks * per + NP, LANES)], [pl.BlockSpec(memory_spac...  1.57 us
    pallas_call x1, Pallas kernels, local(): call(functools.partial(second_kernel, wide), [full, full, full, (HALF + N...  1.16 us
    pallas_call x1, Pallas kernels, local(): call(functools.partial(last_kernel, wide), [(per, PTS), (per, PTS)], [VM]...  0.84 us
    ppermute x2, waiting for transfers between devices, twin(): return lax.ppermute(x, 'narrow', [(v, v ^ 1) for v in range(narrow)])  0.81 us
    pallas_call x1, Pallas kernels, local(): call(functools.partial(first_kernel, per, narrow, wide), [full, full, (3...  0.71 us
  transfers between devices with their start and end apart: 7, of which 5 were waited for; matrix products, arithmetic and copies ran while one was open for 0% of the time, Pallas kernels for 1%

profile of v1, /device:TPU:0, one launch (start us, length us, event | category | flops | bytes accessed | tf_op | source)
XLA Modules:
  0.0 31.7 jit_solution(3420675784714221428)
XLA Ops:
  0.6 1.6 %pack.1 = f32[264,128]{1,0:T(8,128)} custom-call(f32[32,512]{1,0:T(8,128)} %bitcast.7, f32[32,512]{1,0:T(8,128)} %bitcast.8, s32[1,32]{1,0:T(1,128)} %bitcast.9), custom_call_target="tpu_custom_call" | custom-call | tf_op jit(solution)/shard_map/pack/pallas_call | solution.py:557
  2.2 8.9 %all-gather = f32[1056,128]{1,0:T(8,128)S(1)} all-gather(f32[264,128]{1,0:T(8,128)} %pack.1), channel_id=2, replica_groups=mesh['wide'=8,'narrow'=4] {'narrow'}, dimensions={0}, use_global_device_ids=true | all-gather | bytes 675840 | tf_op jit(solution)/shard_map/all_gather | solution.py:571
  11.2 0.7 %first.1 = (f32[512,128]{1,0:T(8,128)S(1)}, f32[512,128]{1,0:T(8,128)S(1)}, f32[96,128]{1,0:T(8,128)S(1)}, f32[96,128]{1,0:T(8,128)S(1)}) custom-call(f32[4,264,128]{2,1,0:T(8,128)S(1)} %bitcast.6), custom_call_target="tpu_custom_call" | custom-call | tf_op jit(solution)/shard_map/first/pallas_call | solution.py:566
  11.9 1.6 %collective-permute-start = (f32[96,128]{1,0:T(8,128)S(1)}, f32[96,128]{1,0:T(8,128)S(1)}, u32[]{:S(2)}, u32[]{:S(2)}) collective-permute-start(f32[96,128]{1,0:T(8,128)S(1)} %get-tuple-element.19), channel_id=1, source_target_pairs={{0,4},{1,5},{2,6},{3,7},{4,0},{5,1},{6,2},{7,3},{8,12},{9,13},{10,... | collective-permute-start | bytes 147464 | tf_op jit(solution)/shard_map/ppermute | solution.py:522
  13.5 0.1 collective-permute-start.1
  13.5 2.5 %collective-permute-done.got_a_ref = f32[96,128]{1,0:T(8,128)S(1)} collective-permute-done((f32[96,128]{1,0:T(8,128)S(1)}, f32[96,128]{1,0:T(8,128)S(1)}, u32[]{:S(2)}, u32[]{:S(2)}) %collective-permute-start) | collective-permute-done | bytes 49184 | tf_op jit(solution)/shard_map/ppermute | solution.py:522
  16.0 0.0 collective-permute-done.1.got_b_ref
  16.0 1.2 %second.1 = (f32[512,128]{1,0:T(8,128)S(1)}, f32[512,128]{1,0:T(8,128)S(1)}, f32[512,128]{1,0:T(8,128)S(1)}, f32[40,128]{1,0:T(8,128)S(1)}, f32[40,128]{1,0:T(8,128)S(1)}) custom-call(f32[512,128]{1,0:T(8,128)S(1)} %get-tuple-element.17.rhs_ref, f32[512,128]{1,0:T(8,128)S(1)} %get-tuple-element.18.reaction_ref, ...), custom_call_target="tpu_custom_call" | custom-call | tf_op jit(solution)/shard_map/second/pallas_call | solution.py:574
  17.2 3.0 %collective-permute-start.2 = (f32[40,128]{1,0:T(8,128)S(1)}, f32[40,128]{1,0:T(8,128)S(1)}, u32[]{:S(2)}, u32[]{:S(2)}) collective-permute-start(f32[40,128]{1,0:T(8,128)S(1)} %get-tuple-element.28), channel_id=1, source_target_pairs={{0,4},{1,5},{2,6},{3,7},{4,0},{5,1},{6,2},{7,3},{8,12},{9,13},{10,... | collective-permute-start | bytes 61448 | tf_op jit(solution)/shard_map/ppermute | solution.py:522
  20.2 1.8 %collective-permute-done.2 = f32[40,128]{1,0:T(8,128)S(1)} collective-permute-done((f32[40,128]{1,0:T(8,128)S(1)}, f32[40,128]{1,0:T(8,128)S(1)}, u32[]{:S(2)}, u32[]{:S(2)}) %collective-permute-start.2) | collective-permute-done | bytes 20512 | tf_op jit(solution)/shard_map/ppermute | solution.py:522
  21.9 4.1 %collective-permute-start.3 = (f32[40,128]{1,0:T(8,128)S(1)}, f32[40,128]{1,0:T(8,128)S(1)}, u32[]{:S(2)}, u32[]{:S(2)}) collective-permute-start(f32[40,128]{1,0:T(8,128)S(1)} %pad_maximum_fusion), channel_id=1, source_target_pairs={{0,16},{1,3},{2,18},{3,1},{4,20},{5,9},{6,22},{7,11},{8,24},{9,5},... | collective-permute-start | bytes 61448 | tf_op jit(solution)/shard_map/ppermute | solution.py:522
  26.0 1.6 %collective-permute-start.5 = (f32[8,128]{1,0:T(8,128)S(1)}, f32[8,128]{1,0:T(8,128)S(1)}, u32[]{:S(2)}, u32[]{:S(2)}) collective-permute-start(f32[8,128]{1,0:T(8,128)S(1)} %slice_add_fusion.1), channel_id=1, source_target_pairs={{0,8},{1,25},{2,10},{3,27},{4,12},{5,29},{6,14},{7,31},{8,0},{9,17... | collective-permute-start | bytes 12296 | tf_op jit(solution)/shard_map/ppermute | solution.py:522
  27.6 0.2 collective-permute-done.3
  27.8 0.0 collective-permute-start.4
  27.8 1.8 %collective-permute-done.5 = f32[8,128]{1,0:T(8,128)S(1)} collective-permute-done((f32[8,128]{1,0:T(8,128)S(1)}, f32[8,128]{1,0:T(8,128)S(1)}, u32[]{:S(2)}, u32[]{:S(2)}) %collective-permute-start.5) | collective-permute-done | bytes 4128 | tf_op jit(solution)/shard_map/ppermute | solution.py:522
  29.6 0.0 collective-permute-start.6
  29.7 0.3 %own.1 = (f32[32,512]{1,0:T(8,128)S(1)}, f32[32,512]{1,0:T(8,128)S(1)}, f32[32,512]{1,0:T(8,128)S(1)}, f32[32,512]{1,0:T(8,128)S(1)}) custom-call(f32[512,128]{1,0:T(8,128)S(1)} %get-tuple-element.21.refs_0_, f32[512,128]{1,0:T(8,128)S(1)} %get-tuple-element.22.refs_1_, f32[512,128]{1,0:T(8,128)S(1)} %get-tuple-element.23.refs_2_), custom_call_target="tpu_custom_call" | custom-call | tf_op jit(solution)/shard_map/own/pallas_call | solution.py:582
  30.0 0.8 %collective-permute-done.6.twin_sums_ref = f32[8,128]{1,0:T(8,128)S(1)} collective-permute-done((f32[8,128]{1,0:T(8,128)S(1)}, f32[8,128]{1,0:T(8,128)S(1)}, u32[]{:S(2)}, u32[]{:S(2)}) %collective-permute-start.6) | collective-permute-done | bytes 4128 | tf_op jit(solution)/shard_map/ppermute | solution.py:534
  30.8 0.0 collective-permute-done.4.twin_b_ref
  30.8 0.8 %last.1 = (f32[32,512]{1,0:T(8,128)}, f32[32,512]{1,0:T(8,128)}) custom-call(f32[32,512]{1,0:T(8,128)S(1)} %get-tuple-element.24.v0_ref, f32[32,512]{1,0:T(8,128)S(1)} %get-tuple-element.25.v1_ref, f32[32,512]{1,0:T(8,128)S(1)} %get-tuple-element.26.v2_ref, f32[32,512]{1,0:T(8,128)S(1)} %get-tuple-element.27.scale_ref, f32[32,128]{1,0:T(8,128)S(1)} %slice.25.got_a_ref, ...), custom_call_target="tpu_custom_call" | custom-call | tf_op jit(solution)/shard_map/last/pallas_call | solution.py:589
  (6 shorter events, 0.0 us)
Async XLA Ops:
  11.9 4.2 %collective-permute-start = (f32[96,128]{1,0:T(8,128)S(1)}, f32[96,128]{1,0:T(8,128)S(1)}, u32[]{:S(2)}, u32[]{:S(2)}) collective-permute-start(f32[96,128]{1,0:T(8,128)S(1)} %get-tuple-element.19), channel_id=1, source_target_pairs={{0,4},{1,5},{2,6},{3,7},{4,0},{5,1},{6,2},{7,3},{8,12},{9,13},{10,... | collective-permute-start | bytes 147464 | tf_op jit(solution)/shard_map/ppermute | solution.py:522
  13.5 2.6 %collective-permute-start.1 = (f32[96,128]{1,0:T(8,128)S(1)}, f32[96,128]{1,0:T(8,128)S(1)}, u32[]{:S(2)}, u32[]{:S(2)}) collective-permute-start(f32[96,128]{1,0:T(8,128)S(1)} %get-tuple-element.20), channel_id=1, source_target_pairs={{0,1},{1,0},{2,3},{3,2},{4,8},{5,9},{6,10},{7,11},{8,4},{9,5},{10,... | collective-permute-start | bytes 147464 | tf_op jit(solution)/shard_map/ppermute | solution.py:522
  17.2 4.7 %collective-permute-start.2 = (f32[40,128]{1,0:T(8,128)S(1)}, f32[40,128]{1,0:T(8,128)S(1)}, u32[]{:S(2)}, u32[]{:S(2)}) collective-permute-start(f32[40,128]{1,0:T(8,128)S(1)} %get-tuple-element.28), channel_id=1, source_target_pairs={{0,4},{1,5},{2,6},{3,7},{4,0},{5,1},{6,2},{7,3},{8,12},{9,13},{10,... | collective-permute-start | bytes 61448 | tf_op jit(solution)/shard_map/ppermute | solution.py:522
  21.9 5.9 %collective-permute-start.3 = (f32[40,128]{1,0:T(8,128)S(1)}, f32[40,128]{1,0:T(8,128)S(1)}, u32[]{:S(2)}, u32[]{:S(2)}) collective-permute-start(f32[40,128]{1,0:T(8,128)S(1)} %pad_maximum_fusion), channel_id=1, source_target_pairs={{0,16},{1,3},{2,18},{3,1},{4,20},{5,9},{6,22},{7,11},{8,24},{9,5},... | collective-permute-start | bytes 61448 | tf_op jit(solution)/shard_map/ppermute | solution.py:522
  26.0 3.6 %collective-permute-start.5 = (f32[8,128]{1,0:T(8,128)S(1)}, f32[8,128]{1,0:T(8,128)S(1)}, u32[]{:S(2)}, u32[]{:S(2)}) collective-permute-start(f32[8,128]{1,0:T(8,128)S(1)} %slice_add_fusion.1), channel_id=1, source_target_pairs={{0,8},{1,25},{2,10},{3,27},{4,12},{5,29},{6,14},{7,31},{8,0},{9,17... | collective-permute-start | bytes 12296 | tf_op jit(solution)/shard_map/ppermute | solution.py:522
  27.8 3.0 %collective-permute-start.4 = (f32[32,128]{1,0:T(8,128)S(1)}, f32[32,128]{1,0:T(8,128)S(1)}, u32[]{:S(2)}, u32[]{:S(2)}) collective-permute-start(f32[32,128]{1,0:T(8,128)S(1)} %slice.27.got_b_ref), channel_id=1, source_target_pairs={{0,1},{1,0},{2,3},{3,2},{4,5},{5,4},{6,7},{7,6},{8,9},{9,8},{10,11... | collective-permute-start | bytes 49160 | tf_op jit(solution)/shard_map/ppermute | solution.py:534
  29.6 1.2 %collective-permute-start.6 = (f32[8,128]{1,0:T(8,128)S(1)}, f32[8,128]{1,0:T(8,128)S(1)}, u32[]{:S(2)}, u32[]{:S(2)}) collective-permute-start(f32[8,128]{1,0:T(8,128)S(1)} %fusion.1.sums_ref), channel_id=1, source_target_pairs={{0,1},{1,0},{2,3},{3,2},{4,5},{5,4},{6,7},{7,6},{8,9},{9,8},{10,11... | collective-permute-start | bytes 12296 | tf_op jit(solution)/shard_map/ppermute | solution.py:534

commit v2 on v1

--- a/solution.py
+++ b/solution.py
@@ -249,46 +249,61 @@
         copy.wait()
 
 
-def first_kernel(per, narrow, wide, got_ref, rhs_ref, reaction_ref, msg_a_ref, msg_b_ref):
+class Arrived:
+    def __init__(self, per, narrow, got_ref):
+        self.per = per
+        self.got = got_ref
+        self.tiles = per * narrow // LANES
+        self.groups = LANES // per
+        self.blocks = PTS // LANES
+        lanes = per * narrow
+        spot = lax.broadcasted_iota(jnp.int32, (LANES, lanes), 1).astype(jnp.float32)
+        row = lax.broadcasted_iota(jnp.int32, (LANES, lanes), 0)
+        places = sum_of([got_ref[v, 2 * self.blocks * per :, :] for v in range(narrow)])
+        came = jnp.zeros((1, lanes), jnp.float32)
+        for t in range(self.tiles):
+            new = jnp.transpose(jnp.broadcast_to(places[t : t + 1, :], (LANES, LANES)))
+            new = jnp.concatenate([new] * self.tiles, axis=1)
+            old = (row + t * LANES).astype(jnp.float32)
+            came = came + jnp.sum(jnp.where(new == spot, old, 0.0), axis=0, keepdims=True)
+        came = jnp.broadcast_to(came.astype(jnp.int32), (NP, lanes))
+        owners = [came[:, t * LANES : (t + 1) * LANES] for t in range(self.tiles)]
+        self.source = [(owner // LANES, owner % LANES) for owner in owners]
+
+    def block(self, field, q, t):
+        rows_of = pl.ds(self.per * (self.blocks * field + q), self.per)
+        return jnp.concatenate(
+            [self.got[self.groups * t + g, rows_of, :] for g in range(self.groups)], axis=0
+        )
+
+    def turned(self, old):
+        old = [jnp.transpose(x) for x in old]
+        for r in range(LANES // NP):
+            for t, (home, lane) in enumerate(self.source):
+                value = None
+                for h in range(self.tiles):
+                    pick = jnp.take_along_axis(old[h][NP * r : NP * (r + 1), :], lane, axis=1)
+                    value = pick if value is None else jnp.where(home == h, pick, value)
+                yield r, slice(t * LANES, (t + 1) * LANES), value
+
+
+def first_kernel(per, narrow, wide, got_ref, rhs_ref, msg_a_ref, msg_b_ref, ends_ref):
     lanes = per * narrow
-    tiles = lanes // LANES
-    groups = LANES // per
-    blocks = PTS // LANES
     grid = Grid(lanes, wide)
-    spot = lax.broadcasted_iota(jnp.int32, (LANES, lanes), 1).astype(jnp.float32)
-    row = lax.broadcasted_iota(jnp.int32, (LANES, lanes), 0)
-    places = sum_of([got_ref[v, 2 * blocks * per :, :] for v in range(narrow)])
-    came = jnp.zeros((1, lanes), jnp.float32)
-    for t in range(tiles):
-        new = jnp.transpose(jnp.broadcast_to(places[t : t + 1, :], (LANES, LANES)))
-        new = jnp.concatenate([new] * tiles, axis=1)
-        old = (row + t * LANES).astype(jnp.float32)
-        came = came + jnp.sum(jnp.where(new == spot, old, 0.0), axis=0, keepdims=True)
-    came = jnp.broadcast_to(came.astype(jnp.int32), (NP, lanes))
-    for k, out_ref in enumerate((rhs_ref, reaction_ref)):
-        for q in range(blocks):
-            block = pl.ds(per * (blocks * k + q), per)
-            old = [
-                jnp.transpose(
-                    jnp.concatenate([got_ref[groups * t + g, block, :] for g in range(groups)], axis=0)
-                )
-                for t in range(tiles)
-            ]
-            for r in range(LANES // NP):
-                at = q * LANES + NP * r
-                a, b = at // PLANE, (at % PLANE) // NP
-                for t in range(tiles):
-                    owner = came[:, t * LANES : (t + 1) * LANES]
-                    value = None
-                    for h in range(tiles):
-                        pick = jnp.take_along_axis(
-                            old[h][NP * r : NP * (r + 1), :], owner % LANES, axis=1
-                        )
-                        value = pick if value is None else jnp.where(owner // LANES == h, pick, value)
-                    if k == 0:
-                        mass = float(WEIGHTS[a]) * float(WEIGHTS[b])
-                        value = value * (mass * grid.w[:, t * LANES : (t + 1) * LANES])
-                    out_ref[pl.ds(at, NP), t * LANES : (t + 1) * LANES] = value
+    arrived = Arrived(per, narrow, got_ref)
+    tiles = range(arrived.tiles)
+    for q in range(arrived.blocks):
+        for r, cols, value in arrived.turned([arrived.block(0, q, t) for t in tiles]):
+            at = q * LANES + NP * r
+            a, b = at // PLANE, (at % PLANE) // NP
+            mass = float(WEIGHTS[a]) * float(WEIGHTS[b])
+            rhs_ref[pl.ds(at, NP), cols] = value * (mass * grid.w[:, cols])
+    low = lax.broadcasted_iota(jnp.int32, (LANES, LANES), 1) < PLANE
+    ends = [
+        jnp.where(low, arrived.block(1, 0, t), arrived.block(1, arrived.blocks - 1, t)) for t in tiles
+    ]
+    for r, cols, value in arrived.turned(ends):
+        ends_ref[pl.ds(NP * r, NP), cols] = value
     grid.assemble(rhs_ref)
 
     def write(part):
@@ -314,17 +329,37 @@
     pack_face(
         grid,
         [
-            jnp.where(grid.lower, reaction_ref[rows(0, b), :], reaction_ref[rows(last, b), :])
+            jnp.where(
+                grid.lower, ends_ref[pl.ds(NP * b, NP), :], ends_ref[pl.ds(PLANE + NP * b, NP), :]
+            )
             for b in range(NP)
         ],
         write(2),
     )
 
 
+def middle_kernel(per, narrow, wide, got_ref, rhs_ref, reaction_ref, part_ref, flat_ref, tmp_ref):
+    grid = Grid(per * narrow, wide)
+    arrived = Arrived(per, narrow, got_ref)
+    for q in range(arrived.blocks):
+        blocks = [arrived.block(1, q, t) for t in range(arrived.tiles)]
+        for r, cols, value in arrived.turned(blocks):
+            reaction_ref[pl.ds(q * LANES + NP * r, NP), cols] = value
+    grid.local(rhs_ref, reaction_ref, part_ref, tmp_ref)
+    for b in range(NP):
+        low, high = rhs_ref[rows(0, b), :], rhs_ref[rows(NP - 1, b), :]
+        flat_ref[pl.ds(NP * b, NP), :] = jnp.where(grid.lower, low, high)
+    flat = grid.plane_product(flat_ref, 0, tmp_ref)
+    for b in range(NP):
+        flat_ref[pl.ds(NP * b, NP), :] = flat[b]
+
+
 def second_kernel(
     wide,
     rhs_ref,
     reaction_ref,
+    part_ref,
+    flat0_ref,
     got_a_ref,
     got_b_ref,
     v0_ref,
@@ -350,27 +385,34 @@
         return first, second
 
     extra = unpack_face(grid, *reader(0), nb)
-    v0_ref[...] = rhs_ref[...]
-    for b in range(NP):
-        low = rhs_ref[rows(0, b), :] + jnp.where(grid.lower, extra[b], 0.0)
-        high = rhs_ref[rows(last, b), :] + jnp.where(grid.lower, 0.0, extra[b])
-        v0_ref[rows(0, b), :] = low
-        v0_ref[rows(last, b), :] = high
-        face_ref[pl.ds(NP * b, NP), :] = jnp.where(grid.lower, low, high)
-    grid.local(v0_ref, reaction_ref, v1_ref, tmp_ref)
-    flat = grid.plane_product(face_ref, 0, tmp_ref)
     slopes = unpack_face(grid, *reader(1), nb)
     reactions = unpack_face(grid, *reader(2), nb)
     for b in range(NP):
+        face_ref[pl.ds(NP * b, NP), :] = extra[b]
+    flat = grid.plane_product(face_ref, 0, tmp_ref)
+    pull = [jnp.where(grid.lower, float(STIFF[a, 0]), float(STIFF[a, last])) for a in range(NP)]
+    w0 = float(WEIGHTS[0])
+    for b in range(NP):
         wb = float(WEIGHTS[b]) * grid.w
-        face = face_ref[pl.ds(NP * b, NP), :]
-        own = float(WEIGHTS[0]) * flat[b] + wb * (
-            float(STIFF[0, 0]) * face + (float(WEIGHTS[0]) * reactions[b]) * face
+        more = wb * extra[b]
+        for a in range(1, last):
+            r = rows(a, b)
+            v0_ref[r, :] = rhs_ref[r, :]
+            v1_ref[r, :] = part_ref[r, :] + pull[a] * more
+        r_low, r_high = rows(0, b), rows(last, b)
+        low = rhs_ref[r_low, :] + jnp.where(grid.lower, extra[b], 0.0)
+        high = rhs_ref[r_high, :] + jnp.where(grid.lower, 0.0, extra[b])
+        v0_ref[r_low, :] = low
+        v0_ref[r_high, :] = high
+        face = jnp.where(grid.lower, low, high)
+        own = jnp.where(grid.lower, reaction_ref[r_low, :], reaction_ref[r_high, :])
+        theirs = slopes[b] + w0 * (flat0_ref[pl.ds(NP * b, NP), :] + flat[b])
+        theirs = theirs + wb * ((float(STIFF[0, 0]) + w0 * reactions[b]) * face)
+        more_face = w0 * (flat[b] + own * more) + jnp.where(nb, theirs, 0.0)
+        v1_ref[r_low, :] = part_ref[r_low, :] + pull[0] * more + jnp.where(grid.lower, more_face, 0.0)
+        v1_ref[r_high, :] = (
+            part_ref[r_high, :] + pull[last] * more + jnp.where(grid.lower, 0.0, more_face)
         )
-        more = jnp.where(nb, slopes[b] + own, 0.0)
-        low, high = rows(0, b), rows(last, b)
-        v1_ref[low, :] = v1_ref[low, :] + jnp.where(grid.lower, more, 0.0)
-        v1_ref[high, :] = v1_ref[high, :] + jnp.where(grid.lower, 0.0, more)
     grid.assemble(v1_ref)
     grid.local(v1_ref, reaction_ref, v2_ref, tmp_ref)
     weight = grid.count_weights()
@@ -497,16 +539,20 @@
 VM = pl.BlockSpec(memory_space=pltpu.VMEM)
 
 
-def call(kernel, out_shapes, in_specs, scratch=(), name=None, grant=16 * 1024 * 1024):
+def call(kernel, out_shapes, in_specs, scratch=(), name=None):
     return pl.pallas_call(
         kernel,
         out_shape=[jax.ShapeDtypeStruct(s, jnp.float32) for s in out_shapes],
         in_specs=in_specs,
         out_specs=[VM] * len(out_shapes),
         scratch_shapes=list(scratch),
-        compiler_params=pltpu.CompilerParams(vmem_limit_bytes=grant),
+        compiler_params=pltpu.CompilerParams(vmem_limit_bytes=16 * 1024 * 1024),
         name=name,
     )
+
+
+def in_hbm(*arrays):
+    return [pltpu.with_memory_space_constraint(x, pltpu.HBM) for x in arrays]
 
 
 def swap(x, wide, narrow, *partner_of):
@@ -560,24 +606,32 @@
         [pl.BlockSpec(memory_space=pltpu.HBM)] * 3,
         [pltpu.VMEM((1, per), jnp.int32), pltpu.SemaphoreType.DMA((blocks + 1,))],
         name="pack",
-        grant=None,
-    )(source_old.T, reaction_old.T, new_place.reshape(1, per))[0]
+    )(*in_hbm(source_old.T, reaction_old.T, new_place.reshape(1, per)))[0]
     full = (PTS, lanes)
-    rhs, reaction, msg_a, msg_b = call(
+    got = lax.all_gather(packed, "narrow")
+    rhs, msg_a, msg_b = call(
         functools.partial(first_kernel, per, narrow, wide),
-        [full, full, (3 * HALF, lanes), (3 * HALF, lanes)],
+        [full, (3 * HALF, lanes), (3 * HALF, lanes)],
         [VM],
+        [pltpu.VMEM((2 * PLANE, lanes), jnp.float32)],
         name="first",
-    )(lax.all_gather(packed, "narrow"))
+    )(got)
     got_a = swap(msg_a, wide, narrow, same_pair)
     got_b = swap(msg_b, wide, narrow, next_pair)
+    reaction, part, flat = call(
+        functools.partial(middle_kernel, per, narrow, wide),
+        [full, full, (PLANE, lanes)],
+        [VM] * 2,
+        [pltpu.VMEM((PLANE, lanes), jnp.float32)],
+        name="middle",
+    )(got, rhs)
     v0, v1, v2, msg_a, msg_b = call(
         functools.partial(second_kernel, wide),
         [full, full, full, (HALF + NP, lanes), (HALF + NP, lanes)],
-        [VM] * 4,
+        [VM] * 6,
         [pltpu.VMEM((PLANE, lanes), jnp.float32), pltpu.VMEM((PLANE, lanes), jnp.float32)],
         name="second",
-    )(rhs, reaction, got_a, got_b)
+    )(rhs, reaction, part, flat, got_a, got_b)
     arrived = finish(msg_a, msg_b, wide, narrow)
     own = call(
         functools.partial(own_kernel, per, wide),

time: 31.9 us -> 30.8 us (0.966)
  waiting for transfers between devices: 7.1 us -> 6.59 us
  Pallas kernels: 4.62 us -> 4.24 us
    pallas_call x1, Pallas kernels: 1.57 us -> 0.93 us  [local(): call(pack_kernel, [(blocks * per + NP, LANES)], [pl.BlockSpec(memory_spac...]
    ppermute x5, waiting for transfers between devices: 6.29 us -> 5.79 us  [swap(): return lax.ppermute(x, ('wide', 'narrow'), pairs)]
    pallas_call x1 -> x2, Pallas kernels: 0.71 us -> 1.17 us  [the longest x1 0.68 us: local(): call(functools.partial(first_kernel, per, narrow, wide), [full, (3 * HALF...]
  transfers between devices with their start and end apart: 7 -> 7, of which waited for: 5 -> 5; matrix products, arithmetic and copies ran while one was open for 0% -> 0% of each run, Pallas kernels for 1% -> 3%
where the time goes in v2:
time: 30.8 us; the launch traced here: 30.6 us
  starting transfers between devices  10.3 us (33%)
  blocking collectives  8.74 us (28%)
  waiting for transfers between devices  6.59 us (21%)
  Pallas kernels  4.24 us (14%)
  between operations  0.68 us (2%)
    ppermute x5, starting transfers between devices, swap(): return lax.ppermute(x, ('wide', 'narrow'), pairs)  10.3 us
    all_gather x1, blocking collectives, local(): got = lax.all_gather(packed, 'narrow')  8.74 us
    ppermute x5, waiting for transfers between devices, swap(): return lax.ppermute(x, ('wide', 'narrow'), pairs)  5.79 us
    pallas_call x1, Pallas kernels, local(): call(functools.partial(second_kernel, wide), [full, full, full, (HALF + N...  0.95 us
    pallas_call x1, Pallas kernels, local(): call(pack_kernel, [(blocks * per + NP, LANES)], [pl.BlockSpec(memory_spac...  0.93 us
    pallas_call x1, Pallas kernels, local(): call(functools.partial(last_kernel, wide), [(per, PTS), (per, PTS)], [VM]...  0.84 us
    ppermute x2, waiting for transfers between devices, twin(): return lax.ppermute(x, 'narrow', [(v, v ^ 1) for v in range(narrow)])  0.81 us
    pallas_call x1, Pallas kernels, local(): call(functools.partial(first_kernel, per, narrow, wide), [full, (3 * HALF...  0.68 us
  transfers between devices with their start and end apart: 7, of which 5 were waited for; matrix products, arithmetic and copies ran while one was open for 0% of the time, Pallas kernels for 3%

profile of v2, /device:TPU:0, one launch (start us, length us, event | category | flops | bytes accessed | tf_op | source)
XLA Modules:
  0.0 30.6 jit_solution(9072301177412433097)
XLA Ops:
  0.6 0.9 %pack.1 = f32[264,128]{1,0:T(8,128)S(1)} custom-call(f32[32,512]{1,0:T(8,128)} %bitcast.8, f32[32,512]{1,0:T(8,128)} %bitcast.9, s32[1,32]{1,0:T(1,128)} %bitcast.10), custom_call_target="tpu_custom_call" | custom-call | tf_op jit(solution)/shard_map/pack/pallas_call | solution.py:603
  1.6 8.7 %all-gather = f32[1056,128]{1,0:T(8,128)S(1)} all-gather(f32[264,128]{1,0:T(8,128)S(1)} %pack.1), channel_id=2, replica_groups=mesh['wide'=8,'narrow'=4] {'narrow'}, dimensions={0}, use_global_device_ids=true | all-gather | bytes 675840 | tf_op jit(solution)/shard_map/all_gather | solution.py:611
  10.3 0.7 %first.1 = (f32[512,128]{1,0:T(8,128)S(1)}, f32[96,128]{1,0:T(8,128)S(1)}, f32[96,128]{1,0:T(8,128)S(1)}) custom-call(f32[4,264,128]{2,1,0:T(8,128)S(1)} %bitcast.6), custom_call_target="tpu_custom_call" | custom-call | tf_op jit(solution)/shard_map/first/pallas_call | solution.py:612
  11.0 1.6 %collective-permute-start = (f32[96,128]{1,0:T(8,128)S(1)}, f32[96,128]{1,0:T(8,128)S(1)}, u32[]{:S(2)}, u32[]{:S(2)}) collective-permute-start(f32[96,128]{1,0:T(8,128)S(1)} %get-tuple-element.23), channel_id=1, source_target_pairs={{0,4},{1,5},{2,6},{3,7},{4,0},{5,1},{6,2},{7,3},{8,12},{9,13},{10,... | collective-permute-start | bytes 147464 | tf_op jit(solution)/shard_map/ppermute | solution.py:568
  12.6 0.1 collective-permute-start.1
  12.6 0.5 %middle.1 = (f32[512,128]{1,0:T(8,128)S(1)}, f32[512,128]{1,0:T(8,128)S(1)}, f32[64,128]{1,0:T(8,128)S(1)}) custom-call(f32[4,264,128]{2,1,0:T(8,128)S(1)} %bitcast.7, f32[512,128]{1,0:T(8,128)S(1)} %get-tuple-element.19.rhs_ref), custom_call_target="tpu_custom_call" | custom-call | tf_op jit(solution)/shard_map/middle/pallas_call | solution.py:621
  13.2 2.0 %collective-permute-done.got_a_ref = f32[96,128]{1,0:T(8,128)S(1)} collective-permute-done((f32[96,128]{1,0:T(8,128)S(1)}, f32[96,128]{1,0:T(8,128)S(1)}, u32[]{:S(2)}, u32[]{:S(2)}) %collective-permute-start) | collective-permute-done | bytes 49184 | tf_op jit(solution)/shard_map/ppermute | solution.py:568
  15.1 0.0 collective-permute-done.1.got_b_ref
  15.2 1.0 %second.1 = (f32[512,128]{1,0:T(8,128)S(1)}, f32[512,128]{1,0:T(8,128)S(1)}, f32[512,128]{1,0:T(8,128)S(1)}, f32[40,128]{1,0:T(8,128)S(1)}, f32[40,128]{1,0:T(8,128)S(1)}) custom-call(f32[512,128]{1,0:T(8,128)S(1)} %get-tuple-element.19.rhs_ref, f32[512,128]{1,0:T(8,128)S(1)} %get-tuple-element.20.reaction_ref, f32[512,128]{1,0:T(8,128)S(1)} %get-tuple-element.21.part_ref, ...), custom_call_target="tpu_custom_call" | custom-call | tf_op jit(solution)/shard_map/second/pallas_call | solution.py:628
  16.1 3.0 %collective-permute-start.2 = (f32[40,128]{1,0:T(8,128)S(1)}, f32[40,128]{1,0:T(8,128)S(1)}, u32[]{:S(2)}, u32[]{:S(2)}) collective-permute-start(f32[40,128]{1,0:T(8,128)S(1)} %get-tuple-element.32), channel_id=1, source_target_pairs={{0,4},{1,5},{2,6},{3,7},{4,0},{5,1},{6,2},{7,3},{8,12},{9,13},{10,... | collective-permute-start | bytes 61448 | tf_op jit(solution)/shard_map/ppermute | solution.py:568
  19.1 1.8 %collective-permute-done.2 = f32[40,128]{1,0:T(8,128)S(1)} collective-permute-done((f32[40,128]{1,0:T(8,128)S(1)}, f32[40,128]{1,0:T(8,128)S(1)}, u32[]{:S(2)}, u32[]{:S(2)}) %collective-permute-start.2) | collective-permute-done | bytes 20512 | tf_op jit(solution)/shard_map/ppermute | solution.py:568
  20.8 4.1 %collective-permute-start.3 = (f32[40,128]{1,0:T(8,128)S(1)}, f32[40,128]{1,0:T(8,128)S(1)}, u32[]{:S(2)}, u32[]{:S(2)}) collective-permute-start(f32[40,128]{1,0:T(8,128)S(1)} %pad_maximum_fusion), channel_id=1, source_target_pairs={{0,16},{1,3},{2,18},{3,1},{4,20},{5,9},{6,22},{7,11},{8,24},{9,5},... | collective-permute-start | bytes 61448 | tf_op jit(solution)/shard_map/ppermute | solution.py:568
  24.9 1.6 %collective-permute-start.5 = (f32[8,128]{1,0:T(8,128)S(1)}, f32[8,128]{1,0:T(8,128)S(1)}, u32[]{:S(2)}, u32[]{:S(2)}) collective-permute-start(f32[8,128]{1,0:T(8,128)S(1)} %slice_add_fusion.1), channel_id=1, source_target_pairs={{0,8},{1,25},{2,10},{3,27},{4,12},{5,29},{6,14},{7,31},{8,0},{9,17... | collective-permute-start | bytes 12296 | tf_op jit(solution)/shard_map/ppermute | solution.py:568
  26.5 0.2 collective-permute-done.3
  26.7 0.0 collective-permute-start.4
  26.7 1.8 %collective-permute-done.5 = f32[8,128]{1,0:T(8,128)S(1)} collective-permute-done((f32[8,128]{1,0:T(8,128)S(1)}, f32[8,128]{1,0:T(8,128)S(1)}, u32[]{:S(2)}, u32[]{:S(2)}) %collective-permute-start.5) | collective-permute-done | bytes 4128 | tf_op jit(solution)/shard_map/ppermute | solution.py:568
  28.6 0.0 collective-permute-start.6
  28.6 0.3 %own.1 = (f32[32,512]{1,0:T(8,128)S(1)}, f32[32,512]{1,0:T(8,128)S(1)}, f32[32,512]{1,0:T(8,128)S(1)}, f32[32,512]{1,0:T(8,128)S(1)}) custom-call(f32[512,128]{1,0:T(8,128)S(1)} %get-tuple-element.25.refs_0_, f32[512,128]{1,0:T(8,128)S(1)} %get-tuple-element.26.refs_1_, f32[512,128]{1,0:T(8,128)S(1)} %get-tuple-element.27.refs_2_), custom_call_target="tpu_custom_call" | custom-call | tf_op jit(solution)/shard_map/own/pallas_call | solution.py:636
  28.9 0.8 %collective-permute-done.6.twin_sums_ref = f32[8,128]{1,0:T(8,128)S(1)} collective-permute-done((f32[8,128]{1,0:T(8,128)S(1)}, f32[8,128]{1,0:T(8,128)S(1)}, u32[]{:S(2)}, u32[]{:S(2)}) %collective-permute-start.6) | collective-permute-done | bytes 4128 | tf_op jit(solution)/shard_map/ppermute | solution.py:580
  29.7 0.0 collective-permute-done.4.twin_b_ref
  29.7 0.8 %last.1 = (f32[32,512]{1,0:T(8,128)}, f32[32,512]{1,0:T(8,128)}) custom-call(f32[32,512]{1,0:T(8,128)S(1)} %get-tuple-element.28.v0_ref, f32[32,512]{1,0:T(8,128)S(1)} %get-tuple-element.29.v1_ref, f32[32,512]{1,0:T(8,128)S(1)} %get-tuple-element.30.v2_ref, f32[32,512]{1,0:T(8,128)S(1)} %get-tuple-element.31.scale_ref, f32[32,128]{1,0:T(8,128)S(1)} %slice.25.got_a_ref, ...), custom_call_target="tpu_custom_call" | custom-call | tf_op jit(solution)/shard_map/last/pallas_call | solution.py:643
  (6 shorter events, 0.0 us)
Async XLA Ops:
  11.0 4.2 %collective-permute-start = (f32[96,128]{1,0:T(8,128)S(1)}, f32[96,128]{1,0:T(8,128)S(1)}, u32[]{:S(2)}, u32[]{:S(2)}) collective-permute-start(f32[96,128]{1,0:T(8,128)S(1)} %get-tuple-element.23), channel_id=1, source_target_pairs={{0,4},{1,5},{2,6},{3,7},{4,0},{5,1},{6,2},{7,3},{8,12},{9,13},{10,... | collective-permute-start | bytes 147464 | tf_op jit(solution)/shard_map/ppermute | solution.py:568
  12.6 2.6 %collective-permute-start.1 = (f32[96,128]{1,0:T(8,128)S(1)}, f32[96,128]{1,0:T(8,128)S(1)}, u32[]{:S(2)}, u32[]{:S(2)}) collective-permute-start(f32[96,128]{1,0:T(8,128)S(1)} %get-tuple-element.24), channel_id=1, source_target_pairs={{0,1},{1,0},{2,3},{3,2},{4,8},{5,9},{6,10},{7,11},{8,4},{9,5},{10,... | collective-permute-start | bytes 147464 | tf_op jit(solution)/shard_map/ppermute | solution.py:568
  16.1 4.7 %collective-permute-start.2 = (f32[40,128]{1,0:T(8,128)S(1)}, f32[40,128]{1,0:T(8,128)S(1)}, u32[]{:S(2)}, u32[]{:S(2)}) collective-permute-start(f32[40,128]{1,0:T(8,128)S(1)} %get-tuple-element.32), channel_id=1, source_target_pairs={{0,4},{1,5},{2,6},{3,7},{4,0},{5,1},{6,2},{7,3},{8,12},{9,13},{10,... | collective-permute-start | bytes 61448 | tf_op jit(solution)/shard_map/ppermute | solution.py:568
  20.8 5.9 %collective-permute-start.3 = (f32[40,128]{1,0:T(8,128)S(1)}, f32[40,128]{1,0:T(8,128)S(1)}, u32[]{:S(2)}, u32[]{:S(2)}) collective-permute-start(f32[40,128]{1,0:T(8,128)S(1)} %pad_maximum_fusion), channel_id=1, source_target_pairs={{0,16},{1,3},{2,18},{3,1},{4,20},{5,9},{6,22},{7,11},{8,24},{9,5},... | collective-permute-start | bytes 61448 | tf_op jit(solution)/shard_map/ppermute | solution.py:568
  24.9 3.6 %collective-permute-start.5 = (f32[8,128]{1,0:T(8,128)S(1)}, f32[8,128]{1,0:T(8,128)S(1)}, u32[]{:S(2)}, u32[]{:S(2)}) collective-permute-start(f32[8,128]{1,0:T(8,128)S(1)} %slice_add_fusion.1), channel_id=1, source_target_pairs={{0,8},{1,25},{2,10},{3,27},{4,12},{5,29},{6,14},{7,31},{8,0},{9,17... | collective-permute-start | bytes 12296 | tf_op jit(solution)/shard_map/ppermute | solution.py:568
  26.7 3.0 %collective-permute-start.4 = (f32[32,128]{1,0:T(8,128)S(1)}, f32[32,128]{1,0:T(8,128)S(1)}, u32[]{:S(2)}, u32[]{:S(2)}) collective-permute-start(f32[32,128]{1,0:T(8,128)S(1)} %slice.27.got_b_ref), channel_id=1, source_target_pairs={{0,1},{1,0},{2,3},{3,2},{4,5},{5,4},{6,7},{7,6},{8,9},{9,8},{10,11... | collective-permute-start | bytes 49160 | tf_op jit(solution)/shard_map/ppermute | solution.py:580
  28.6 1.2 %collective-permute-start.6 = (f32[8,128]{1,0:T(8,128)S(1)}, f32[8,128]{1,0:T(8,128)S(1)}, u32[]{:S(2)}, u32[]{:S(2)}) collective-permute-start(f32[8,128]{1,0:T(8,128)S(1)} %fusion.1.sums_ref), channel_id=1, source_target_pairs={{0,1},{1,0},{2,3},{3,2},{4,5},{5,4},{6,7},{7,6},{8,9},{9,8},{10,11... | collective-permute-start | bytes 12296 | tf_op jit(solution)/shard_map/ppermute | solution.py:580

commit v3 on v2

--- a/solution.py
+++ b/solution.py
@@ -483,7 +483,6 @@
     got_b_ref,
     twin_b_ref,
     sums_ref,
-    twin_sums_ref,
     solution_ref,
     strong_ref,
     face_ref,
@@ -517,8 +516,7 @@
         0: jnp.where((spot < PLANE) & (layer == 0), face, 0.0),
         PTS // LANES - 1: jnp.where((spot >= PLANE) & (layer == BX - 1), face, 0.0),
     }
-    total = sums_ref[...] + twin_sums_ref[...]
-    g = [jnp.sum(total[k : k + 1, :], axis=1, keepdims=True) for k in range(4)]
+    g = [jnp.sum(sums_ref[k : k + 1, :], axis=1, keepdims=True) for k in range(4)]
     alpha = g[0] / g[1]
     norm = g[0] - 2.0 * alpha * g[1] + (alpha * alpha) * g[2]
     beta = norm / g[0]
@@ -581,19 +579,23 @@
 
 
 def finish(msg_a, msg_b, wide, narrow):
+    sums = msg_a[HALF:]
+    if wide == 8:
+        got_b = swap(msg_b, wide, narrow, lambda u: u ^ 4, next_pair)
+        more = swap(sums, wide, narrow, lambda u: u ^ 2, lambda u: u ^ 6)
+        twin_b = twin(got_b[:HALF], narrow)
+        even = lax.axis_index("narrow") % 2 == 0
+        part = more + jnp.where(even, sums + got_b[HALF:], 0.0)
+        got_a = swap(jnp.concatenate([msg_a[:HALF], part], axis=0), wide, narrow, same_pair)
+        cross = [
+            (u * narrow + v, (u ^ 1) * narrow + (v ^ 1)) for u in range(wide) for v in range(narrow)
+        ]
+        theirs = got_a[HALF:] + lax.ppermute(part, ("wide", "narrow"), cross)
+        total = (part + twin(part, narrow)) + theirs
+        return got_a[:HALF], got_b[:HALF], twin_b, total
     got_a = swap(msg_a, wide, narrow, same_pair)
-    if wide == 8:
-        pair = msg_a[HALF:] + got_a[HALF:]
-        got_b = swap(
-            jnp.concatenate([msg_b[:HALF], pair], axis=0), wide, narrow, lambda u: u ^ 4, next_pair
-        )
-        more = swap(pair, wide, narrow, lambda u: u ^ 2, lambda u: u ^ 6)
-        even = lax.axis_index("narrow") % 2 == 0
-        sums = more + jnp.where(even, pair + got_b[HALF:], 0.0)
-        return got_a[:HALF], got_b[:HALF], twin(got_b[:HALF], narrow), sums, twin(sums, narrow)
     got_b = swap(msg_b, wide, narrow, next_pair)[:HALF]
-    sums = lax.psum(msg_a[HALF:], "wide")
-    return got_a[:HALF], got_b, got_b, sums, jnp.zeros_like(sums)
+    return got_a[:HALF], got_b, got_b, lax.psum(sums, "wide")
 
 
 def local(wide, narrow, source_old, reaction_old, new_place):
@@ -643,7 +645,7 @@
     out = call(
         functools.partial(last_kernel, wide),
         [(per, PTS), (per, PTS)],
-        [VM] * 9,
+        [VM] * 8,
         [pltpu.VMEM((LANES, lanes), jnp.float32), pltpu.VMEM((lanes, LANES), jnp.float32)],
         name="last",
     )(*own, *arrived)

time: 30.8 us -> 29.7 us (0.964)
  waiting for transfers between devices: 6.59 us -> 5.24 us
    ppermute x2, starting transfers between devices: 0.01 us -> 1.7 us  [twin(): return lax.ppermute(x, 'narrow', [(v, v ^ 1) for v in range(narrow)])]
    ppermute x5, waiting for transfers between devices: 5.79 us -> 4.27 us  [swap(): return lax.ppermute(x, ('wide', 'narrow'), pairs)]
    ppermute x5, starting transfers between devices: 10.3 us -> 8.85 us  [swap(): return lax.ppermute(x, ('wide', 'narrow'), pairs)]
    ppermute x0 -> x1, waiting for transfers between devices: none -> 0.96 us  [finish(): theirs = got_a[HALF:] + lax.ppermute(part, ('wide', 'narrow'), cross)]
    ppermute x2, waiting for transfers between devices: 0.81 us -> 0.01 us  [twin(): return lax.ppermute(x, 'narrow', [(v, v ^ 1) for v in range(narrow)])]
  transfers between devices with their start and end apart: 7 -> 8, of which waited for: 5 -> 4; matrix products, arithmetic and copies ran while one was open for 0% -> 0% of each run, Pallas kernels for 3% -> 3%
where the time goes in v3:
time: 29.7 us; the launch traced here: 29.5 us
  starting transfers between devices  10.6 us (36%)
  blocking collectives  8.74 us (29%)
  waiting for transfers between devices  5.24 us (18%)
  Pallas kernels  4.23 us (14%)
  between operations  0.7 us (2%)
    ppermute x5, starting transfers between devices, swap(): return lax.ppermute(x, ('wide', 'narrow'), pairs)  8.85 us
    all_gather x1, blocking collectives, local(): got = lax.all_gather(packed, 'narrow')  8.74 us
    ppermute x5, waiting for transfers between devices, swap(): return lax.ppermute(x, ('wide', 'narrow'), pairs)  4.27 us
    ppermute x2, starting transfers between devices, twin(): return lax.ppermute(x, 'narrow', [(v, v ^ 1) for v in range(narrow)])  1.7 us
    ppermute x1, waiting for transfers between devices, finish(): theirs = got_a[HALF:] + lax.ppermute(part, ('wide', 'narrow'), cross)  0.96 us
    pallas_call x1, Pallas kernels, local(): call(functools.partial(second_kernel, wide), [full, full, full, (HALF + N...  0.95 us
    pallas_call x1, Pallas kernels, local(): call(pack_kernel, [(blocks * per + NP, LANES)], [pl.BlockSpec(memory_spac...  0.93 us
    pallas_call x1, Pallas kernels, local(): call(functools.partial(last_kernel, wide), [(per, PTS), (per, PTS)], [VM]...  0.84 us
  transfers between devices with their start and end apart: 8, of which 4 were waited for; matrix products, arithmetic and copies ran while one was open for 0% of the time, Pallas kernels for 3%

profile of v3, /device:TPU:0, one launch (start us, length us, event | category | flops | bytes accessed | tf_op | source)
XLA Modules:
  0.0 29.5 jit_solution(4152302693096813757)
XLA Ops:
  0.6 0.9 %pack.1 = f32[264,128]{1,0:T(8,128)S(1)} custom-call(f32[32,512]{1,0:T(8,128)} %bitcast.8, f32[32,512]{1,0:T(8,128)} %bitcast.9, s32[1,32]{1,0:T(1,128)} %bitcast.10), custom_call_target="tpu_custom_call" | custom-call | tf_op jit(solution)/shard_map/pack/pallas_call | solution.py:605
  1.6 8.7 %all-gather = f32[1056,128]{1,0:T(8,128)S(1)} all-gather(f32[264,128]{1,0:T(8,128)S(1)} %pack.1), channel_id=2, replica_groups=mesh['wide'=8,'narrow'=4] {'narrow'}, dimensions={0}, use_global_device_ids=true | all-gather | bytes 675840 | tf_op jit(solution)/shard_map/all_gather | solution.py:613
  10.3 0.7 %first.1 = (f32[512,128]{1,0:T(8,128)S(1)}, f32[96,128]{1,0:T(8,128)S(1)}, f32[96,128]{1,0:T(8,128)S(1)}) custom-call(f32[4,264,128]{2,1,0:T(8,128)S(1)} %bitcast.6), custom_call_target="tpu_custom_call" | custom-call | tf_op jit(solution)/shard_map/first/pallas_call | solution.py:614
  11.0 1.6 %collective-permute-start = (f32[96,128]{1,0:T(8,128)S(1)}, f32[96,128]{1,0:T(8,128)S(1)}, u32[]{:S(2)}, u32[]{:S(2)}) collective-permute-start(f32[96,128]{1,0:T(8,128)S(1)} %get-tuple-element.23), channel_id=1, source_target_pairs={{0,4},{1,5},{2,6},{3,7},{4,0},{5,1},{6,2},{7,3},{8,12},{9,13},{10,... | collective-permute-start | bytes 147464 | tf_op jit(solution)/shard_map/ppermute | solution.py:566
  12.6 0.1 collective-permute-start.1
  12.6 0.5 %middle.1 = (f32[512,128]{1,0:T(8,128)S(1)}, f32[512,128]{1,0:T(8,128)S(1)}, f32[64,128]{1,0:T(8,128)S(1)}) custom-call(f32[4,264,128]{2,1,0:T(8,128)S(1)} %bitcast.7, f32[512,128]{1,0:T(8,128)S(1)} %get-tuple-element.19.rhs_ref), custom_call_target="tpu_custom_call" | custom-call | tf_op jit(solution)/shard_map/middle/pallas_call | solution.py:623
  13.2 2.0 %collective-permute-done.got_a_ref = f32[96,128]{1,0:T(8,128)S(1)} collective-permute-done((f32[96,128]{1,0:T(8,128)S(1)}, f32[96,128]{1,0:T(8,128)S(1)}, u32[]{:S(2)}, u32[]{:S(2)}) %collective-permute-start) | collective-permute-done | bytes 49184 | tf_op jit(solution)/shard_map/ppermute | solution.py:566
  15.1 0.0 collective-permute-done.1.got_b_ref
  15.2 1.0 %second.1 = (f32[512,128]{1,0:T(8,128)S(1)}, f32[512,128]{1,0:T(8,128)S(1)}, f32[512,128]{1,0:T(8,128)S(1)}, f32[40,128]{1,0:T(8,128)S(1)}, f32[40,128]{1,0:T(8,128)S(1)}) custom-call(f32[512,128]{1,0:T(8,128)S(1)} %get-tuple-element.19.rhs_ref, f32[512,128]{1,0:T(8,128)S(1)} %get-tuple-element.20.reaction_ref, f32[512,128]{1,0:T(8,128)S(1)} %get-tuple-element.21.part_ref, ...), custom_call_target="tpu_custom_call" | custom-call | tf_op jit(solution)/shard_map/second/pallas_call | solution.py:630
  16.1 5.0 %collective-permute-start.3 = (f32[40,128]{1,0:T(8,128)S(1)}, f32[40,128]{1,0:T(8,128)S(1)}, u32[]{:S(2)}, u32[]{:S(2)}) collective-permute-start(f32[40,128]{1,0:T(8,128)S(1)} %get-tuple-element.33), channel_id=1, source_target_pairs={{0,16},{1,3},{2,18},{3,1},{4,20},{5,9},{6,22},{7,11},{8,24},{9,5},... | collective-permute-start | bytes 61448 | tf_op jit(solution)/shard_map/ppermute | solution.py:566
  21.2 1.6 %collective-permute-start.2 = (f32[8,128]{1,0:T(8,128)S(1)}, f32[8,128]{1,0:T(8,128)S(1)}, u32[]{:S(2)}, u32[]{:S(2)}) collective-permute-start(f32[8,128]{1,0:T(8,128)S(1)} %slice.20), channel_id=1, source_target_pairs={{0,8},{1,25},{2,10},{3,27},{4,12},{5,29},{6,14},{7,31},{8,0},{9,17... | collective-permute-start | bytes 12296 | tf_op jit(solution)/shard_map/ppermute | solution.py:566
  22.7 2.0 %collective-permute-done.2 = f32[8,128]{1,0:T(8,128)S(1)} collective-permute-done((f32[8,128]{1,0:T(8,128)S(1)}, f32[8,128]{1,0:T(8,128)S(1)}, u32[]{:S(2)}, u32[]{:S(2)}) %collective-permute-start.2) | collective-permute-done | bytes 4128 | tf_op jit(solution)/shard_map/ppermute | solution.py:566
  24.8 0.0 collective-permute-done.3
  24.8 0.6 %collective-permute-start.4 = (f32[40,128]{1,0:T(8,128)S(1)}, f32[40,128]{1,0:T(8,128)S(1)}, u32[]{:S(2)}, u32[]{:S(2)}) collective-permute-start(f32[40,128]{1,0:T(8,128)S(1)} %pad_maximum_fusion), channel_id=1, source_target_pairs={{0,4},{1,5},{2,6},{3,7},{4,0},{5,1},{6,2},{7,3},{8,12},{9,13},{10,... | collective-permute-start | bytes 61448 | tf_op jit(solution)/shard_map/ppermute | solution.py:566
  25.4 0.0 collective-permute-start.7
  25.4 1.6 %collective-permute-start.6 = (f32[8,128]{1,0:T(8,128)S(1)}, f32[8,128]{1,0:T(8,128)S(1)}, u32[]{:S(2)}, u32[]{:S(2)}) collective-permute-start(f32[8,128]{1,0:T(8,128)S(1)} %fusion.2), channel_id=1, source_target_pairs={{0,1},{1,0},{2,3},{3,2},{4,5},{5,4},{6,7},{7,6},{8,9},{9,8},{10,11... | collective-permute-start | bytes 12296 | tf_op jit(solution)/shard_map/ppermute | solution.py:578
  27.0 0.3 %own.1 = (f32[32,512]{1,0:T(8,128)S(1)}, f32[32,512]{1,0:T(8,128)S(1)}, f32[32,512]{1,0:T(8,128)S(1)}, f32[32,512]{1,0:T(8,128)S(1)}) custom-call(f32[512,128]{1,0:T(8,128)S(1)} %get-tuple-element.25.refs_0_, f32[512,128]{1,0:T(8,128)S(1)} %get-tuple-element.26.refs_1_, f32[512,128]{1,0:T(8,128)S(1)} %get-tuple-element.27.refs_2_), custom_call_target="tpu_custom_call" | custom-call | tf_op jit(solution)/shard_map/own/pallas_call | solution.py:638
  27.3 0.1 collective-permute-start.5
  27.4 1.0 %collective-permute-done.7 = f32[8,128]{1,0:T(8,128)S(1)} collective-permute-done((f32[8,128]{1,0:T(8,128)S(1)}, f32[8,128]{1,0:T(8,128)S(1)}, u32[]{:S(2)}, u32[]{:S(2)}) %collective-permute-start.7) | collective-permute-done | bytes 4128 | tf_op jit(solution)/shard_map/ppermute | solution.py:593
  28.4 0.0 collective-permute-done.6
  28.4 0.2 collective-permute-done.4
  28.6 0.0 collective-permute-done.5.twin_b_ref
  28.6 0.8 %last.1 = (f32[32,512]{1,0:T(8,128)}, f32[32,512]{1,0:T(8,128)}) custom-call(f32[32,512]{1,0:T(8,128)S(1)} %get-tuple-element.28.v0_ref, f32[32,512]{1,0:T(8,128)S(1)} %get-tuple-element.29.v1_ref, f32[32,512]{1,0:T(8,128)S(1)} %get-tuple-element.30.v2_ref, f32[32,512]{1,0:T(8,128)S(1)} %get-tuple-element.31.scale_ref, f32[32,128]{1,0:T(8,128)S(1)} %slice.26.got_a_ref, ...), custom_call_target="tpu_custom_call" | custom-call | tf_op jit(solution)/shard_map/last/pallas_call | solution.py:645
  (7 shorter events, 0.0 us)
Async XLA Ops:
  11.0 4.2 %collective-permute-start = (f32[96,128]{1,0:T(8,128)S(1)}, f32[96,128]{1,0:T(8,128)S(1)}, u32[]{:S(2)}, u32[]{:S(2)}) collective-permute-start(f32[96,128]{1,0:T(8,128)S(1)} %get-tuple-element.23), channel_id=1, source_target_pairs={{0,4},{1,5},{2,6},{3,7},{4,0},{5,1},{6,2},{7,3},{8,12},{9,13},{10,... | collective-permute-start | bytes 147464 | tf_op jit(solution)/shard_map/ppermute | solution.py:566
  12.6 2.6 %collective-permute-start.1 = (f32[96,128]{1,0:T(8,128)S(1)}, f32[96,128]{1,0:T(8,128)S(1)}, u32[]{:S(2)}, u32[]{:S(2)}) collective-permute-start(f32[96,128]{1,0:T(8,128)S(1)} %get-tuple-element.24), channel_id=1, source_target_pairs={{0,1},{1,0},{2,3},{3,2},{4,8},{5,9},{6,10},{7,11},{8,4},{9,5},{10,... | collective-permute-start | bytes 147464 | tf_op jit(solution)/shard_map/ppermute | solution.py:566
  16.1 8.7 %collective-permute-start.3 = (f32[40,128]{1,0:T(8,128)S(1)}, f32[40,128]{1,0:T(8,128)S(1)}, u32[]{:S(2)}, u32[]{:S(2)}) collective-permute-start(f32[40,128]{1,0:T(8,128)S(1)} %get-tuple-element.33), channel_id=1, source_target_pairs={{0,16},{1,3},{2,18},{3,1},{4,20},{5,9},{6,22},{7,11},{8,24},{9,5},... | collective-permute-start | bytes 61448 | tf_op jit(solution)/shard_map/ppermute | solution.py:566
  21.2 3.6 %collective-permute-start.2 = (f32[8,128]{1,0:T(8,128)S(1)}, f32[8,128]{1,0:T(8,128)S(1)}, u32[]{:S(2)}, u32[]{:S(2)}) collective-permute-start(f32[8,128]{1,0:T(8,128)S(1)} %slice.20), channel_id=1, source_target_pairs={{0,8},{1,25},{2,10},{3,27},{4,12},{5,29},{6,14},{7,31},{8,0},{9,17... | collective-permute-start | bytes 12296 | tf_op jit(solution)/shard_map/ppermute | solution.py:566
  24.8 3.8 %collective-permute-start.4 = (f32[40,128]{1,0:T(8,128)S(1)}, f32[40,128]{1,0:T(8,128)S(1)}, u32[]{:S(2)}, u32[]{:S(2)}) collective-permute-start(f32[40,128]{1,0:T(8,128)S(1)} %pad_maximum_fusion), channel_id=1, source_target_pairs={{0,4},{1,5},{2,6},{3,7},{4,0},{5,1},{6,2},{7,3},{8,12},{9,13},{10,... | collective-permute-start | bytes 61448 | tf_op jit(solution)/shard_map/ppermute | solution.py:566
  25.4 3.0 %collective-permute-start.7 = (f32[8,128]{1,0:T(8,128)S(1)}, f32[8,128]{1,0:T(8,128)S(1)}, u32[]{:S(2)}, u32[]{:S(2)}) collective-permute-start(f32[8,128]{1,0:T(8,128)S(1)} %fusion.2), channel_id=1, source_target_pairs={{0,5},{1,4},{2,7},{3,6},{4,1},{5,0},{6,3},{7,2},{8,13},{9,12},{10,... | collective-permute-start | bytes 12296 | tf_op jit(solution)/shard_map/ppermute | solution.py:593
  25.4 3.0 %collective-permute-start.6 = (f32[8,128]{1,0:T(8,128)S(1)}, f32[8,128]{1,0:T(8,128)S(1)}, u32[]{:S(2)}, u32[]{:S(2)}) collective-permute-start(f32[8,128]{1,0:T(8,128)S(1)} %fusion.2), channel_id=1, source_target_pairs={{0,1},{1,0},{2,3},{3,2},{4,5},{5,4},{6,7},{7,6},{8,9},{9,8},{10,11... | collective-permute-start | bytes 12296 | tf_op jit(solution)/shard_map/ppermute | solution.py:578
  27.3 1.3 %collective-permute-start.5 = (f32[32,128]{1,0:T(8,128)S(1)}, f32[32,128]{1,0:T(8,128)S(1)}, u32[]{:S(2)}, u32[]{:S(2)}) collective-permute-start(f32[32,128]{1,0:T(8,128)S(1)} %slice.27.got_b_ref), channel_id=1, source_target_pairs={{0,1},{1,0},{2,3},{3,2},{4,5},{5,4},{6,7},{7,6},{8,9},{9,8},{10,11... | collective-permute-start | bytes 49160 | tf_op jit(solution)/shard_map/ppermute | solution.py:578

commit v4 on v3

--- a/solution.py
+++ b/solution.py
@@ -7,6 +7,7 @@
 from jax.experimental import pallas as pl
 from jax.experimental.pallas import tpu as pltpu
 from jax.sharding import PartitionSpec as P
+
 
 NP = 8
 BX = 2
@@ -34,7 +35,7 @@
 def gll_tables(num_points):
     poly_order = num_points - 1
     abscissa = np.cos(np.pi * np.arange(num_points) / poly_order)
-    for newton_step in range(60):
+    for _ in range(60):
         legendre = legendre_values(abscissa, num_points)
         abscissa = abscissa - (abscissa * legendre[:, poly_order] - legendre[:, poly_order - 1]) / (
             num_points * legendre[:, poly_order]
@@ -145,14 +146,16 @@
         y = apply_stiff([f_ref[pl.ds(base + NP * b, NP), :] for b in range(NP)])
         return [self.w * y[b] + out_ref[pl.ds(NP * b, NP), :] for b in range(NP)]
 
-    def local(self, f_ref, reaction_ref, out_ref, tmp_ref):
+    def local(self, f_ref, massed_ref, out_ref, tmp_ref):
         for a in range(NP):
             flat = self.plane_product(f_ref, PLANE * a, tmp_ref)
             wa = float(WEIGHTS[a])
             for b in range(NP):
                 r = rows(a, b)
-                mass = (wa * float(WEIGHTS[b])) * self.w
-                out_ref[r, :] = wa * flat[b] + (reaction_ref[r, :] * mass) * f_ref[r, :]
+                value = wa * flat[b]
+                if massed_ref is not None:
+                    value = value + massed_ref[r, :] * f_ref[r, :]
+                out_ref[r, :] = value
         for b in range(NP):
             x = apply_stiff([f_ref[rows(a, b), :] for a in range(NP)])
             wb = float(WEIGHTS[b]) * self.w
@@ -223,86 +226,83 @@
     return tops + bottoms
 
 
-def pack_kernel(source_ref, reaction_ref, place_ref, out_ref, near_ref, sems):
+def pack_kernel(source_ref, reaction_ref, place_ref, early_ref, late_ref, near_ref, sems):
     per = source_ref.shape[0]
-    blocks = 2 * (PTS // LANES)
-    places = pltpu.make_async_copy(place_ref, near_ref, sems.at[blocks])
+    blocks = PTS // LANES
+    places = pltpu.make_async_copy(place_ref, near_ref, sems.at[2 * blocks])
     places.start()
     copies = []
-    for k, ref in enumerate((source_ref, reaction_ref)):
-        for q in range(PTS // LANES):
-            n = len(copies)
+    for ref, out_ref in ((reaction_ref, late_ref), (source_ref, early_ref)):
+        for q in range(blocks):
             copy = pltpu.make_async_copy(
-                ref.at[:, pl.ds(q * LANES, LANES)], out_ref.at[pl.ds(per * n, per), :], sems.at[n]
+                ref.at[:, pl.ds(q * LANES, LANES)],
+                out_ref.at[pl.ds(per * q, per), :],
+                sems.at[len(copies)],
             )
             copy.start()
             copies.append(copy)
-    v = lax.axis_index("narrow")
-    groups = LANES // per
-    row = lax.broadcasted_iota(jnp.int32, (NP, LANES), 0)
-    lane = lax.broadcasted_iota(jnp.int32, (NP, LANES), 1)
-    mine = (row == v // groups) & (lane // per == v % groups)
     places.wait()
-    places = jnp.concatenate([near_ref[...].astype(jnp.float32)] * groups, axis=1)
-    out_ref[per * blocks :, :] = jnp.where(mine, jnp.broadcast_to(places, (NP, LANES)), 0.0)
+    near = jnp.concatenate([near_ref[...].astype(jnp.float32)] * (LANES // per), axis=1)
+    early_ref[per * (blocks + 1) :, :] = jnp.broadcast_to(near, (NP, LANES))
     for copy in copies:
         copy.wait()
-
-
-class Arrived:
-    def __init__(self, per, narrow, got_ref):
-        self.per = per
-        self.got = got_ref
-        self.tiles = per * narrow // LANES
-        self.groups = LANES // per
-        self.blocks = PTS // LANES
-        lanes = per * narrow
-        spot = lax.broadcasted_iota(jnp.int32, (LANES, lanes), 1).astype(jnp.float32)
-        row = lax.broadcasted_iota(jnp.int32, (LANES, lanes), 0)
-        places = sum_of([got_ref[v, 2 * self.blocks * per :, :] for v in range(narrow)])
-        came = jnp.zeros((1, lanes), jnp.float32)
-        for t in range(self.tiles):
-            new = jnp.transpose(jnp.broadcast_to(places[t : t + 1, :], (LANES, LANES)))
-            new = jnp.concatenate([new] * self.tiles, axis=1)
-            old = (row + t * LANES).astype(jnp.float32)
-            came = came + jnp.sum(jnp.where(new == spot, old, 0.0), axis=0, keepdims=True)
-        came = jnp.broadcast_to(came.astype(jnp.int32), (NP, lanes))
-        owners = [came[:, t * LANES : (t + 1) * LANES] for t in range(self.tiles)]
-        self.source = [(owner // LANES, owner % LANES) for owner in owners]
-
-    def block(self, field, q, t):
-        rows_of = pl.ds(self.per * (self.blocks * field + q), self.per)
-        return jnp.concatenate(
-            [self.got[self.groups * t + g, rows_of, :] for g in range(self.groups)], axis=0
+    low = lax.broadcasted_iota(jnp.int32, (per, LANES), 1) < PLANE
+    early_ref[per * blocks : per * (blocks + 1), :] = jnp.where(
+        low, late_ref[:per, :], late_ref[per * (blocks - 1) :, :]
+    )
+
+
+def came_from(per, refs):
+    lanes = per * len(refs)
+    tiles, groups = lanes // LANES, LANES // per
+    at = pl.ds(per * (PTS // LANES + 1), NP)
+    group = lax.broadcasted_iota(jnp.int32, (NP, LANES), 1) // per
+    spot = lax.broadcasted_iota(jnp.int32, (LANES, lanes), 1).astype(jnp.float32)
+    row = lax.broadcasted_iota(jnp.int32, (LANES, lanes), 0)
+    came = jnp.zeros((1, lanes), jnp.float32)
+    for t in range(tiles):
+        new = refs[groups * t][at, :]
+        for g in range(1, groups):
+            new = jnp.where(group == g, refs[groups * t + g][at, :], new)
+        new = jnp.transpose(jnp.concatenate([new] * (LANES // NP), axis=0))
+        new = jnp.concatenate([new] * tiles, axis=1)
+        old = (row + t * LANES).astype(jnp.float32)
+        came = came + jnp.sum(jnp.where(new == spot, old, 0.0), axis=0, keepdims=True)
+    return jnp.broadcast_to(came.astype(jnp.int32), (NP, lanes))
+
+
+def turned(per, refs, start, came):
+    tiles, groups = per * len(refs) // LANES, LANES // per
+    old = [
+        jnp.transpose(
+            jnp.concatenate([refs[groups * t + g][pl.ds(start, per), :] for g in range(groups)], axis=0)
         )
-
-    def turned(self, old):
-        old = [jnp.transpose(x) for x in old]
-        for r in range(LANES // NP):
-            for t, (home, lane) in enumerate(self.source):
-                value = None
-                for h in range(self.tiles):
-                    pick = jnp.take_along_axis(old[h][NP * r : NP * (r + 1), :], lane, axis=1)
-                    value = pick if value is None else jnp.where(home == h, pick, value)
-                yield r, slice(t * LANES, (t + 1) * LANES), value
-
-
-def first_kernel(per, narrow, wide, got_ref, rhs_ref, msg_a_ref, msg_b_ref, ends_ref):
-    lanes = per * narrow
-    grid = Grid(lanes, wide)
-    arrived = Arrived(per, narrow, got_ref)
-    tiles = range(arrived.tiles)
-    for q in range(arrived.blocks):
-        for r, cols, value in arrived.turned([arrived.block(0, q, t) for t in tiles]):
+        for t in range(tiles)
+    ]
+    for r in range(LANES // NP):
+        for t in range(tiles):
+            cols = slice(t * LANES, (t + 1) * LANES)
+            home, lane = came[:, cols] // LANES, came[:, cols] % LANES
+            value = None
+            for h in range(tiles):
+                pick = jnp.take_along_axis(old[h][NP * r : NP * (r + 1), :], lane, axis=1)
+                value = pick if value is None else jnp.where(home == h, pick, value)
+            yield r, cols, value
+
+
+def first_kernel(per, narrow, wide, *refs):
+    got, (rhs_ref, came_ref, msg_a_ref, msg_b_ref, ends_ref) = refs[:narrow], refs[narrow:]
+    grid = Grid(per * narrow, wide)
+    blocks = PTS // LANES
+    came = came_from(per, got)
+    came_ref[...] = came
+    for q in range(blocks):
+        for r, cols, value in turned(per, got, per * q, came):
             at = q * LANES + NP * r
             a, b = at // PLANE, (at % PLANE) // NP
             mass = float(WEIGHTS[a]) * float(WEIGHTS[b])
             rhs_ref[pl.ds(at, NP), cols] = value * (mass * grid.w[:, cols])
-    low = lax.broadcasted_iota(jnp.int32, (LANES, LANES), 1) < PLANE
-    ends = [
-        jnp.where(low, arrived.block(1, 0, t), arrived.block(1, arrived.blocks - 1, t)) for t in tiles
-    ]
-    for r, cols, value in arrived.turned(ends):
+    for r, cols, value in turned(per, got, per * blocks, came):
         ends_ref[pl.ds(NP * r, NP), cols] = value
     grid.assemble(rhs_ref)
 
@@ -338,14 +338,21 @@
     )
 
 
-def middle_kernel(per, narrow, wide, got_ref, rhs_ref, reaction_ref, part_ref, flat_ref, tmp_ref):
+def reaction_kernel(per, narrow, wide, *refs):
+    got, (came_ref, massed_ref) = refs[:narrow], refs[narrow:]
     grid = Grid(per * narrow, wide)
-    arrived = Arrived(per, narrow, got_ref)
-    for q in range(arrived.blocks):
-        blocks = [arrived.block(1, q, t) for t in range(arrived.tiles)]
-        for r, cols, value in arrived.turned(blocks):
-            reaction_ref[pl.ds(q * LANES + NP * r, NP), cols] = value
-    grid.local(rhs_ref, reaction_ref, part_ref, tmp_ref)
+    came = came_ref[...]
+    for q in range(PTS // LANES):
+        for r, cols, value in turned(per, got, per * q, came):
+            at = q * LANES + NP * r
+            a, b = at // PLANE, (at % PLANE) // NP
+            mass = float(WEIGHTS[a]) * float(WEIGHTS[b])
+            massed_ref[pl.ds(at, NP), cols] = value * (mass * grid.w[:, cols])
+
+
+def middle_kernel(wide, rhs_ref, part_ref, flat_ref, tmp_ref):
+    grid = Grid(rhs_ref.shape[1], wide)
+    grid.local(rhs_ref, None, part_ref, tmp_ref)
     for b in range(NP):
         low, high = rhs_ref[rows(0, b), :], rhs_ref[rows(NP - 1, b), :]
         flat_ref[pl.ds(NP * b, NP), :] = jnp.where(grid.lower, low, high)
@@ -357,7 +364,7 @@
 def second_kernel(
     wide,
     rhs_ref,
-    reaction_ref,
+    massed_ref,
     part_ref,
     flat0_ref,
     got_a_ref,
@@ -397,24 +404,24 @@
         more = wb * extra[b]
         for a in range(1, last):
             r = rows(a, b)
-            v0_ref[r, :] = rhs_ref[r, :]
-            v1_ref[r, :] = part_ref[r, :] + pull[a] * more
+            value = rhs_ref[r, :]
+            v0_ref[r, :] = value
+            v1_ref[r, :] = part_ref[r, :] + pull[a] * more + massed_ref[r, :] * value
         r_low, r_high = rows(0, b), rows(last, b)
         low = rhs_ref[r_low, :] + jnp.where(grid.lower, extra[b], 0.0)
         high = rhs_ref[r_high, :] + jnp.where(grid.lower, 0.0, extra[b])
         v0_ref[r_low, :] = low
         v0_ref[r_high, :] = high
         face = jnp.where(grid.lower, low, high)
-        own = jnp.where(grid.lower, reaction_ref[r_low, :], reaction_ref[r_high, :])
         theirs = slopes[b] + w0 * (flat0_ref[pl.ds(NP * b, NP), :] + flat[b])
         theirs = theirs + wb * ((float(STIFF[0, 0]) + w0 * reactions[b]) * face)
-        more_face = w0 * (flat[b] + own * more) + jnp.where(nb, theirs, 0.0)
-        v1_ref[r_low, :] = part_ref[r_low, :] + pull[0] * more + jnp.where(grid.lower, more_face, 0.0)
-        v1_ref[r_high, :] = (
-            part_ref[r_high, :] + pull[last] * more + jnp.where(grid.lower, 0.0, more_face)
-        )
+        end = w0 * flat[b] + jnp.where(nb, theirs, 0.0)
+        v1_low = part_ref[r_low, :] + pull[0] * more + massed_ref[r_low, :] * low
+        v1_high = part_ref[r_high, :] + pull[last] * more + massed_ref[r_high, :] * high
+        v1_ref[r_low, :] = v1_low + jnp.where(grid.lower, end, 0.0)
+        v1_ref[r_high, :] = v1_high + jnp.where(grid.lower, 0.0, end)
     grid.assemble(v1_ref)
-    grid.local(v1_ref, reaction_ref, v2_ref, tmp_ref)
+    grid.local(v1_ref, massed_ref, v2_ref, tmp_ref)
     weight = grid.count_weights()
     parts = [[], [], [], []]
     for a in range(NP):
@@ -537,15 +544,17 @@
 VM = pl.BlockSpec(memory_space=pltpu.VMEM)
 
 
-def call(kernel, out_shapes, in_specs, scratch=(), name=None):
+def call(kernel, out_shapes, in_specs, scratch=()):
     return pl.pallas_call(
         kernel,
-        out_shape=[jax.ShapeDtypeStruct(s, jnp.float32) for s in out_shapes],
+        out_shape=[
+            jax.ShapeDtypeStruct(*(s if isinstance(s[0], tuple) else (s, jnp.float32)))
+            for s in out_shapes
+        ],
         in_specs=in_specs,
         out_specs=[VM] * len(out_shapes),
         scratch_shapes=list(scratch),
         compiler_params=pltpu.CompilerParams(vmem_limit_bytes=16 * 1024 * 1024),
-        name=name,
     )
 
 
@@ -572,6 +581,18 @@
 
 def next_pair(u):
     return u + 1 if u % 2 else u - 1
+
+
+def far_copy(x, narrow):
+    if narrow != 4:
+        return list(lax.all_gather(x, "narrow"))
+    return [x, lax.ppermute(x, "narrow", [(v, v ^ 2) for v in range(narrow)])]
+
+
+def near_copies(blocks, narrow):
+    if narrow != 4:
+        return blocks
+    return blocks + [twin(x, narrow) for x in blocks]
 
 
 def twin(x, narrow):
@@ -601,53 +622,53 @@
 def local(wide, narrow, source_old, reaction_old, new_place):
     per = source_old.shape[1]
     lanes = per * narrow
-    blocks = 2 * (PTS // LANES)
-    packed = call(
+    blocks = PTS // LANES
+    early, late = call(
         pack_kernel,
-        [(blocks * per + NP, LANES)],
+        [(per * (blocks + 1) + NP, LANES), (per * blocks, LANES)],
         [pl.BlockSpec(memory_space=pltpu.HBM)] * 3,
-        [pltpu.VMEM((1, per), jnp.int32), pltpu.SemaphoreType.DMA((blocks + 1,))],
-        name="pack",
-    )(*in_hbm(source_old.T, reaction_old.T, new_place.reshape(1, per)))[0]
+        [pltpu.VMEM((1, per), jnp.int32), pltpu.SemaphoreType.DMA((2 * blocks + 1,))],
+    )(*in_hbm(source_old.T, reaction_old.T, new_place.reshape(1, per)))
     full = (PTS, lanes)
-    got = lax.all_gather(packed, "narrow")
-    rhs, msg_a, msg_b = call(
+    late = far_copy(late, narrow)
+    early = near_copies(far_copy(early, narrow), narrow)
+    rhs, came, msg_a, msg_b = call(
         functools.partial(first_kernel, per, narrow, wide),
-        [full, (3 * HALF, lanes), (3 * HALF, lanes)],
-        [VM],
+        [full, ((NP, lanes), jnp.int32), (3 * HALF, lanes), (3 * HALF, lanes)],
+        [VM] * narrow,
         [pltpu.VMEM((2 * PLANE, lanes), jnp.float32)],
-        name="first",
-    )(got)
+    )(*early)
     got_a = swap(msg_a, wide, narrow, same_pair)
     got_b = swap(msg_b, wide, narrow, next_pair)
-    reaction, part, flat = call(
-        functools.partial(middle_kernel, per, narrow, wide),
-        [full, full, (PLANE, lanes)],
-        [VM] * 2,
+    part, flat = call(
+        functools.partial(middle_kernel, wide),
+        [full, (PLANE, lanes)],
+        [VM],
         [pltpu.VMEM((PLANE, lanes), jnp.float32)],
-        name="middle",
-    )(got, rhs)
+    )(rhs)
+    late, came = lax.optimization_barrier((late, came))
+    late = near_copies(late, narrow)
+    massed = call(
+        functools.partial(reaction_kernel, per, narrow, wide), [full], [VM] * (narrow + 1)
+    )(*late, came)[0]
     v0, v1, v2, msg_a, msg_b = call(
         functools.partial(second_kernel, wide),
         [full, full, full, (HALF + NP, lanes), (HALF + NP, lanes)],
         [VM] * 6,
         [pltpu.VMEM((PLANE, lanes), jnp.float32), pltpu.VMEM((PLANE, lanes), jnp.float32)],
-        name="second",
-    )(rhs, reaction, part, flat, got_a, got_b)
+    )(rhs, massed, part, flat, got_a, got_b)
     arrived = finish(msg_a, msg_b, wide, narrow)
     own = call(
         functools.partial(own_kernel, per, wide),
         [(per, PTS)] * 4,
         [VM] * 3,
         [pltpu.VMEM((4, lanes, LANES), jnp.float32)],
-        name="own",
     )(v0, v1, v2)
     out = call(
         functools.partial(last_kernel, wide),
         [(per, PTS), (per, PTS)],
         [VM] * 8,
         [pltpu.VMEM((LANES, lanes), jnp.float32), pltpu.VMEM((lanes, LANES), jnp.float32)],
-        name="last",
     )(*own, *arrived)
     return tuple(x.T for x in out)
 

time: 29.7 us -> 31.2 us (1.051)
  blocking collectives: 8.74 us -> 0 us
  starting transfers between devices: 10.6 us -> 16.4 us
  waiting for transfers between devices: 5.24 us -> 9.48 us
    all_gather x1 -> x0, blocking collectives: 8.74 us -> none  [local(): got = lax.all_gather(packed, 'narrow')]
    ppermute x0 -> x2, starting transfers between devices: none -> 4.99 us  [far_copy(): return [x, lax.ppermute(x, 'narrow', [(v, v ^ 2) for v in range(narrow)])]]
    ppermute x0 -> x2, waiting for transfers between devices: none -> 4.59 us  [far_copy(): return [x, lax.ppermute(x, 'narrow', [(v, v ^ 2) for v in range(narrow)])]]
    ppermute x1, starting transfers between devices: 0.01 us -> 1.63 us  [finish(): theirs = got_a[HALF:] + lax.ppermute(part, ('wide', 'narrow'), cross)]
    ppermute x2 -> x6, starting transfers between devices: 1.7 us -> 0.59 us  [twin(): return lax.ppermute(x, 'narrow', [(v, v ^ 1) for v in range(narrow)])]
    ppermute x5, starting transfers between devices: 8.85 us -> 9.22 us  [swap(): return lax.ppermute(x, ('wide', 'narrow'), pairs)]
    ppermute x5, waiting for transfers between devices: 4.27 us -> 3.92 us  [swap(): return lax.ppermute(x, ('wide', 'narrow'), pairs)]
    pallas_call x3 -> x4, Pallas kernels: 2.11 us -> 2.26 us  [the longest x1 0.94 us: local(): call(pack_kernel, [(per * (blocks + 1) + NP, LANES), (per * blocks, LANES...]
  transfers between devices with their start and end apart: 8 -> 14, of which waited for: 4 -> 6; matrix products, arithmetic and copies ran while one was open for 0% -> 0% of each run, Pallas kernels for 3% -> 5%
where the time goes in v4:
time: 31.2 us; the launch traced here: 31.1 us
  starting transfers between devices  16.4 us (53%)
  waiting for transfers between devices  9.48 us (30%)
  Pallas kernels  4.38 us (14%)
  between operations  0.73 us (2%)
    ppermute x5, starting transfers between devices, swap(): return lax.ppermute(x, ('wide', 'narrow'), pairs)  9.22 us
    ppermute x2, starting transfers between devices, far_copy(): return [x, lax.ppermute(x, 'narrow', [(v, v ^ 2) for v in range(narrow)])]  4.99 us
    ppermute x2, waiting for transfers between devices, far_copy(): return [x, lax.ppermute(x, 'narrow', [(v, v ^ 2) for v in range(narrow)])]  4.59 us
    ppermute x5, waiting for transfers between devices, swap(): return lax.ppermute(x, ('wide', 'narrow'), pairs)  3.92 us
    ppermute x1, starting transfers between devices, finish(): theirs = got_a[HALF:] + lax.ppermute(part, ('wide', 'narrow'), cross)  1.63 us
    pallas_call x1, Pallas kernels, local(): call(functools.partial(second_kernel, wide), [full, full, full, (HALF + N...  0.96 us
    ppermute x1, waiting for transfers between devices, finish(): theirs = got_a[HALF:] + lax.ppermute(part, ('wide', 'narrow'), cross)  0.96 us
    pallas_call x1, Pallas kernels, local(): call(pack_kernel, [(per * (blocks + 1) + NP, LANES), (per * blocks, LANES...  0.94 us
  transfers between devices with their start and end apart: 14, of which 6 were waited for; matrix products, arithmetic and copies ran while one was open for 0% of the time, Pallas kernels for 5%

profile of v4, /device:TPU:0, one launch (start us, length us, event | category | flops | bytes accessed | tf_op | source)
XLA Modules:
  0.0 31.1 jit_solution(2293652964665601465)
XLA Ops:
  0.6 0.9 %shard_map.50 = (f32[168,128]{1,0:T(8,128)S(1)}, f32[128,128]{1,0:T(8,128)S(1)}) custom-call(f32[32,512]{1,0:T(8,128)} %bitcast.5, f32[32,512]{1,0:T(8,128)} %bitcast.6, s32[1,32]{1,0:T(1,128)} %bitcast.7), custom_call_target="tpu_custom_call" | custom-call | tf_op jit(solution)/shard_map/pallas_call | solution.py:626
  1.6 3.0 %collective-permute-start = (f32[168,128]{1,0:T(8,128)S(1)}, f32[168,128]{1,0:T(8,128)S(1)}, u32[]{:S(2)}, u32[]{:S(2)}) collective-permute-start(f32[168,128]{1,0:T(8,128)S(1)} %get-tuple-element.24.refs_0_), channel_id=1, source_target_pairs={{0,2},{1,3},{2,0},{3,1},{4,6},{5,7},{6,4},{7,5},{8,10},{9,11},{10,... | collective-permute-start | bytes 258056 | tf_op jit(solution)/shard_map/ppermute | solution.py:589
  4.6 0.0 collective-permute-start.1
  4.6 2.5 %collective-permute-done.refs_1_ = f32[168,128]{1,0:T(8,128)S(1)} collective-permute-done((f32[168,128]{1,0:T(8,128)S(1)}, f32[168,128]{1,0:T(8,128)S(1)}, u32[]{:S(2)}, u32[]{:S(2)}) %collective-permute-start) | collective-permute-done | bytes 86048 | tf_op jit(solution)/shard_map/ppermute | solution.py:589
  7.1 0.0 collective-permute-start.2
  7.1 2.0 %collective-permute-start.3 = (f32[128,128]{1,0:T(8,128)S(1)}, f32[128,128]{1,0:T(8,128)S(1)}, u32[]{:S(2)}, u32[]{:S(2)}) collective-permute-start(f32[128,128]{1,0:T(8,128)S(1)} %get-tuple-element.28.refs_0_), channel_id=1, source_target_pairs={{0,2},{1,3},{2,0},{3,1},{4,6},{5,7},{6,4},{7,5},{8,10},{9,11},{10,... | collective-permute-start | bytes 196616 | tf_op jit(solution)/shard_map/ppermute | solution.py:589
  9.1 0.0 collective-permute-done.1.refs_2_
  9.1 0.0 collective-permute-done.2.refs_3_
  9.1 0.7 %shard_map.51 = (f32[512,128]{1,0:T(8,128)S(1)}, s32[8,128]{1,0:T(8,128)S(1)}, f32[96,128]{1,0:T(8,128)S(1)}, f32[96,128]{1,0:T(8,128)S(1)}) custom-call(f32[168,128]{1,0:T(8,128)S(1)} %get-tuple-element.24.refs_0_, f32[168,128]{1,0:T(8,128)S(1)} %collective-permute-done.refs_1_, f32[168,128]{1,0:T(8,128)S(1)} %collective-permute-done.1.refs_2_, ...), custom_call_target="tpu_custom_call" | custom-call | tf_op jit(solution)/shard_map/pallas_call | solution.py:635
  9.8 2.1 %collective-permute-done.3.refs_1_ = f32[128,128]{1,0:T(8,128)S(1)} collective-permute-done((f32[128,128]{1,0:T(8,128)S(1)}, f32[128,128]{1,0:T(8,128)S(1)}, u32[]{:S(2)}, u32[]{:S(2)}) %collective-permute-start.3) | collective-permute-done | bytes 65568 | tf_op jit(solution)/shard_map/ppermute | solution.py:589
  11.9 0.0 collective-permute-start.4
  11.9 0.5 %collective-permute-start.5 = (f32[128,128]{1,0:T(8,128)S(1)}, f32[128,128]{1,0:T(8,128)S(1)}, u32[]{:S(2)}, u32[]{:S(2)}) collective-permute-start(f32[128,128]{1,0:T(8,128)S(1)} %collective-permute-done.3.refs_1_), channel_id=1, source_target_pairs={{0,1},{1,0},{2,3},{3,2},{4,5},{5,4},{6,7},{7,6},{8,9},{9,8},{10,11... | collective-permute-start | bytes 196616 | tf_op jit(solution)/shard_map/ppermute | solution.py:599
  12.4 1.8 %collective-permute-start.6 = (f32[96,128]{1,0:T(8,128)S(1)}, f32[96,128]{1,0:T(8,128)S(1)}, u32[]{:S(2)}, u32[]{:S(2)}) collective-permute-start(f32[96,128]{1,0:T(8,128)S(1)} %get-tuple-element.33), channel_id=1, source_target_pairs={{0,4},{1,5},{2,6},{3,7},{4,0},{5,1},{6,2},{7,3},{8,12},{9,13},{10,... | collective-permute-start | bytes 147464 | tf_op jit(solution)/shard_map/ppermute | solution.py:575
  14.1 0.0 collective-permute-start.7
  14.1 0.4 %shard_map.53 = (f32[512,128]{1,0:T(8,128)S(1)}, f32[64,128]{1,0:T(8,128)S(1)}) custom-call(f32[512,128]{1,0:T(8,128)S(1)} %get-tuple-element.25.rhs_ref), custom_call_target="tpu_custom_call" | custom-call | tf_op jit(solution)/shard_map/pallas_call | solution.py:643
  14.5 0.0 collective-permute-done.4.refs_2_
  14.5 0.0 collective-permute-done.5.refs_3_
  14.5 0.3 shard_map.52.massed_ref
  14.8 1.6 %collective-permute-done.6.got_a_ref = f32[96,128]{1,0:T(8,128)S(1)} collective-permute-done((f32[96,128]{1,0:T(8,128)S(1)}, f32[96,128]{1,0:T(8,128)S(1)}, u32[]{:S(2)}, u32[]{:S(2)}) %collective-permute-start.6) | collective-permute-done | bytes 49184 | tf_op jit(solution)/shard_map/ppermute | solution.py:575
  16.5 0.0 collective-permute-done.7.got_b_ref
  16.5 1.0 %shard_map.54 = (f32[512,128]{1,0:T(8,128)S(1)}, f32[512,128]{1,0:T(8,128)S(1)}, f32[512,128]{1,0:T(8,128)S(1)}, f32[40,128]{1,0:T(8,128)S(1)}, f32[40,128]{1,0:T(8,128)S(1)}) custom-call(f32[512,128]{1,0:T(8,128)S(1)} %get-tuple-element.25.rhs_ref, f32[512,128]{1,0:T(8,128)S(1)} %shard_map.52.massed_ref, f32[512,128]{1,0:T(8,128)S(1)} %get-tuple-element.31.part_ref, ...), custom_call_target="tpu_custom_call" | custom-call | tf_op jit(solution)/shard_map/pallas_call | solution.py:654
  17.4 5.3 %collective-permute-start.9 = (f32[40,128]{1,0:T(8,128)S(1)}, f32[40,128]{1,0:T(8,128)S(1)}, u32[]{:S(2)}, u32[]{:S(2)}) collective-permute-start(f32[40,128]{1,0:T(8,128)S(1)} %get-tuple-element.43), channel_id=1, source_target_pairs={{0,16},{1,3},{2,18},{3,1},{4,20},{5,9},{6,22},{7,11},{8,24},{9,5},... | collective-permute-start | bytes 61448 | tf_op jit(solution)/shard_map/ppermute | solution.py:575
  22.7 1.6 %collective-permute-start.8 = (f32[8,128]{1,0:T(8,128)S(1)}, f32[8,128]{1,0:T(8,128)S(1)}, u32[]{:S(2)}, u32[]{:S(2)}) collective-permute-start(f32[8,128]{1,0:T(8,128)S(1)} %slice.20), channel_id=1, source_target_pairs={{0,8},{1,25},{2,10},{3,27},{4,12},{5,29},{6,14},{7,31},{8,0},{9,17... | collective-permute-start | bytes 12296 | tf_op jit(solution)/shard_map/ppermute | solution.py:575
  24.3 2.0 %collective-permute-done.8 = f32[8,128]{1,0:T(8,128)S(1)} collective-permute-done((f32[8,128]{1,0:T(8,128)S(1)}, f32[8,128]{1,0:T(8,128)S(1)}, u32[]{:S(2)}, u32[]{:S(2)}) %collective-permute-start.8) | collective-permute-done | bytes 4128 | tf_op jit(solution)/shard_map/ppermute | solution.py:575
  26.3 0.0 collective-permute-done.9
  26.4 0.6 %collective-permute-start.10 = (f32[40,128]{1,0:T(8,128)S(1)}, f32[40,128]{1,0:T(8,128)S(1)}, u32[]{:S(2)}, u32[]{:S(2)}) collective-permute-start(f32[40,128]{1,0:T(8,128)S(1)} %pad_maximum_fusion), channel_id=1, source_target_pairs={{0,4},{1,5},{2,6},{3,7},{4,0},{5,1},{6,2},{7,3},{8,12},{9,13},{10,... | collective-permute-start | bytes 61448 | tf_op jit(solution)/shard_map/ppermute | solution.py:575
  26.9 0.0 collective-permute-start.12
  26.9 1.6 %collective-permute-start.13 = (f32[8,128]{1,0:T(8,128)S(1)}, f32[8,128]{1,0:T(8,128)S(1)}, u32[]{:S(2)}, u32[]{:S(2)}) collective-permute-start(f32[8,128]{1,0:T(8,128)S(1)} %fusion.2), channel_id=1, source_target_pairs={{0,5},{1,4},{2,7},{3,6},{4,1},{5,0},{6,3},{7,2},{8,13},{9,12},{10,... | collective-permute-start | bytes 12296 | tf_op jit(solution)/shard_map/ppermute | solution.py:614
  28.6 0.3 %shard_map.55 = (f32[32,512]{1,0:T(8,128)S(1)}, f32[32,512]{1,0:T(8,128)S(1)}, f32[32,512]{1,0:T(8,128)S(1)}, f32[32,512]{1,0:T(8,128)S(1)}) custom-call(f32[512,128]{1,0:T(8,128)S(1)} %get-tuple-element.35.refs_0_, f32[512,128]{1,0:T(8,128)S(1)} %get-tuple-element.36.refs_1_, f32[512,128]{1,0:T(8,128)S(1)} %get-tuple-element.37.refs_2_), custom_call_target="tpu_custom_call" | custom-call | tf_op jit(solution)/shard_map/pallas_call | solution.py:661
  28.9 0.1 collective-permute-start.11
  29.0 0.0 collective-permute-done.12
  29.0 1.0 %collective-permute-done.13 = f32[8,128]{1,0:T(8,128)S(1)} collective-permute-done((f32[8,128]{1,0:T(8,128)S(1)}, f32[8,128]{1,0:T(8,128)S(1)}, u32[]{:S(2)}, u32[]{:S(2)}) %collective-permute-start.13) | collective-permute-done | bytes 4128 | tf_op jit(solution)/shard_map/ppermute | solution.py:614
  30.0 0.2 collective-permute-done.10
  30.2 0.0 collective-permute-done.11.twin_b_ref
  30.2 0.8 %shard_map.56 = (f32[32,512]{1,0:T(8,128)}, f32[32,512]{1,0:T(8,128)}) custom-call(f32[32,512]{1,0:T(8,128)S(1)} %get-tuple-element.38.v0_ref, f32[32,512]{1,0:T(8,128)S(1)} %get-tuple-element.39.v1_ref, f32[32,512]{1,0:T(8,128)S(1)} %get-tuple-element.40.v2_ref, f32[32,512]{1,0:T(8,128)S(1)} %get-tuple-element.41.scale_ref, f32[32,128]{1,0:T(8,128)S(1)} %slice.26.got_a_ref, ...), custom_call_target="tpu_custom_call" | custom-call | tf_op jit(solution)/shard_map/pallas_call | solution.py:667
  (7 shorter events, 0.0 us)
Async XLA Ops:
  1.6 5.6 %collective-permute-start = (f32[168,128]{1,0:T(8,128)S(1)}, f32[168,128]{1,0:T(8,128)S(1)}, u32[]{:S(2)}, u32[]{:S(2)}) collective-permute-start(f32[168,128]{1,0:T(8,128)S(1)} %get-tuple-element.24.refs_0_), channel_id=1, source_target_pairs={{0,2},{1,3},{2,0},{3,1},{4,6},{5,7},{6,4},{7,5},{8,10},{9,11},{10,... | collective-permute-start | bytes 258056 | tf_op jit(solution)/shard_map/ppermute | solution.py:589
  4.6 4.5 %collective-permute-start.1 = (f32[168,128]{1,0:T(8,128)S(1)}, f32[168,128]{1,0:T(8,128)S(1)}, u32[]{:S(2)}, u32[]{:S(2)}) collective-permute-start(f32[168,128]{1,0:T(8,128)S(1)} %get-tuple-element.24.refs_0_), channel_id=1, source_target_pairs={{0,1},{1,0},{2,3},{3,2},{4,5},{5,4},{6,7},{7,6},{8,9},{9,8},{10,11... | collective-permute-start | bytes 258056 | tf_op jit(solution)/shard_map/ppermute | solution.py:599
  7.1 2.0 %collective-permute-start.2 = (f32[168,128]{1,0:T(8,128)S(1)}, f32[168,128]{1,0:T(8,128)S(1)}, u32[]{:S(2)}, u32[]{:S(2)}) collective-permute-start(f32[168,128]{1,0:T(8,128)S(1)} %collective-permute-done.refs_1_), channel_id=1, source_target_pairs={{0,1},{1,0},{2,3},{3,2},{4,5},{5,4},{6,7},{7,6},{8,9},{9,8},{10,11... | collective-permute-start | bytes 258056 | tf_op jit(solution)/shard_map/ppermute | solution.py:599
  7.1 4.7 %collective-permute-start.3 = (f32[128,128]{1,0:T(8,128)S(1)}, f32[128,128]{1,0:T(8,128)S(1)}, u32[]{:S(2)}, u32[]{:S(2)}) collective-permute-start(f32[128,128]{1,0:T(8,128)S(1)} %get-tuple-element.28.refs_0_), channel_id=1, source_target_pairs={{0,2},{1,3},{2,0},{3,1},{4,6},{5,7},{6,4},{7,5},{8,10},{9,11},{10,... | collective-permute-start | bytes 196616 | tf_op jit(solution)/shard_map/ppermute | solution.py:589
  11.9 2.7 %collective-permute-start.4 = (f32[128,128]{1,0:T(8,128)S(1)}, f32[128,128]{1,0:T(8,128)S(1)}, u32[]{:S(2)}, u32[]{:S(2)}) collective-permute-start(f32[128,128]{1,0:T(8,128)S(1)} %get-tuple-element.28.refs_0_), channel_id=1, source_target_pairs={{0,1},{1,0},{2,3},{3,2},{4,5},{5,4},{6,7},{7,6},{8,9},{9,8},{10,11... | collective-permute-start | bytes 196616 | tf_op jit(solution)/shard_map/ppermute | solution.py:599
  11.9 2.7 %collective-permute-start.5 = (f32[128,128]{1,0:T(8,128)S(1)}, f32[128,128]{1,0:T(8,128)S(1)}, u32[]{:S(2)}, u32[]{:S(2)}) collective-permute-start(f32[128,128]{1,0:T(8,128)S(1)} %collective-permute-done.3.refs_1_), channel_id=1, source_target_pairs={{0,1},{1,0},{2,3},{3,2},{4,5},{5,4},{6,7},{7,6},{8,9},{9,8},{10,11... | collective-permute-start | bytes 196616 | tf_op jit(solution)/shard_map/ppermute | solution.py:599
  12.4 4.1 %collective-permute-start.6 = (f32[96,128]{1,0:T(8,128)S(1)}, f32[96,128]{1,0:T(8,128)S(1)}, u32[]{:S(2)}, u32[]{:S(2)}) collective-permute-start(f32[96,128]{1,0:T(8,128)S(1)} %get-tuple-element.33), channel_id=1, source_target_pairs={{0,4},{1,5},{2,6},{3,7},{4,0},{5,1},{6,2},{7,3},{8,12},{9,13},{10,... | collective-permute-start | bytes 147464 | tf_op jit(solution)/shard_map/ppermute | solution.py:575
  14.1 2.3 %collective-permute-start.7 = (f32[96,128]{1,0:T(8,128)S(1)}, f32[96,128]{1,0:T(8,128)S(1)}, u32[]{:S(2)}, u32[]{:S(2)}) collective-permute-start(f32[96,128]{1,0:T(8,128)S(1)} %get-tuple-element.34), channel_id=1, source_target_pairs={{0,1},{1,0},{2,3},{3,2},{4,8},{5,9},{6,10},{7,11},{8,4},{9,5},{10,... | collective-permute-start | bytes 147464 | tf_op jit(solution)/shard_map/ppermute | solution.py:575
  17.4 8.9 %collective-permute-start.9 = (f32[40,128]{1,0:T(8,128)S(1)}, f32[40,128]{1,0:T(8,128)S(1)}, u32[]{:S(2)}, u32[]{:S(2)}) collective-permute-start(f32[40,128]{1,0:T(8,128)S(1)} %get-tuple-element.43), channel_id=1, source_target_pairs={{0,16},{1,3},{2,18},{3,1},{4,20},{5,9},{6,22},{7,11},{8,24},{9,5},... | collective-permute-start | bytes 61448 | tf_op jit(solution)/shard_map/ppermute | solution.py:575
  22.7 3.6 %collective-permute-start.8 = (f32[8,128]{1,0:T(8,128)S(1)}, f32[8,128]{1,0:T(8,128)S(1)}, u32[]{:S(2)}, u32[]{:S(2)}) collective-permute-start(f32[8,128]{1,0:T(8,128)S(1)} %slice.20), channel_id=1, source_target_pairs={{0,8},{1,25},{2,10},{3,27},{4,12},{5,29},{6,14},{7,31},{8,0},{9,17... | collective-permute-start | bytes 12296 | tf_op jit(solution)/shard_map/ppermute | solution.py:575
  26.4 3.8 %collective-permute-start.10 = (f32[40,128]{1,0:T(8,128)S(1)}, f32[40,128]{1,0:T(8,128)S(1)}, u32[]{:S(2)}, u32[]{:S(2)}) collective-permute-start(f32[40,128]{1,0:T(8,128)S(1)} %pad_maximum_fusion), channel_id=1, source_target_pairs={{0,4},{1,5},{2,6},{3,7},{4,0},{5,1},{6,2},{7,3},{8,12},{9,13},{10,... | collective-permute-start | bytes 61448 | tf_op jit(solution)/shard_map/ppermute | solution.py:575
  26.9 2.1 %collective-permute-start.12 = (f32[8,128]{1,0:T(8,128)S(1)}, f32[8,128]{1,0:T(8,128)S(1)}, u32[]{:S(2)}, u32[]{:S(2)}) collective-permute-start(f32[8,128]{1,0:T(8,128)S(1)} %fusion.2), channel_id=1, source_target_pairs={{0,1},{1,0},{2,3},{3,2},{4,5},{5,4},{6,7},{7,6},{8,9},{9,8},{10,11... | collective-permute-start | bytes 12296 | tf_op jit(solution)/shard_map/ppermute | solution.py:599
  26.9 3.0 %collective-permute-start.13 = (f32[8,128]{1,0:T(8,128)S(1)}, f32[8,128]{1,0:T(8,128)S(1)}, u32[]{:S(2)}, u32[]{:S(2)}) collective-permute-start(f32[8,128]{1,0:T(8,128)S(1)} %fusion.2), channel_id=1, source_target_pairs={{0,5},{1,4},{2,7},{3,6},{4,1},{5,0},{6,3},{7,2},{8,13},{9,12},{10,... | collective-permute-start | bytes 12296 | tf_op jit(solution)/shard_map/ppermute | solution.py:614
  28.9 1.3 %collective-permute-start.11 = (f32[32,128]{1,0:T(8,128)S(1)}, f32[32,128]{1,0:T(8,128)S(1)}, u32[]{:S(2)}, u32[]{:S(2)}) collective-permute-start(f32[32,128]{1,0:T(8,128)S(1)} %slice.27.got_b_ref), channel_id=1, source_target_pairs={{0,1},{1,0},{2,3},{3,2},{4,5},{5,4},{6,7},{7,6},{8,9},{9,8},{10,11... | collective-permute-start | bytes 49160 | tf_op jit(solution)/shard_map/ppermute | solution.py:599

commit v5 on v4

--- a/solution.py
+++ b/solution.py
@@ -62,17 +62,26 @@
 WEIGHTS, STIFF = stiffness()
 EVEN = 0.5 * (STIFF[:4, :4] + STIFF[:4, 7:3:-1])
 ODD = 0.5 * (STIFF[:4, :4] - STIFF[:4, 7:3:-1])
+EVEN = 0.5 * (EVEN + EVEN.T)
+ODD = 0.5 * (ODD + ODD.T)
 
 
 def apply_stiff(f):
     even = [f[j] + f[7 - j] for j in range(4)]
     odd = [f[j] - f[7 - j] for j in range(4)]
+    flux = {(i, j): float(EVEN[i, j]) * (even[j] - even[i]) for i in range(4) for j in range(i + 1, 4)}
+    e = [
+        (flux[0, 1] + flux[0, 2]) + flux[0, 3],
+        (flux[1, 2] + flux[1, 3]) - flux[0, 1],
+        (flux[2, 3] - flux[0, 2]) - flux[1, 2],
+        None,
+    ]
+    e[3] = -((flux[0, 3] + flux[1, 3]) + flux[2, 3])
     out = [None] * NP
     for i in range(4):
-        e = sum_of([float(EVEN[i, j]) * even[j] for j in range(4)])
-        o = sum_of([float(ODD[i, j]) * odd[j] for j in range(4)])
-        out[i] = e + o
-        out[7 - i] = e - o
+        o = sum_of([float(ODD[min(i, j), max(i, j)]) * odd[j] for j in range(4)])
+        out[i] = e[i] + o
+        out[7 - i] = e[i] - o
     return out
 
 
@@ -139,20 +148,20 @@
             put_column(ref, PLANE * a, lo)
             put_column(ref, PLANE * a + NP - 1, hi)
 
-    def plane_product(self, f_ref, base, out_ref):
+    def plane_product(self, f_ref, base, out_ref, wa=1.0):
+        scale = wa * self.w
         z = apply_stiff([column(f_ref, base + c) for c in range(NP)])
         for c in range(NP):
-            put_column(out_ref, c, self.w * z[c])
+            put_column(out_ref, c, scale * z[c])
         y = apply_stiff([f_ref[pl.ds(base + NP * b, NP), :] for b in range(NP)])
-        return [self.w * y[b] + out_ref[pl.ds(NP * b, NP), :] for b in range(NP)]
+        return [scale * y[b] + out_ref[pl.ds(NP * b, NP), :] for b in range(NP)]
 
     def local(self, f_ref, massed_ref, out_ref, tmp_ref):
         for a in range(NP):
-            flat = self.plane_product(f_ref, PLANE * a, tmp_ref)
-            wa = float(WEIGHTS[a])
+            flat = self.plane_product(f_ref, PLANE * a, tmp_ref, float(WEIGHTS[a]))
             for b in range(NP):
                 r = rows(a, b)
-                value = wa * flat[b]
+                value = flat[b]
                 if massed_ref is not None:
                     value = value + massed_ref[r, :] * f_ref[r, :]
                 out_ref[r, :] = value
@@ -424,17 +433,19 @@
     grid.local(v1_ref, massed_ref, v2_ref, tmp_ref)
     weight = grid.count_weights()
     parts = [[], [], [], []]
+    kinds = {}
     for a in range(NP):
+        for b in range(NP):
+            kinds.setdefault((place(a), place(b)), []).append(rows(a, b))
+    for (i, j), where_in in kinds.items():
         terms = [[], [], [], []]
-        for b in range(NP):
-            r = rows(a, b)
+        for r in where_in:
             v0, v1, v2 = v0_ref[r, :], v1_ref[r, :], v2_ref[r, :]
-            wt = weight[place(a)][place(b)]
-            w1 = wt * v1
-            for t, value in zip(terms, ((wt * v0) * v0, w1 * v0, w1 * v1, v1 * v2)):
+            for t, value in zip(terms, (v0 * v0, v1 * v0, v1 * v1, v1 * v2)):
                 t.append(value)
-        for p, t in zip(parts, terms):
-            p.append(sum_of(t))
+        for k, t in enumerate(terms):
+            total = sum_of(t)
+            parts[k].append(total if k == 3 else weight[i][j] * total)
     row = grid.row
     out = jnp.zeros((NP, lanes), jnp.float32)
     for k, p in enumerate(parts):

time: 31.2 us -> 31.2 us (level)
  no operation moved by 1% of the time
where the time goes in v5:
time: 31.2 us; the launch traced here: 31 us
  starting transfers between devices  16.4 us (53%)
  waiting for transfers between devices  9.53 us (31%)
  Pallas kernels  4.3 us (14%)
  between operations  0.73 us (2%)
    ppermute x5, starting transfers between devices, swap(): return lax.ppermute(x, ('wide', 'narrow'), pairs)  9.22 us
    ppermute x2, starting transfers between devices, far_copy(): return [x, lax.ppermute(x, 'narrow', [(v, v ^ 2) for v in range(narrow)])]  4.99 us
    ppermute x2, waiting for transfers between devices, far_copy(): return [x, lax.ppermute(x, 'narrow', [(v, v ^ 2) for v in range(narrow)])]  4.59 us
    ppermute x5, waiting for transfers between devices, swap(): return lax.ppermute(x, ('wide', 'narrow'), pairs)  3.97 us
    ppermute x1, starting transfers between devices, finish(): theirs = got_a[HALF:] + lax.ppermute(part, ('wide', 'narrow'), cross)  1.63 us
    ppermute x1, waiting for transfers between devices, finish(): theirs = got_a[HALF:] + lax.ppermute(part, ('wide', 'narrow'), cross)  0.96 us
    pallas_call x1, Pallas kernels, local(): call(pack_kernel, [(per * (blocks + 1) + NP, LANES), (per * blocks, LANES...  0.94 us
    pallas_call x1, Pallas kernels, local(): call(functools.partial(second_kernel, wide), [full, full, full, (HALF + N...  0.91 us
  transfers between devices with their start and end apart: 14, of which 6 were waited for; matrix products, arithmetic and copies ran while one was open for 0% of the time, Pallas kernels for 5%

profile of v5, /device:TPU:0, one launch (start us, length us, event | category | flops | bytes accessed | tf_op | source)
XLA Modules:
  0.0 31.0 jit_solution(12251622269969205314)
XLA Ops:
  0.6 0.9 %shard_map.50 = (f32[168,128]{1,0:T(8,128)S(1)}, f32[128,128]{1,0:T(8,128)S(1)}) custom-call(f32[32,512]{1,0:T(8,128)} %bitcast.5, f32[32,512]{1,0:T(8,128)} %bitcast.6, s32[1,32]{1,0:T(1,128)} %bitcast.7), custom_call_target="tpu_custom_call" | custom-call | tf_op jit(solution)/shard_map/pallas_call | solution.py:637
  1.6 3.0 %collective-permute-start = (f32[168,128]{1,0:T(8,128)S(1)}, f32[168,128]{1,0:T(8,128)S(1)}, u32[]{:S(2)}, u32[]{:S(2)}) collective-permute-start(f32[168,128]{1,0:T(8,128)S(1)} %get-tuple-element.24.refs_0_), channel_id=1, source_target_pairs={{0,2},{1,3},{2,0},{3,1},{4,6},{5,7},{6,4},{7,5},{8,10},{9,11},{10,... | collective-permute-start | bytes 258056 | tf_op jit(solution)/shard_map/ppermute | solution.py:600
  4.6 0.0 collective-permute-start.1
  4.6 2.5 %collective-permute-done.refs_1_ = f32[168,128]{1,0:T(8,128)S(1)} collective-permute-done((f32[168,128]{1,0:T(8,128)S(1)}, f32[168,128]{1,0:T(8,128)S(1)}, u32[]{:S(2)}, u32[]{:S(2)}) %collective-permute-start) | collective-permute-done | bytes 86048 | tf_op jit(solution)/shard_map/ppermute | solution.py:600
  7.1 0.0 collective-permute-start.2
  7.1 2.0 %collective-permute-start.3 = (f32[128,128]{1,0:T(8,128)S(1)}, f32[128,128]{1,0:T(8,128)S(1)}, u32[]{:S(2)}, u32[]{:S(2)}) collective-permute-start(f32[128,128]{1,0:T(8,128)S(1)} %get-tuple-element.28.refs_0_), channel_id=1, source_target_pairs={{0,2},{1,3},{2,0},{3,1},{4,6},{5,7},{6,4},{7,5},{8,10},{9,11},{10,... | collective-permute-start | bytes 196616 | tf_op jit(solution)/shard_map/ppermute | solution.py:600
  9.1 0.0 collective-permute-done.1.refs_2_
  9.1 0.0 collective-permute-done.2.refs_3_
  9.1 0.7 %shard_map.51 = (f32[512,128]{1,0:T(8,128)S(1)}, s32[8,128]{1,0:T(8,128)S(1)}, f32[96,128]{1,0:T(8,128)S(1)}, f32[96,128]{1,0:T(8,128)S(1)}) custom-call(f32[168,128]{1,0:T(8,128)S(1)} %get-tuple-element.24.refs_0_, f32[168,128]{1,0:T(8,128)S(1)} %collective-permute-done.refs_1_, f32[168,128]{1,0:T(8,128)S(1)} %collective-permute-done.1.refs_2_, ...), custom_call_target="tpu_custom_call" | custom-call | tf_op jit(solution)/shard_map/pallas_call | solution.py:646
  9.8 2.1 %collective-permute-done.3.refs_1_ = f32[128,128]{1,0:T(8,128)S(1)} collective-permute-done((f32[128,128]{1,0:T(8,128)S(1)}, f32[128,128]{1,0:T(8,128)S(1)}, u32[]{:S(2)}, u32[]{:S(2)}) %collective-permute-start.3) | collective-permute-done | bytes 65568 | tf_op jit(solution)/shard_map/ppermute | solution.py:600
  11.9 0.0 collective-permute-start.4
  11.9 0.5 %collective-permute-start.5 = (f32[128,128]{1,0:T(8,128)S(1)}, f32[128,128]{1,0:T(8,128)S(1)}, u32[]{:S(2)}, u32[]{:S(2)}) collective-permute-start(f32[128,128]{1,0:T(8,128)S(1)} %collective-permute-done.3.refs_1_), channel_id=1, source_target_pairs={{0,1},{1,0},{2,3},{3,2},{4,5},{5,4},{6,7},{7,6},{8,9},{9,8},{10,11... | collective-permute-start | bytes 196616 | tf_op jit(solution)/shard_map/ppermute | solution.py:610
  12.4 1.8 %collective-permute-start.6 = (f32[96,128]{1,0:T(8,128)S(1)}, f32[96,128]{1,0:T(8,128)S(1)}, u32[]{:S(2)}, u32[]{:S(2)}) collective-permute-start(f32[96,128]{1,0:T(8,128)S(1)} %get-tuple-element.33), channel_id=1, source_target_pairs={{0,4},{1,5},{2,6},{3,7},{4,0},{5,1},{6,2},{7,3},{8,12},{9,13},{10,... | collective-permute-start | bytes 147464 | tf_op jit(solution)/shard_map/ppermute | solution.py:586
  14.1 0.0 collective-permute-start.7
  14.1 0.3 %shard_map.53 = (f32[512,128]{1,0:T(8,128)S(1)}, f32[64,128]{1,0:T(8,128)S(1)}) custom-call(f32[512,128]{1,0:T(8,128)S(1)} %get-tuple-element.25.rhs_ref), custom_call_target="tpu_custom_call" | custom-call | tf_op jit(solution)/shard_map/pallas_call | solution.py:654
  14.5 0.0 collective-permute-done.4.refs_2_
  14.5 0.0 collective-permute-done.5.refs_3_
  14.5 0.3 shard_map.52.massed_ref
  14.8 1.7 %collective-permute-done.6.got_a_ref = f32[96,128]{1,0:T(8,128)S(1)} collective-permute-done((f32[96,128]{1,0:T(8,128)S(1)}, f32[96,128]{1,0:T(8,128)S(1)}, u32[]{:S(2)}, u32[]{:S(2)}) %collective-permute-start.6) | collective-permute-done | bytes 49184 | tf_op jit(solution)/shard_map/ppermute | solution.py:586
  16.5 0.0 collective-permute-done.7.got_b_ref
  16.5 0.9 %shard_map.54 = (f32[512,128]{1,0:T(8,128)S(1)}, f32[512,128]{1,0:T(8,128)S(1)}, f32[512,128]{1,0:T(8,128)S(1)}, f32[40,128]{1,0:T(8,128)S(1)}, f32[40,128]{1,0:T(8,128)S(1)}) custom-call(f32[512,128]{1,0:T(8,128)S(1)} %get-tuple-element.25.rhs_ref, f32[512,128]{1,0:T(8,128)S(1)} %shard_map.52.massed_ref, f32[512,128]{1,0:T(8,128)S(1)} %get-tuple-element.31.part_ref, ...), custom_call_target="tpu_custom_call" | custom-call | tf_op jit(solution)/shard_map/pallas_call | solution.py:665
  17.4 5.3 %collective-permute-start.9 = (f32[40,128]{1,0:T(8,128)S(1)}, f32[40,128]{1,0:T(8,128)S(1)}, u32[]{:S(2)}, u32[]{:S(2)}) collective-permute-start(f32[40,128]{1,0:T(8,128)S(1)} %get-tuple-element.43), channel_id=1, source_target_pairs={{0,16},{1,3},{2,18},{3,1},{4,20},{5,9},{6,22},{7,11},{8,24},{9,5},... | collective-permute-start | bytes 61448 | tf_op jit(solution)/shard_map/ppermute | solution.py:586
  22.7 1.6 %collective-permute-start.8 = (f32[8,128]{1,0:T(8,128)S(1)}, f32[8,128]{1,0:T(8,128)S(1)}, u32[]{:S(2)}, u32[]{:S(2)}) collective-permute-start(f32[8,128]{1,0:T(8,128)S(1)} %slice.20), channel_id=1, source_target_pairs={{0,8},{1,25},{2,10},{3,27},{4,12},{5,29},{6,14},{7,31},{8,0},{9,17... | collective-permute-start | bytes 12296 | tf_op jit(solution)/shard_map/ppermute | solution.py:586
  24.3 2.0 %collective-permute-done.8 = f32[8,128]{1,0:T(8,128)S(1)} collective-permute-done((f32[8,128]{1,0:T(8,128)S(1)}, f32[8,128]{1,0:T(8,128)S(1)}, u32[]{:S(2)}, u32[]{:S(2)}) %collective-permute-start.8) | collective-permute-done | bytes 4128 | tf_op jit(solution)/shard_map/ppermute | solution.py:586
  26.3 0.0 collective-permute-done.9
  26.3 0.6 %collective-permute-start.10 = (f32[40,128]{1,0:T(8,128)S(1)}, f32[40,128]{1,0:T(8,128)S(1)}, u32[]{:S(2)}, u32[]{:S(2)}) collective-permute-start(f32[40,128]{1,0:T(8,128)S(1)} %pad_maximum_fusion), channel_id=1, source_target_pairs={{0,4},{1,5},{2,6},{3,7},{4,0},{5,1},{6,2},{7,3},{8,12},{9,13},{10,... | collective-permute-start | bytes 61448 | tf_op jit(solution)/shard_map/ppermute | solution.py:586
  26.9 0.0 collective-permute-start.12
  26.9 1.6 %collective-permute-start.13 = (f32[8,128]{1,0:T(8,128)S(1)}, f32[8,128]{1,0:T(8,128)S(1)}, u32[]{:S(2)}, u32[]{:S(2)}) collective-permute-start(f32[8,128]{1,0:T(8,128)S(1)} %fusion.2), channel_id=1, source_target_pairs={{0,5},{1,4},{2,7},{3,6},{4,1},{5,0},{6,3},{7,2},{8,13},{9,12},{10,... | collective-permute-start | bytes 12296 | tf_op jit(solution)/shard_map/ppermute | solution.py:625
  28.5 0.3 %shard_map.55 = (f32[32,512]{1,0:T(8,128)S(1)}, f32[32,512]{1,0:T(8,128)S(1)}, f32[32,512]{1,0:T(8,128)S(1)}, f32[32,512]{1,0:T(8,128)S(1)}) custom-call(f32[512,128]{1,0:T(8,128)S(1)} %get-tuple-element.35.refs_0_, f32[512,128]{1,0:T(8,128)S(1)} %get-tuple-element.36.refs_1_, f32[512,128]{1,0:T(8,128)S(1)} %get-tuple-element.37.refs_2_), custom_call_target="tpu_custom_call" | custom-call | tf_op jit(solution)/shard_map/pallas_call | solution.py:672
  28.9 0.1 collective-permute-start.11
  29.0 0.0 collective-permute-done.12
  29.0 1.0 %collective-permute-done.13 = f32[8,128]{1,0:T(8,128)S(1)} collective-permute-done((f32[8,128]{1,0:T(8,128)S(1)}, f32[8,128]{1,0:T(8,128)S(1)}, u32[]{:S(2)}, u32[]{:S(2)}) %collective-permute-start.13) | collective-permute-done | bytes 4128 | tf_op jit(solution)/shard_map/ppermute | solution.py:625
  29.9 0.2 collective-permute-done.10
  30.2 0.0 collective-permute-done.11.twin_b_ref
  30.2 0.8 %shard_map.56 = (f32[32,512]{1,0:T(8,128)}, f32[32,512]{1,0:T(8,128)}) custom-call(f32[32,512]{1,0:T(8,128)S(1)} %get-tuple-element.38.v0_ref, f32[32,512]{1,0:T(8,128)S(1)} %get-tuple-element.39.v1_ref, f32[32,512]{1,0:T(8,128)S(1)} %get-tuple-element.40.v2_ref, f32[32,512]{1,0:T(8,128)S(1)} %get-tuple-element.41.scale_ref, f32[32,128]{1,0:T(8,128)S(1)} %slice.26.got_a_ref, ...), custom_call_target="tpu_custom_call" | custom-call | tf_op jit(solution)/shard_map/pallas_call | solution.py:678
  (7 shorter events, 0.0 us)
Async XLA Ops:
  1.6 5.6 %collective-permute-start = (f32[168,128]{1,0:T(8,128)S(1)}, f32[168,128]{1,0:T(8,128)S(1)}, u32[]{:S(2)}, u32[]{:S(2)}) collective-permute-start(f32[168,128]{1,0:T(8,128)S(1)} %get-tuple-element.24.refs_0_), channel_id=1, source_target_pairs={{0,2},{1,3},{2,0},{3,1},{4,6},{5,7},{6,4},{7,5},{8,10},{9,11},{10,... | collective-permute-start | bytes 258056 | tf_op jit(solution)/shard_map/ppermute | solution.py:600
  4.6 4.5 %collective-permute-start.1 = (f32[168,128]{1,0:T(8,128)S(1)}, f32[168,128]{1,0:T(8,128)S(1)}, u32[]{:S(2)}, u32[]{:S(2)}) collective-permute-start(f32[168,128]{1,0:T(8,128)S(1)} %get-tuple-element.24.refs_0_), channel_id=1, source_target_pairs={{0,1},{1,0},{2,3},{3,2},{4,5},{5,4},{6,7},{7,6},{8,9},{9,8},{10,11... | collective-permute-start | bytes 258056 | tf_op jit(solution)/shard_map/ppermute | solution.py:610
  7.1 2.0 %collective-permute-start.2 = (f32[168,128]{1,0:T(8,128)S(1)}, f32[168,128]{1,0:T(8,128)S(1)}, u32[]{:S(2)}, u32[]{:S(2)}) collective-permute-start(f32[168,128]{1,0:T(8,128)S(1)} %collective-permute-done.refs_1_), channel_id=1, source_target_pairs={{0,1},{1,0},{2,3},{3,2},{4,5},{5,4},{6,7},{7,6},{8,9},{9,8},{10,11... | collective-permute-start | bytes 258056 | tf_op jit(solution)/shard_map/ppermute | solution.py:610
  7.1 4.7 %collective-permute-start.3 = (f32[128,128]{1,0:T(8,128)S(1)}, f32[128,128]{1,0:T(8,128)S(1)}, u32[]{:S(2)}, u32[]{:S(2)}) collective-permute-start(f32[128,128]{1,0:T(8,128)S(1)} %get-tuple-element.28.refs_0_), channel_id=1, source_target_pairs={{0,2},{1,3},{2,0},{3,1},{4,6},{5,7},{6,4},{7,5},{8,10},{9,11},{10,... | collective-permute-start | bytes 196616 | tf_op jit(solution)/shard_map/ppermute | solution.py:600
  11.9 2.6 %collective-permute-start.4 = (f32[128,128]{1,0:T(8,128)S(1)}, f32[128,128]{1,0:T(8,128)S(1)}, u32[]{:S(2)}, u32[]{:S(2)}) collective-permute-start(f32[128,128]{1,0:T(8,128)S(1)} %get-tuple-element.28.refs_0_), channel_id=1, source_target_pairs={{0,1},{1,0},{2,3},{3,2},{4,5},{5,4},{6,7},{7,6},{8,9},{9,8},{10,11... | collective-permute-start | bytes 196616 | tf_op jit(solution)/shard_map/ppermute | solution.py:610
  11.9 2.6 %collective-permute-start.5 = (f32[128,128]{1,0:T(8,128)S(1)}, f32[128,128]{1,0:T(8,128)S(1)}, u32[]{:S(2)}, u32[]{:S(2)}) collective-permute-start(f32[128,128]{1,0:T(8,128)S(1)} %collective-permute-done.3.refs_1_), channel_id=1, source_target_pairs={{0,1},{1,0},{2,3},{3,2},{4,5},{5,4},{6,7},{7,6},{8,9},{9,8},{10,11... | collective-permute-start | bytes 196616 | tf_op jit(solution)/shard_map/ppermute | solution.py:610
  12.4 4.1 %collective-permute-start.6 = (f32[96,128]{1,0:T(8,128)S(1)}, f32[96,128]{1,0:T(8,128)S(1)}, u32[]{:S(2)}, u32[]{:S(2)}) collective-permute-start(f32[96,128]{1,0:T(8,128)S(1)} %get-tuple-element.33), channel_id=1, source_target_pairs={{0,4},{1,5},{2,6},{3,7},{4,0},{5,1},{6,2},{7,3},{8,12},{9,13},{10,... | collective-permute-start | bytes 147464 | tf_op jit(solution)/shard_map/ppermute | solution.py:586
  14.1 2.3 %collective-permute-start.7 = (f32[96,128]{1,0:T(8,128)S(1)}, f32[96,128]{1,0:T(8,128)S(1)}, u32[]{:S(2)}, u32[]{:S(2)}) collective-permute-start(f32[96,128]{1,0:T(8,128)S(1)} %get-tuple-element.34), channel_id=1, source_target_pairs={{0,1},{1,0},{2,3},{3,2},{4,8},{5,9},{6,10},{7,11},{8,4},{9,5},{10,... | collective-permute-start | bytes 147464 | tf_op jit(solution)/shard_map/ppermute | solution.py:586
  17.4 8.9 %collective-permute-start.9 = (f32[40,128]{1,0:T(8,128)S(1)}, f32[40,128]{1,0:T(8,128)S(1)}, u32[]{:S(2)}, u32[]{:S(2)}) collective-permute-start(f32[40,128]{1,0:T(8,128)S(1)} %get-tuple-element.43), channel_id=1, source_target_pairs={{0,16},{1,3},{2,18},{3,1},{4,20},{5,9},{6,22},{7,11},{8,24},{9,5},... | collective-permute-start | bytes 61448 | tf_op jit(solution)/shard_map/ppermute | solution.py:586
  22.7 3.6 %collective-permute-start.8 = (f32[8,128]{1,0:T(8,128)S(1)}, f32[8,128]{1,0:T(8,128)S(1)}, u32[]{:S(2)}, u32[]{:S(2)}) collective-permute-start(f32[8,128]{1,0:T(8,128)S(1)} %slice.20), channel_id=1, source_target_pairs={{0,8},{1,25},{2,10},{3,27},{4,12},{5,29},{6,14},{7,31},{8,0},{9,17... | collective-permute-start | bytes 12296 | tf_op jit(solution)/shard_map/ppermute | solution.py:586
  26.3 3.8 %collective-permute-start.10 = (f32[40,128]{1,0:T(8,128)S(1)}, f32[40,128]{1,0:T(8,128)S(1)}, u32[]{:S(2)}, u32[]{:S(2)}) collective-permute-start(f32[40,128]{1,0:T(8,128)S(1)} %pad_maximum_fusion), channel_id=1, source_target_pairs={{0,4},{1,5},{2,6},{3,7},{4,0},{5,1},{6,2},{7,3},{8,12},{9,13},{10,... | collective-permute-start | bytes 61448 | tf_op jit(solution)/shard_map/ppermute | solution.py:586
  26.9 2.1 %collective-permute-start.12 = (f32[8,128]{1,0:T(8,128)S(1)}, f32[8,128]{1,0:T(8,128)S(1)}, u32[]{:S(2)}, u32[]{:S(2)}) collective-permute-start(f32[8,128]{1,0:T(8,128)S(1)} %fusion.2), channel_id=1, source_target_pairs={{0,1},{1,0},{2,3},{3,2},{4,5},{5,4},{6,7},{7,6},{8,9},{9,8},{10,11... | collective-permute-start | bytes 12296 | tf_op jit(solution)/shard_map/ppermute | solution.py:610
  26.9 3.0 %collective-permute-start.13 = (f32[8,128]{1,0:T(8,128)S(1)}, f32[8,128]{1,0:T(8,128)S(1)}, u32[]{:S(2)}, u32[]{:S(2)}) collective-permute-start(f32[8,128]{1,0:T(8,128)S(1)} %fusion.2), channel_id=1, source_target_pairs={{0,5},{1,4},{2,7},{3,6},{4,1},{5,0},{6,3},{7,2},{8,13},{9,12},{10,... | collective-permute-start | bytes 12296 | tf_op jit(solution)/shard_map/ppermute | solution.py:625
  28.9 1.3 %collective-permute-start.11 = (f32[32,128]{1,0:T(8,128)S(1)}, f32[32,128]{1,0:T(8,128)S(1)}, u32[]{:S(2)}, u32[]{:S(2)}) collective-permute-start(f32[32,128]{1,0:T(8,128)S(1)} %slice.27.got_b_ref), channel_id=1, source_target_pairs={{0,1},{1,0},{2,3},{3,2},{4,5},{5,4},{6,7},{7,6},{8,9},{9,8},{10,11... | collective-permute-start | bytes 49160 | tf_op jit(solution)/shard_map/ppermute | solution.py:610

commit v6 on v5

--- a/solution.py
+++ b/solution.py
@@ -300,7 +300,7 @@
 
 
 def first_kernel(per, narrow, wide, *refs):
-    got, (rhs_ref, came_ref, msg_a_ref, msg_b_ref, ends_ref) = refs[:narrow], refs[narrow:]
+    got, (rhs_ref, came_ref, msg_ref, ends_ref) = refs[:narrow], refs[narrow:]
     grid = Grid(per * narrow, wide)
     blocks = PTS // LANES
     came = came_from(per, got)
@@ -315,10 +315,11 @@
         ends_ref[pl.ds(NP * r, NP), cols] = value
     grid.assemble(rhs_ref)
 
+    even = lax.axis_index("narrow") % 2 == 0
+
     def write(part):
         def put(b, first, second):
-            msg_a_ref[pl.ds(part * HALF + NP * b, NP), :] = first
-            msg_b_ref[pl.ds(part * HALF + NP * b, NP), :] = second
+            msg_ref[pl.ds(part * HALF + NP * b, NP), :] = jnp.where(even, first, second)
 
         return put
 
@@ -376,8 +377,8 @@
     massed_ref,
     part_ref,
     flat0_ref,
-    got_a_ref,
-    got_b_ref,
+    mine_ref,
+    other_ref,
     v0_ref,
     v1_ref,
     v2_ref,
@@ -391,12 +392,16 @@
     nb = grid.has_neighbour()
     last = NP - 1
 
+    even = lax.axis_index("narrow") % 2 == 0
+
     def reader(part):
         def first(b):
-            return got_a_ref[pl.ds(part * HALF + NP * b, NP), :]
+            r = pl.ds(part * HALF + NP * b, NP)
+            return jnp.where(even, mine_ref[r, :], other_ref[r, :])
 
         def second(b):
-            return got_b_ref[pl.ds(part * HALF + NP * b, NP), :]
+            r = pl.ds(part * HALF + NP * b, NP)
+            return jnp.where(even, other_ref[r, :], mine_ref[r, :])
 
         return first, second
 
@@ -643,14 +648,14 @@
     full = (PTS, lanes)
     late = far_copy(late, narrow)
     early = near_copies(far_copy(early, narrow), narrow)
-    rhs, came, msg_a, msg_b = call(
+    rhs, came, msg = call(
         functools.partial(first_kernel, per, narrow, wide),
-        [full, ((NP, lanes), jnp.int32), (3 * HALF, lanes), (3 * HALF, lanes)],
+        [full, ((NP, lanes), jnp.int32), (3 * HALF, lanes)],
         [VM] * narrow,
         [pltpu.VMEM((2 * PLANE, lanes), jnp.float32)],
     )(*early)
-    got_a = swap(msg_a, wide, narrow, same_pair)
-    got_b = swap(msg_b, wide, narrow, next_pair)
+    mine = swap(msg, wide, narrow, same_pair, next_pair)
+    other = twin(mine, narrow)
     part, flat = call(
         functools.partial(middle_kernel, wide),
         [full, (PLANE, lanes)],
@@ -667,7 +672,7 @@
         [full, full, full, (HALF + NP, lanes), (HALF + NP, lanes)],
         [VM] * 6,
         [pltpu.VMEM((PLANE, lanes), jnp.float32), pltpu.VMEM((PLANE, lanes), jnp.float32)],
-    )(rhs, massed, part, flat, got_a, got_b)
+    )(rhs, massed, part, flat, mine, other)
     arrived = finish(msg_a, msg_b, wide, narrow)
     own = call(
         functools.partial(own_kernel, per, wide),

time: 31.2 us -> 28.6 us (0.917)
  starting transfers between devices: 16.4 us -> 14.1 us
    ppermute x2, waiting for transfers between devices: 4.59 us -> 3 us  [far_copy(): return [x, lax.ppermute(x, 'narrow', [(v, v ^ 2) for v in range(narrow)])]]
    ppermute x5 -> x4, starting transfers between devices: 9.22 us -> 7.91 us  [swap(): return lax.ppermute(x, ('wide', 'narrow'), pairs)]
    ppermute x1, starting transfers between devices: 1.63 us -> 0.62 us  [finish(): theirs = got_a[HALF:] + lax.ppermute(part, ('wide', 'narrow'), cross)]
    ppermute x1, waiting for transfers between devices: 0.96 us -> 1.87 us  [finish(): theirs = got_a[HALF:] + lax.ppermute(part, ('wide', 'narrow'), cross)]
    ppermute x6 -> x7, waiting for transfers between devices: 0.02 us -> 0.73 us  [twin(): return lax.ppermute(x, 'narrow', [(v, v ^ 1) for v in range(narrow)])]
    ppermute x5 -> x4, waiting for transfers between devices: 3.97 us -> 3.62 us  [swap(): return lax.ppermute(x, ('wide', 'narrow'), pairs)]
  transfers between devices with their start and end apart: 14 -> 14, of which waited for: 6 -> 7; matrix products, arithmetic and copies ran while one was open for 0% -> 0% of each run, Pallas kernels for 5% -> 6%
where the time goes in v6:
time: 28.6 us; the launch traced here: 28.4 us
  starting transfers between devices  14.1 us (49%)
  waiting for transfers between devices  9.22 us (32%)
  Pallas kernels  4.3 us (15%)
  between operations  0.74 us (3%)
    ppermute x4, starting transfers between devices, swap(): return lax.ppermute(x, ('wide', 'narrow'), pairs)  7.91 us
    ppermute x2, starting transfers between devices, far_copy(): return [x, lax.ppermute(x, 'narrow', [(v, v ^ 2) for v in range(narrow)])]  4.99 us
    ppermute x4, waiting for transfers between devices, swap(): return lax.ppermute(x, ('wide', 'narrow'), pairs)  3.62 us
    ppermute x2, waiting for transfers between devices, far_copy(): return [x, lax.ppermute(x, 'narrow', [(v, v ^ 2) for v in range(narrow)])]  3 us
    ppermute x1, waiting for transfers between devices, finish(): theirs = got_a[HALF:] + lax.ppermute(part, ('wide', 'narrow'), cross)  1.87 us
    pallas_call x1, Pallas kernels, local(): call(pack_kernel, [(per * (blocks + 1) + NP, LANES), (per * blocks, LANES...  0.94 us
    pallas_call x1, Pallas kernels, local(): call(functools.partial(second_kernel, wide), [full, full, full, (HALF + N...  0.91 us
    pallas_call x1, Pallas kernels, local(): call(functools.partial(last_kernel, wide), [(per, PTS), (per, PTS)], [VM]...  0.84 us
  transfers between devices with their start and end apart: 14, of which 7 were waited for; matrix products, arithmetic and copies ran while one was open for 0% of the time, Pallas kernels for 6%

profile of v6, /device:TPU:0, one launch (start us, length us, event | category | flops | bytes accessed | tf_op | source)
XLA Modules:
  0.0 28.4 jit_solution(2309871715809332570)
XLA Ops:
  0.6 0.9 %shard_map.50 = (f32[168,128]{1,0:T(8,128)S(1)}, f32[128,128]{1,0:T(8,128)S(1)}) custom-call(f32[32,512]{1,0:T(8,128)} %bitcast.5, f32[32,512]{1,0:T(8,128)} %bitcast.6, s32[1,32]{1,0:T(1,128)} %bitcast.7), custom_call_target="tpu_custom_call" | custom-call | tf_op jit(solution)/shard_map/pallas_call | solution.py:642
  1.6 3.0 %collective-permute-start = (f32[168,128]{1,0:T(8,128)S(1)}, f32[168,128]{1,0:T(8,128)S(1)}, u32[]{:S(2)}, u32[]{:S(2)}) collective-permute-start(f32[168,128]{1,0:T(8,128)S(1)} %get-tuple-element.23.refs_0_), channel_id=1, source_target_pairs={{0,2},{1,3},{2,0},{3,1},{4,6},{5,7},{6,4},{7,5},{8,10},{9,11},{10,... | collective-permute-start | bytes 258056 | tf_op jit(solution)/shard_map/ppermute | solution.py:605
  4.6 0.0 collective-permute-start.1
  4.6 2.5 %collective-permute-done.refs_1_ = f32[168,128]{1,0:T(8,128)S(1)} collective-permute-done((f32[168,128]{1,0:T(8,128)S(1)}, f32[168,128]{1,0:T(8,128)S(1)}, u32[]{:S(2)}, u32[]{:S(2)}) %collective-permute-start) | collective-permute-done | bytes 86048 | tf_op jit(solution)/shard_map/ppermute | solution.py:605
  7.1 0.0 collective-permute-start.2
  7.1 2.0 %collective-permute-start.3 = (f32[128,128]{1,0:T(8,128)S(1)}, f32[128,128]{1,0:T(8,128)S(1)}, u32[]{:S(2)}, u32[]{:S(2)}) collective-permute-start(f32[128,128]{1,0:T(8,128)S(1)} %get-tuple-element.27.refs_0_), channel_id=1, source_target_pairs={{0,2},{1,3},{2,0},{3,1},{4,6},{5,7},{6,4},{7,5},{8,10},{9,11},{10,... | collective-permute-start | bytes 196616 | tf_op jit(solution)/shard_map/ppermute | solution.py:605
  9.1 0.0 collective-permute-done.1.refs_2_
  9.1 0.0 collective-permute-done.2.refs_3_
  9.1 0.7 %shard_map.51 = (f32[512,128]{1,0:T(8,128)S(1)}, s32[8,128]{1,0:T(8,128)S(1)}, f32[96,128]{1,0:T(8,128)S(1)}) custom-call(f32[168,128]{1,0:T(8,128)S(1)} %get-tuple-element.23.refs_0_, f32[168,128]{1,0:T(8,128)S(1)} %collective-permute-done.refs_1_, f32[168,128]{1,0:T(8,128)S(1)} %collective-permute-done.1.refs_2_, f32[168,128]{1,0:T(8,128)S(1)} %collective-permute-done.2.refs_3_), custom_call_target="tpu_custom_call" | custom-call | tf_op jit(solution)/shard_map/pallas_call | solution.py:651
  9.8 1.6 %collective-permute-start.6 = (f32[96,128]{1,0:T(8,128)S(1)}, f32[96,128]{1,0:T(8,128)S(1)}, u32[]{:S(2)}, u32[]{:S(2)}) collective-permute-start(f32[96,128]{1,0:T(8,128)S(1)} %get-tuple-element.32), channel_id=1, source_target_pairs={{0,4},{1,3},{2,6},{3,1},{4,0},{5,9},{6,2},{7,11},{8,12},{9,5},{10,... | collective-permute-start | bytes 147464 | tf_op jit(solution)/shard_map/ppermute | solution.py:591
  11.4 0.5 %collective-permute-done.3.refs_1_ = f32[128,128]{1,0:T(8,128)S(1)} collective-permute-done((f32[128,128]{1,0:T(8,128)S(1)}, f32[128,128]{1,0:T(8,128)S(1)}, u32[]{:S(2)}, u32[]{:S(2)}) %collective-permute-start.3) | collective-permute-done | bytes 65568 | tf_op jit(solution)/shard_map/ppermute | solution.py:605
  11.9 0.0 collective-permute-start.4
  11.9 0.5 %collective-permute-start.5 = (f32[128,128]{1,0:T(8,128)S(1)}, f32[128,128]{1,0:T(8,128)S(1)}, u32[]{:S(2)}, u32[]{:S(2)}) collective-permute-start(f32[128,128]{1,0:T(8,128)S(1)} %collective-permute-done.3.refs_1_), channel_id=1, source_target_pairs={{0,1},{1,0},{2,3},{3,2},{4,5},{5,4},{6,7},{7,6},{8,9},{9,8},{10,11... | collective-permute-start | bytes 196616 | tf_op jit(solution)/shard_map/ppermute | solution.py:615
  12.4 1.6 %collective-permute-done.6.mine_ref = f32[96,128]{1,0:T(8,128)S(1)} collective-permute-done((f32[96,128]{1,0:T(8,128)S(1)}, f32[96,128]{1,0:T(8,128)S(1)}, u32[]{:S(2)}, u32[]{:S(2)}) %collective-permute-start.6) | collective-permute-done | bytes 49184 | tf_op jit(solution)/shard_map/ppermute | solution.py:591
  14.0 0.0 collective-permute-start.7
  14.0 0.3 %shard_map.53 = (f32[512,128]{1,0:T(8,128)S(1)}, f32[64,128]{1,0:T(8,128)S(1)}) custom-call(f32[512,128]{1,0:T(8,128)S(1)} %get-tuple-element.24.rhs_ref), custom_call_target="tpu_custom_call" | custom-call | tf_op jit(solution)/shard_map/pallas_call | solution.py:659
  14.3 0.0 collective-permute-done.4.refs_2_
  14.3 0.0 collective-permute-done.5.refs_3_
  14.3 0.3 shard_map.52.massed_ref
  14.6 0.6 %collective-permute-done.7.other_ref = f32[96,128]{1,0:T(8,128)S(1)} collective-permute-done((f32[96,128]{1,0:T(8,128)S(1)}, f32[96,128]{1,0:T(8,128)S(1)}, u32[]{:S(2)}, u32[]{:S(2)}) %collective-permute-start.7) | collective-permute-done | bytes 49184 | tf_op jit(solution)/shard_map/ppermute | solution.py:615
  15.2 0.9 %shard_map.54 = (f32[512,128]{1,0:T(8,128)S(1)}, f32[512,128]{1,0:T(8,128)S(1)}, f32[512,128]{1,0:T(8,128)S(1)}, f32[40,128]{1,0:T(8,128)S(1)}, f32[40,128]{1,0:T(8,128)S(1)}) custom-call(f32[512,128]{1,0:T(8,128)S(1)} %get-tuple-element.24.rhs_ref, f32[512,128]{1,0:T(8,128)S(1)} %shard_map.52.massed_ref, f32[512,128]{1,0:T(8,128)S(1)} %get-tuple-element.30.part_ref, ...), custom_call_target="tpu_custom_call" | custom-call | tf_op jit(solution)/shard_map/pallas_call | solution.py:670
  16.1 3.2 %collective-permute-start.9 = (f32[40,128]{1,0:T(8,128)S(1)}, f32[40,128]{1,0:T(8,128)S(1)}, u32[]{:S(2)}, u32[]{:S(2)}) collective-permute-start(f32[40,128]{1,0:T(8,128)S(1)} %get-tuple-element.41), channel_id=1, source_target_pairs={{0,16},{1,3},{2,18},{3,1},{4,20},{5,9},{6,22},{7,11},{8,24},{9,5},... | collective-permute-start | bytes 61448 | tf_op jit(solution)/shard_map/ppermute | solution.py:591
  19.3 1.6 %collective-permute-start.8 = (f32[8,128]{1,0:T(8,128)S(1)}, f32[8,128]{1,0:T(8,128)S(1)}, u32[]{:S(2)}, u32[]{:S(2)}) collective-permute-start(f32[8,128]{1,0:T(8,128)S(1)} %slice.20), channel_id=1, source_target_pairs={{0,8},{1,25},{2,10},{3,27},{4,12},{5,29},{6,14},{7,31},{8,0},{9,17... | collective-permute-start | bytes 12296 | tf_op jit(solution)/shard_map/ppermute | solution.py:591
  20.8 2.0 %collective-permute-done.8 = f32[8,128]{1,0:T(8,128)S(1)} collective-permute-done((f32[8,128]{1,0:T(8,128)S(1)}, f32[8,128]{1,0:T(8,128)S(1)}, u32[]{:S(2)}, u32[]{:S(2)}) %collective-permute-start.8) | collective-permute-done | bytes 4128 | tf_op jit(solution)/shard_map/ppermute | solution.py:591
  22.9 0.0 collective-permute-done.9
  22.9 1.6 %collective-permute-start.10 = (f32[40,128]{1,0:T(8,128)S(1)}, f32[40,128]{1,0:T(8,128)S(1)}, u32[]{:S(2)}, u32[]{:S(2)}) collective-permute-start(f32[40,128]{1,0:T(8,128)S(1)} %pad_maximum_fusion), channel_id=1, source_target_pairs={{0,4},{1,5},{2,6},{3,7},{4,0},{5,1},{6,2},{7,3},{8,12},{9,13},{10,... | collective-permute-start | bytes 61448 | tf_op jit(solution)/shard_map/ppermute | solution.py:591
  24.5 0.0 collective-permute-start.12
  24.5 0.6 %collective-permute-start.13 = (f32[8,128]{1,0:T(8,128)S(1)}, f32[8,128]{1,0:T(8,128)S(1)}, u32[]{:S(2)}, u32[]{:S(2)}) collective-permute-start(f32[8,128]{1,0:T(8,128)S(1)} %fusion.2), channel_id=1, source_target_pairs={{0,5},{1,4},{2,7},{3,6},{4,1},{5,0},{6,3},{7,2},{8,13},{9,12},{10,... | collective-permute-start | bytes 12296 | tf_op jit(solution)/shard_map/ppermute | solution.py:630
  25.1 0.3 %shard_map.55 = (f32[32,512]{1,0:T(8,128)S(1)}, f32[32,512]{1,0:T(8,128)S(1)}, f32[32,512]{1,0:T(8,128)S(1)}, f32[32,512]{1,0:T(8,128)S(1)}) custom-call(f32[512,128]{1,0:T(8,128)S(1)} %get-tuple-element.33.refs_0_, f32[512,128]{1,0:T(8,128)S(1)} %get-tuple-element.34.refs_1_, f32[512,128]{1,0:T(8,128)S(1)} %get-tuple-element.35.refs_2_), custom_call_target="tpu_custom_call" | custom-call | tf_op jit(solution)/shard_map/pallas_call | solution.py:677
  25.5 0.1 collective-permute-start.11
  25.5 0.1 collective-permute-done.12
  25.6 1.9 %collective-permute-done.13 = f32[8,128]{1,0:T(8,128)S(1)} collective-permute-done((f32[8,128]{1,0:T(8,128)S(1)}, f32[8,128]{1,0:T(8,128)S(1)}, u32[]{:S(2)}, u32[]{:S(2)}) %collective-permute-start.13) | collective-permute-done | bytes 4128 | tf_op jit(solution)/shard_map/ppermute | solution.py:630
  27.5 0.0 collective-permute-done.10
  27.5 0.0 collective-permute-done.11.twin_b_ref
  27.5 0.8 %shard_map.56 = (f32[32,512]{1,0:T(8,128)}, f32[32,512]{1,0:T(8,128)}) custom-call(f32[32,512]{1,0:T(8,128)S(1)} %get-tuple-element.36.v0_ref, f32[32,512]{1,0:T(8,128)S(1)} %get-tuple-element.37.v1_ref, f32[32,512]{1,0:T(8,128)S(1)} %get-tuple-element.38.v2_ref, f32[32,512]{1,0:T(8,128)S(1)} %get-tuple-element.39.scale_ref, f32[32,128]{1,0:T(8,128)S(1)} %slice.26.got_a_ref, ...), custom_call_target="tpu_custom_call" | custom-call | tf_op jit(solution)/shard_map/pallas_call | solution.py:683
  (7 shorter events, 0.0 us)
Async XLA Ops:
  1.6 5.6 %collective-permute-start = (f32[168,128]{1,0:T(8,128)S(1)}, f32[168,128]{1,0:T(8,128)S(1)}, u32[]{:S(2)}, u32[]{:S(2)}) collective-permute-start(f32[168,128]{1,0:T(8,128)S(1)} %get-tuple-element.23.refs_0_), channel_id=1, source_target_pairs={{0,2},{1,3},{2,0},{3,1},{4,6},{5,7},{6,4},{7,5},{8,10},{9,11},{10,... | collective-permute-start | bytes 258056 | tf_op jit(solution)/shard_map/ppermute | solution.py:605
  4.6 4.5 %collective-permute-start.1 = (f32[168,128]{1,0:T(8,128)S(1)}, f32[168,128]{1,0:T(8,128)S(1)}, u32[]{:S(2)}, u32[]{:S(2)}) collective-permute-start(f32[168,128]{1,0:T(8,128)S(1)} %get-tuple-element.23.refs_0_), channel_id=1, source_target_pairs={{0,1},{1,0},{2,3},{3,2},{4,5},{5,4},{6,7},{7,6},{8,9},{9,8},{10,11... | collective-permute-start | bytes 258056 | tf_op jit(solution)/shard_map/ppermute | solution.py:615
  7.1 2.0 %collective-permute-start.2 = (f32[168,128]{1,0:T(8,128)S(1)}, f32[168,128]{1,0:T(8,128)S(1)}, u32[]{:S(2)}, u32[]{:S(2)}) collective-permute-start(f32[168,128]{1,0:T(8,128)S(1)} %collective-permute-done.refs_1_), channel_id=1, source_target_pairs={{0,1},{1,0},{2,3},{3,2},{4,5},{5,4},{6,7},{7,6},{8,9},{9,8},{10,11... | collective-permute-start | bytes 258056 | tf_op jit(solution)/shard_map/ppermute | solution.py:615
  7.1 4.7 %collective-permute-start.3 = (f32[128,128]{1,0:T(8,128)S(1)}, f32[128,128]{1,0:T(8,128)S(1)}, u32[]{:S(2)}, u32[]{:S(2)}) collective-permute-start(f32[128,128]{1,0:T(8,128)S(1)} %get-tuple-element.27.refs_0_), channel_id=1, source_target_pairs={{0,2},{1,3},{2,0},{3,1},{4,6},{5,7},{6,4},{7,5},{8,10},{9,11},{10,... | collective-permute-start | bytes 196616 | tf_op jit(solution)/shard_map/ppermute | solution.py:605
  9.8 4.2 %collective-permute-start.6 = (f32[96,128]{1,0:T(8,128)S(1)}, f32[96,128]{1,0:T(8,128)S(1)}, u32[]{:S(2)}, u32[]{:S(2)}) collective-permute-start(f32[96,128]{1,0:T(8,128)S(1)} %get-tuple-element.32), channel_id=1, source_target_pairs={{0,4},{1,3},{2,6},{3,1},{4,0},{5,9},{6,2},{7,11},{8,12},{9,5},{10,... | collective-permute-start | bytes 147464 | tf_op jit(solution)/shard_map/ppermute | solution.py:591
  11.9 2.4 %collective-permute-start.4 = (f32[128,128]{1,0:T(8,128)S(1)}, f32[128,128]{1,0:T(8,128)S(1)}, u32[]{:S(2)}, u32[]{:S(2)}) collective-permute-start(f32[128,128]{1,0:T(8,128)S(1)} %get-tuple-element.27.refs_0_), channel_id=1, source_target_pairs={{0,1},{1,0},{2,3},{3,2},{4,5},{5,4},{6,7},{7,6},{8,9},{9,8},{10,11... | collective-permute-start | bytes 196616 | tf_op jit(solution)/shard_map/ppermute | solution.py:615
  11.9 2.4 %collective-permute-start.5 = (f32[128,128]{1,0:T(8,128)S(1)}, f32[128,128]{1,0:T(8,128)S(1)}, u32[]{:S(2)}, u32[]{:S(2)}) collective-permute-start(f32[128,128]{1,0:T(8,128)S(1)} %collective-permute-done.3.refs_1_), channel_id=1, source_target_pairs={{0,1},{1,0},{2,3},{3,2},{4,5},{5,4},{6,7},{7,6},{8,9},{9,8},{10,11... | collective-permute-start | bytes 196616 | tf_op jit(solution)/shard_map/ppermute | solution.py:615
  14.0 1.2 %collective-permute-start.7 = (f32[96,128]{1,0:T(8,128)S(1)}, f32[96,128]{1,0:T(8,128)S(1)}, u32[]{:S(2)}, u32[]{:S(2)}) collective-permute-start(f32[96,128]{1,0:T(8,128)S(1)} %collective-permute-done.6.mine_ref), channel_id=1, source_target_pairs={{0,1},{1,0},{2,3},{3,2},{4,5},{5,4},{6,7},{7,6},{8,9},{9,8},{10,11... | collective-permute-start | bytes 147464 | tf_op jit(solution)/shard_map/ppermute | solution.py:615
  16.1 6.8 %collective-permute-start.9 = (f32[40,128]{1,0:T(8,128)S(1)}, f32[40,128]{1,0:T(8,128)S(1)}, u32[]{:S(2)}, u32[]{:S(2)}) collective-permute-start(f32[40,128]{1,0:T(8,128)S(1)} %get-tuple-element.41), channel_id=1, source_target_pairs={{0,16},{1,3},{2,18},{3,1},{4,20},{5,9},{6,22},{7,11},{8,24},{9,5},... | collective-permute-start | bytes 61448 | tf_op jit(solution)/shard_map/ppermute | solution.py:591
  19.3 3.6 %collective-permute-start.8 = (f32[8,128]{1,0:T(8,128)S(1)}, f32[8,128]{1,0:T(8,128)S(1)}, u32[]{:S(2)}, u32[]{:S(2)}) collective-permute-start(f32[8,128]{1,0:T(8,128)S(1)} %slice.20), channel_id=1, source_target_pairs={{0,8},{1,25},{2,10},{3,27},{4,12},{5,29},{6,14},{7,31},{8,0},{9,17... | collective-permute-start | bytes 12296 | tf_op jit(solution)/shard_map/ppermute | solution.py:591
  22.9 4.6 %collective-permute-start.10 = (f32[40,128]{1,0:T(8,128)S(1)}, f32[40,128]{1,0:T(8,128)S(1)}, u32[]{:S(2)}, u32[]{:S(2)}) collective-permute-start(f32[40,128]{1,0:T(8,128)S(1)} %pad_maximum_fusion), channel_id=1, source_target_pairs={{0,4},{1,5},{2,6},{3,7},{4,0},{5,1},{6,2},{7,3},{8,12},{9,13},{10,... | collective-permute-start | bytes 61448 | tf_op jit(solution)/shard_map/ppermute | solution.py:591
  24.5 1.2 %collective-permute-start.12 = (f32[8,128]{1,0:T(8,128)S(1)}, f32[8,128]{1,0:T(8,128)S(1)}, u32[]{:S(2)}, u32[]{:S(2)}) collective-permute-start(f32[8,128]{1,0:T(8,128)S(1)} %fusion.2), channel_id=1, source_target_pairs={{0,1},{1,0},{2,3},{3,2},{4,5},{5,4},{6,7},{7,6},{8,9},{9,8},{10,11... | collective-permute-start | bytes 12296 | tf_op jit(solution)/shard_map/ppermute | solution.py:615
  24.5 3.0 %collective-permute-start.13 = (f32[8,128]{1,0:T(8,128)S(1)}, f32[8,128]{1,0:T(8,128)S(1)}, u32[]{:S(2)}, u32[]{:S(2)}) collective-permute-start(f32[8,128]{1,0:T(8,128)S(1)} %fusion.2), channel_id=1, source_target_pairs={{0,5},{1,4},{2,7},{3,6},{4,1},{5,0},{6,3},{7,2},{8,13},{9,12},{10,... | collective-permute-start | bytes 12296 | tf_op jit(solution)/shard_map/ppermute | solution.py:630
  25.5 2.1 %collective-permute-start.11 = (f32[32,128]{1,0:T(8,128)S(1)}, f32[32,128]{1,0:T(8,128)S(1)}, u32[]{:S(2)}, u32[]{:S(2)}) collective-permute-start(f32[32,128]{1,0:T(8,128)S(1)} %slice.27.got_b_ref), channel_id=1, source_target_pairs={{0,1},{1,0},{2,3},{3,2},{4,5},{5,4},{6,7},{7,6},{8,9},{9,8},{10,11... | collective-permute-start | bytes 49160 | tf_op jit(solution)/shard_map/ppermute | solution.py:615
